TPU v7x, 128 devices: a whole 4x4x4 slice. The times are simulated.
128 devices in a mesh: dp: 8 (over y, core), tensor: 16 (over z, x).
Axes of the slice: x: 4, y: 4, z: 4, core: 2. Of those that a mesh axis runs over, the one named last changes fastest.
Arguments:
- ids: int32 [6144], P(('dp', 'tensor')), may hold values from 0 to 16383, as said below
- doc_lengths: int32 [16], replicated, may hold values from 1 to 3072, 6144 in all
- table: bfloat16 [16384, 4096], P('tensor'), may hold values from -6 to 6
- attn_gain: float32 [4096], replicated, may hold values from 0.1 to 1.9
- wq: bfloat16 [4096, 4096], P(None, 'tensor')
- wkv: bfloat16 [4096, 2048], P(None, 'tensor')
- wo: bfloat16 [4096, 4096], P('tensor'), may hold values from -0.09375 to 0.09375
- mlp_gain: float32 [4096], replicated, may hold values from 0.1 to 1.9
- w_gate: bfloat16 [4096, 7168], P(None, 'tensor'), may hold values from -0.09375 to 0.09375
- w_up: bfloat16 [4096, 7168], P(None, 'tensor'), may hold values from -0.09375 to 0.09375
- w_down: bfloat16 [7168, 4096], P('tensor'), may hold values from -0.0625 to 0.0625
Outputs:
- layer_out: bfloat16 [6144, 4096], P(('dp', 'tensor'))
Inputs may be any that keep to these rules, and one draw needn't show every extreme that they name: ids name added rows. In each aligned block of 48 tokens (the tokens of one device), at most 6 ids lie in any one owner range r * 1024 to (r + 1) * 1024 - 1, and in every block some range holds exactly 6.
All inputs are finite; a program needn't handle non-finite values.
Results may differ from a plain program's by a relative error of at most 0.022.
The roundings to bfloat16 on the way count: a program that leaves them out, or rounds other values in their place, can miss the bound.
Values may be sent and summed in bfloat16 or wider, within the bound.
A program may use at most 192 MiB of HBM per device.

v0:
```python
import jax
import jax.numpy as jnp
from jax import lax
from jax.sharding import PartitionSpec as P

HD = 128


EPSILON = 1e-05
ROPE_BASE = 500000.0
NEGATIVE = -1e30


def partner_2(block, axis, bit):
    count = lax.axis_size(axis)
    route = []
    for low in range(count):
        high = low | 1 << bit
        if high != low and high < count:
            route += [(low, high), (high, low)]
    return lax.ppermute(block, axis, route)


def rms_scale(rows_in, gain):
    widened = rows_in.astype(jnp.float32)
    scaled = (
        widened * lax.rsqrt(jnp.mean(widened * widened, axis=-1, keepdims=True) + EPSILON) * gain
    )
    return scaled.astype(jnp.bfloat16)


def document_info(positions, doc_lengths):
    ends = jnp.cumsum(doc_lengths)
    starts = ends - doc_lengths
    began = starts[None, :] <= positions[:, None]
    documents = jnp.sum(began.astype(jnp.int32), axis=1) - 1
    first_pos = jnp.max(jnp.where(began, starts[None, :], 0), axis=1)
    return (documents, positions - first_pos)


def rotate(projected, offsets):
    half_dim = projected.shape[-1] // 2
    inverse = ROPE_BASE ** (-jnp.arange(half_dim, dtype=jnp.float32) * 2.0 / projected.shape[-1])
    angle = offsets.astype(jnp.float32)[:, None] * inverse[None, :]
    cosine = jnp.concatenate([jnp.cos(angle), jnp.cos(angle)], axis=-1)[:, None, :]
    sine = jnp.concatenate([jnp.sin(angle), jnp.sin(angle)], axis=-1)[:, None, :]
    turned = jnp.concatenate([-projected[..., half_dim:], projected[..., :half_dim]], axis=-1)
    return projected * cosine + turned * sine


def rope_pairs(projected, offsets, parity):
    row_count, width = projected.shape
    turned = rotate(projected.reshape(row_count, 1, width), offsets).reshape(row_count, width)
    return jnp.where(parity == 0, turned, projected)


def local(ids, doc_lengths, table, attn_gain, wq, wkv, wo, mlp_gain, w_gate, w_up, w_down):
    tensor_count = lax.axis_size("tensor")
    tensor_index = lax.axis_index("tensor")
    range_index = lax.axis_index("dp")
    own_rows = ids.shape[0]
    tok_range = own_rows * tensor_count
    range_start = range_index * tok_range
    head_dim = HD
    q_width = wq.shape[1]
    q_heads = q_width // head_dim
    kv_width = wkv.shape[1]
    kv_heads = max(kv_width // (2 * head_dim), 1)
    ratio = q_heads // kv_heads
    parity = tensor_index % 2
    rows_owned = table.shape[0]
    range_ids = lax.all_gather(ids, "tensor", axis=0, tiled=True)
    local_rows = range_ids - tensor_index * rows_owned
    inside = (local_rows >= 0) & (local_rows < rows_owned)
    picked = jnp.take(table, jnp.clip(local_rows, 0, rows_owned - 1), axis=0)
    picked = jnp.where(inside[:, None], picked.astype(jnp.float32), 0.0)
    embedded = lax.psum_scatter(
        picked.astype(jnp.bfloat16), "tensor", scatter_dimension=0, tiled=True
    )
    normed = rms_scale(embedded, attn_gain)
    shard_rows = lax.all_gather(normed, "tensor", axis=0, tiled=True)
    row_count = shard_rows.shape[0]
    positions = range_start + jnp.arange(row_count, dtype=jnp.int32)
    unused_docs, offsets = document_info(positions, doc_lengths)
    query_part = jnp.dot(shard_rows, wq, preferred_element_type=jnp.float32).reshape(
        row_count, q_heads, head_dim
    )
    query_part = rotate(query_part, offsets).reshape(row_count, q_width).astype(jnp.bfloat16)
    kv_part = rope_pairs(
        jnp.dot(shard_rows, wkv, preferred_element_type=jnp.float32), offsets, parity
    )
    projected = jnp.concatenate([query_part, kv_part.astype(jnp.bfloat16)], axis=1)
    queries = projected[:, :q_width].reshape(tok_range, kv_heads, ratio, head_dim)
    own_pairs = projected[:, q_width:]
    partner = partner_2(own_pairs, "tensor", 0)
    key_cols = jnp.where(parity == 0, own_pairs, partner)
    value_cols = jnp.where(parity == 0, partner, own_pairs)
    stacked = jnp.concatenate([key_cols, value_cols], axis=1)
    query_pos = range_start + jnp.arange(tok_range, dtype=jnp.int32)
    query_docs, query_offsets = document_info(query_pos, doc_lengths)
    score_scale = head_dim ** (-0.5)
    shard_rows = lax.all_gather(stacked, "dp", axis=0, tiled=True)
    running_max = jnp.full((kv_heads, ratio, tok_range), NEGATIVE, jnp.float32)
    row_count = shard_rows.shape[0]
    grouped = shard_rows.reshape(row_count, kv_heads, 2, head_dim)
    scores = (
        jnp.einsum(
            "qgrd,kgd->grqk", queries, grouped[:, :, 0, :], preferred_element_type=jnp.float32
        )
        * score_scale
    )
    key_pos = jnp.arange(row_count, dtype=jnp.int32)
    key_docs, unused_offsets = document_info(key_pos, doc_lengths)
    allowed = (key_pos[None, :] <= query_pos[:, None]) & (key_docs[None, :] == query_docs[:, None])
    scores = jnp.where(allowed, scores, NEGATIVE)
    new_max = jnp.maximum(running_max, jnp.max(scores, axis=-1))
    weights = jnp.where(allowed, jnp.exp(scores - new_max[..., None]), 0.0)
    running_sum = jnp.sum(weights, axis=-1)
    added = jnp.einsum(
        "grqk,kgd->grqd",
        weights.astype(jnp.bfloat16),
        grouped[:, :, 1, :],
        preferred_element_type=jnp.float32,
    )
    attended = (
        jnp.transpose(added / running_sum[..., None], (2, 0, 1, 3))
        .reshape(tok_range, q_width)
        .astype(jnp.bfloat16)
    )
    selected = attended
    mixed = lax.psum_scatter(
        jnp.dot(selected, wo, preferred_element_type=jnp.float32).astype(jnp.bfloat16),
        "tensor",
        scatter_dimension=0,
        tiled=True,
    ).astype(jnp.float32)
    stream = (embedded.astype(jnp.float32) + mixed).astype(jnp.bfloat16)
    normed_mlp = rms_scale(stream, mlp_gain)
    shard_rows = lax.all_gather(normed_mlp, "tensor", axis=0, tiled=True)
    gate_part = jnp.dot(shard_rows, w_gate, preferred_element_type=jnp.float32)
    up_part = jnp.dot(shard_rows, w_up, preferred_element_type=jnp.float32)
    hidden = (jax.nn.silu(gate_part) * up_part).astype(jnp.bfloat16)
    selected = hidden
    reduced = lax.psum_scatter(
        jnp.dot(selected, w_down, preferred_element_type=jnp.float32).astype(jnp.bfloat16),
        "tensor",
        scatter_dimension=0,
        tiled=True,
    ).astype(jnp.float32)
    return (stream.astype(jnp.float32) + reduced).astype(jnp.bfloat16)


def solution(mesh):
    placed = (
        P(("dp", "tensor")),
        P(),
        P("tensor", None),
        P(),
        P(None, "tensor"),
        P(None, "tensor"),
        P("tensor", None),
        P(),
        P(None, "tensor"),
        P(None, "tensor"),
        P("tensor", None),
    )
    return jax.shard_map(
        local, mesh=mesh, in_specs=placed, out_specs=P(("dp", "tensor"), None), check_vma=False
    )
```

profile of v0, /device:TPU:16, one launch (start us, length us, event | category | flops | bytes accessed | tf_op | source)
XLA Modules:
  0.0 551.5 jit_solution(13898454190667706442)
XLA Ops:
  6.5 1.4 dynamic-slice
  9.4 17.6 %all-reduce = s32[768]{0:T(1024)S(1)} all-reduce(s32[768]{0:T(1024)S(1)} %dynamic-update-slice), channel_id=1, replica_groups=mesh['dp'=8,'tensor'=16] {'tensor'}, use_global_device_ids=true, to_apply=%add | all-reduce | flops 768 | bytes 6144
  27.0 16.4 %gather_fusion = bf16[768,4096]{1,0:T(8,128)(2,1)} fusion(bf16[1024,4096]{1,0:T(8,128)(2,1)} %param.13, s32[1024]{0:T(1024)S(1)} %pad_clamp_fusion), kind=kCustom, calls=%fused_computation | custom fusion | bytes 12585984 | tf_op jit(solution)/shard_map/jit(_take)/gather | solution.py:75
  43.5 8.1 %select_convert_fusion = bf16[768,4096]{1,0:T(8,128)(2,1)} fusion(bf16[768,4096]{1,0:T(8,128)(2,1)} %gather_fusion, pred[768]{0:T(1024)(128)(4,1)S(1)} %get-tuple-element.7, pred[768]{0:T(1024)(128)(4,1)S(1)} %get-tuple-element.20), kind=kLoop, calls=%fused_computation.11 | loop fusion | flops 12582912 | bytes 12584448 | tf_op jit(solution)/shard_map/convert_element_type | solution.py:78
  51.7 78.7 %reduce-scatter.4.cloned.1.call-done = bf16[48,4096]{1,0:T(8,128)(2,1)} async-done(((bf16[768,4096]{1,0:T(8,128)(2,1)}), bf16[48,4096]{1,0:T(8,128)(2,1)}) %reduce-scatter.4.cloned.1.call-update) | async-done | bytes 393232 | tf_op jit(solution)/shard_map/reduce_scatter | solution.py:77
  131.5 1.9 fusion.12
  134.7 59.6 %all-gather.4.cloned.1.call-done = bf16[768,4096]{1,0:T(8,128)(2,1)} async-done(((bf16[48,4096]{1,0:T(8,128)(2,1)}), bf16[768,4096]{1,0:T(8,128)(2,1)}) %all-gather.4.cloned.1.call-update) | async-done | bytes 6291472 | tf_op jit(solution)/shard_map/all_gather | solution.py:81
  194.3 5.0 fusion.31
  199.5 1.6 collective-permute-start
  201.0 5.0 collective-permute-done
  207.3 5.7 %fusion.6 = pred[768,6144]{0,1:T(8,128)(4,1)} fusion(s32[768]{0:T(1024)S(1)} %broadcast_add_fusion.1, s32[768]{0:T(1024)S(1)} %iota_add_fusion, s32[6144]{0:T(1024)S(1)} %broadcast_add_fusion), kind=kLoop, calls=%fused_computation.9 | loop fusion | flops 14155776 | bytes 4749312 | tf_op jit(solution)/shard_map/and | solution.py:114
  212.9 5.4 fusion.32
  218.6 14.3 %all-gather.6.cloned.1.call-done = bf16[6144,256]{0,1:T(8,128)(2,1)} async-done(((bf16[768,256]{0,1:T(8,128)(2,1)}), bf16[6144,256]{0,1:T(8,128)(2,1)}) %all-gather.6.cloned.1.call-update) | async-done | bytes 3145744 | tf_op jit(solution)/shard_map/all_gather | solution.py:102
  232.9 16.2 %fusion = (f32[2,768]{1,0:T(2,128)S(1)}, f32[6144,768,2]{1,0,2:T(8,128)}) fusion(pred[768,6144]{0,1:T(8,128)(4,1)} %fusion.6, bf16[768,2,128]{0,2,1:T(8,128)(2,1)S(1)} %bitcast.75, bf16[6144,1,2,128]{0,3,2,1:T(8,128)(2,1)} %bitcast.77), kind=kOutput, calls=%fused_computation.3 | convolution fusion | flops 2444229120 | bytes 44439552 | tf_op jit(solution)/shard_map/qgrd,kgd->grqk/dot_general | solution.py:107
  249.1 17.7 %fusion.1 = f32[2,768]{1,0:T(2,128)S(1)} fusion(f32[6144,768,2]{1,0,2:T(8,128)} %get-tuple-element.22, f32[2,768]{1,0:T(2,128)S(1)} %broadcast_maximum_fusion, pred[768,6144]{0,1:T(8,128)(4,1)} %fusion.6), kind=kLoop, calls=%fused_computation.4 | loop fusion | flops 47184384 | bytes 42479616 | tf_op jit(solution)/shard_map/reduce_sum | solution.py:118
  266.8 18.4 %divide_convert_fusion = bf16[2,768,128]{1,2,0:T(8,128)(2,1)S(1)} fusion(f32[6144,768,2]{1,0,2:T(8,128)} %get-tuple-element.22, f32[2,768]{1,0:T(2,128)S(1)} %broadcast_maximum_fusion, pred[768,6144]{0,1:T(8,128)(4,1)} %fusion.6, bf16[6144,1,2,128]{0,3,2,1:T(8,128)(2,1)S(1)} %bitcast.78, f32[2,768]{1,0:T(2,128)S(1)} %fusion.1), kind=kOutput, calls=%fused_computation.37 | convolution fusion | flops 2463498240 | bytes 44445696 | tf_op jit(solution)/shard_map/grqk,kgd->grqd/dot_general | solution.py:119
  285.3 4.5 convolution_convert_fusion.1
  289.8 83.1 %reduce-scatter.6.cloned.1.call-done = bf16[48,4096]{1,0:T(8,128)(2,1)} async-done(((bf16[768,4096]{1,0:T(8,128)(2,1)}), bf16[48,4096]{1,0:T(8,128)(2,1)}) %reduce-scatter.6.cloned.1.call-update) | async-done | bytes 393232 | tf_op jit(solution)/shard_map/reduce_scatter | solution.py:131
  374.2 1.9 fusion.16
  376.1 60.8 %all-gather.8.cloned.1.call-done = bf16[768,4096]{1,0:T(8,128)(2,1)} async-done(((bf16[48,4096]{1,0:T(8,128)(2,1)}), bf16[768,4096]{1,0:T(8,128)(2,1)}) %all-gather.8.cloned.1.call-update) | async-done | bytes 6291472 | tf_op jit(solution)/shard_map/all_gather | solution.py:139
  437.0 8.1 %fusion.33 = f32[768,448]{0,1:T(8,128)} fusion(bf16[768,4096]{1,0:T(8,128)(2,1)} %all-gather.8.cloned.1.call-done, bf16[4096,448]{0,1:T(8,128)(2,1)} %param.19), kind=kOutput, calls=%fused_computation.77 | convolution fusion | flops 2818572288 | bytes 11337728 | tf_op jit(solution)/shard_map/dot_general | solution.py:140
  445.0 16.3 %convolution_convert_fusion = bf16[768,4096]{1,0:T(8,128)(2,1)} fusion(bf16[448,4096]{1,0:T(8,128)(2,1)} %param.21, bf16[768,4096]{1,0:T(8,128)(2,1)} %all-gather.8.cloned.1.call-done, bf16[4096,448]{0,1:T(8,128)(2,1)} %param.20, f32[768,448]{0,1:T(8,128)} %fusion.33), kind=kOutput, calls=%fused_computation.12 | convolution fusion | flops 5642354688 | bytes 21299200 | tf_op jit(solution)/shard_map/dot_general | solution.py:145
  461.3 81.4 %reduce-scatter.8.cloned.1.call-done = bf16[48,4096]{1,0:T(8,128)(2,1)} async-done(((bf16[768,4096]{1,0:T(8,128)(2,1)}), bf16[48,4096]{1,0:T(8,128)(2,1)}) %reduce-scatter.8.cloned.1.call-update) | async-done | bytes 393232 | tf_op jit(solution)/shard_map/reduce_scatter | solution.py:144
  542.8 1.9 fusion.17
  (56 shorter events, 6.3 us)
Async XLA Ops:
  6.5 278.7 %copy-start = (bf16[256,4096]{1,0:T(8,128)(2,1)S(1)}, bf16[256,4096]{1,0:T(8,128)(2,1)}, u32[]{:S(2)}) copy-start(bf16[256,4096]{1,0:T(8,128)(2,1)} %param.17) | copy-start | bytes 6291460
  6.5 123.8 %reduce-scatter.4.cloned.1.call-start = ((), (), s32[]{:S(2)}) async-start(), calls=%async_computation.3 | async-start | bytes 6684672 | tf_op jit(solution)/shard_map/reduce_scatter | solution.py:77
  51.6 80.0 %copy-start.5 = (f32[4096]{0:T(1024)S(1)}, f32[4096]{0:T(1024)}, u32[]{:S(2)}) copy-start(f32[4096]{0:T(1024)} %param.14) | copy-start | bytes 49156
  51.6 82.0 %copy-start.6 = (s32[16]{0:T(128)S(1)}, s32[16]{0:T(128)}, u32[]{:S(2)}) copy-start(s32[16]{0:T(128)} %param.12) | copy-start | bytes 196
  51.6 142.7 %copy-start.3 = (bf16[4096,128]{1,0:T(8,128)(2,1)S(1)}, bf16[4096,128]{1,0:T(8,128)(2,1)}, u32[]{:S(2)}) copy-start(bf16[4096,128]{1,0:T(8,128)(2,1)} %param.16) | copy-start | bytes 3145732
  51.6 142.7 %all-gather.4.cloned.1.call-start = ((), (), s32[]{:S(2)}) async-start(), calls=%async_computation.4 | async-start | bytes 6684672 | tf_op jit(solution)/shard_map/all_gather | solution.py:81
  133.5 99.4 %all-gather.6.cloned.1.call-start = ((), (), s32[]{:S(2)}) async-start(), calls=%async_computation.5 | async-start | bytes 3538944 | tf_op jit(solution)/shard_map/all_gather | solution.py:102
  199.5 6.6 %collective-permute-start = (bf16[768,128]{0,1:T(8,128)(2,1)S(1)}, bf16[768,128]{0,1:T(8,128)(2,1)S(1)}, u32[]{:S(2)}, u32[]{:S(2)}) collective-permute-start(bf16[768,128]{0,1:T(8,128)(2,1)S(1)} %get-tuple-element.15), channel_id=1, source_target_pairs={{0,1},{1,0},{2,3},{3,2},{4,5},{5,4},{6,7},{7,6},{8,9},{9,8},{10,11... | collective-permute-start | bytes 589832 | tf_op jit(solution)/shard_map/ppermute | solution.py:21
  206.9 166.1 %reduce-scatter.6.cloned.1.call-start = ((), (), s32[]{:S(2)}) async-start(), calls=%async_computation.6 | async-start | bytes 6684672 | tf_op jit(solution)/shard_map/reduce_scatter | solution.py:131
  249.1 17.7 %copy-start.7 = (bf16[6144,256]{0,1:T(8,128)(2,1)S(1)}, bf16[6144,256]{0,1:T(8,128)(2,1)}, u32[]{:S(2)}) copy-start(bf16[6144,256]{0,1:T(8,128)(2,1)} %all-gather.6.cloned.1.call-done) | copy-start | bytes 9437188
  285.2 87.7 %copy-start.1 = (bf16[48,4096]{1,0:T(8,128)(2,1)S(1)}, bf16[48,4096]{1,0:T(8,128)(2,1)}, u32[]{:S(2)}) copy-start(bf16[48,4096]{1,0:T(8,128)(2,1)} %reduce-scatter.4.cloned.1.call-done) | copy-start | bytes 1179652
  285.2 88.9 %copy-start.4 = (f32[4096]{0:T(1024)S(1)}, f32[4096]{0:T(1024)}, u32[]{:S(2)}) copy-start(f32[4096]{0:T(1024)} %param.18) | copy-start | bytes 49156
  289.8 147.2 %all-gather.8.cloned.1.call-start = ((), (), s32[]{:S(2)}) async-start(), calls=%async_computation.7 | async-start | bytes 6684672 | tf_op jit(solution)/shard_map/all_gather | solution.py:139
  376.1 166.7 %reduce-scatter.8.cloned.1.call-start = ((), (), s32[]{:S(2)}) async-start(), calls=%async_computation.8 | async-start | bytes 6684672 | tf_op jit(solution)/shard_map/reduce_scatter | solution.py:144
  461.3 81.5 %copy-start.2 = (bf16[48,4096]{1,0:T(8,128)(2,1)S(1)}, bf16[48,4096]{1,0:T(8,128)(2,1)}, u32[]{:S(2)}) copy-start(bf16[48,4096]{1,0:T(8,128)(2,1)} %reduce-scatter.6.cloned.1.call-done) | copy-start | bytes 1179652
Sparse Core Ops, SparseCore 0:
  51.7 78.5 reduce-scatter.3
  133.6 60.6 all-gather.3
  207.0 25.8 all-gather.5
  289.9 82.9 reduce-scatter.5
  376.2 60.6 all-gather.7
  461.5 81.2 reduce-scatter.7
where the time goes:
time: 552 us
  waiting for transfers between devices  383 us (69%)
  matrix products  73.8 us (13%)
  other arithmetic  42 us (8%)
  local copies, waits for them, and re-layouts  18.8 us (3%)
  blocking collectives  17.6 us (3%)
  between operations  14.3 us (3%)
    reduce_scatter x1, waiting for transfers between devices, local(): lax.psum_scatter(jnp.dot(selected, wo, preferred_element_type=jnp.float32...  83.1 us
    reduce_scatter x1, waiting for transfers between devices, local(): lax.psum_scatter(jnp.dot(selected, w_down, preferred_element_type=jnp.flo...  81.4 us
    reduce_scatter x1, waiting for transfers between devices, local(): lax.psum_scatter(picked.astype(jnp.bfloat16), 'tensor', scatter_dimension...  78.7 us
    all_gather x1, waiting for transfers between devices, local(): shard_rows = lax.all_gather(normed_mlp, 'tensor', axis=0, tiled=True)  60.8 us
    all_gather x1, waiting for transfers between devices, local(): shard_rows = lax.all_gather(normed, 'tensor', axis=0, tiled=True)  59.6 us
    dot_general x1, matrix products, local(): jnp.einsum('grqk,kgd->grqd', weights.astype(jnp.bfloat16), grouped[:, :,...  18.4 us
    reduce_sum x1, other arithmetic, local(): running_sum = jnp.sum(weights, axis=-1)  17.7 us
    unnamed x1, blocking collectives  17.6 us
  transfers between devices with their start and end apart: 7, of which 7 were waited for; matrix products, arithmetic and copies ran while one was open for 2% of the time, Pallas kernels for 0%

commit v1 on v0

v1 whole, which is shorter than its diff:
```python
import functools

import jax
import jax.numpy as jnp
from jax import lax
from jax.experimental import pallas as pl
from jax.experimental.pallas import tpu as pltpu
from jax.sharding import PartitionSpec as P

HD = 128
SIDE = 4
GROUP = SIDE * SIDE
SLOTS = 8
MAXDOC = 3072

EPSILON = 1e-05
ROPE_BASE = 500000.0
NEGATIVE = -1e30
MESH = pl.DeviceIdType.MESH
VMEM = pltpu.VMEM
DMA = pltpu.SemaphoreType.DMA
BF16 = jnp.bfloat16
F32 = jnp.float32


def document_info(positions, doc_lengths):
    ends = jnp.cumsum(doc_lengths)
    starts = ends - doc_lengths
    began = starts[None, :] <= positions[:, None]
    first_pos = jnp.max(jnp.where(began, starts[None, :], 0), axis=1)
    return first_pos, positions - first_pos


def rotate(projected, offsets):
    half_dim = projected.shape[-1] // 2
    inverse = ROPE_BASE ** (-jnp.arange(half_dim, dtype=jnp.float32) * 2.0 / projected.shape[-1])
    angle = offsets.astype(jnp.float32)[:, None] * inverse[None, :]
    cosine = jnp.concatenate([jnp.cos(angle), jnp.cos(angle)], axis=-1)[:, None, :]
    sine = jnp.concatenate([jnp.sin(angle), jnp.sin(angle)], axis=-1)[:, None, :]
    turned = jnp.concatenate([-projected[..., half_dim:], projected[..., :half_dim]], axis=-1)
    return projected * cosine + turned * sine


def wrap(v):
    return lax.rem(v + 2 * SIDE, SIDE)


def place(z, x):
    return wrap(z) * SIDE + wrap(x)


def here():
    t = lax.axis_index("tensor")
    return t // SIDE, lax.rem(t, SIDE)


def greet(peers):
    barrier = pltpu.get_barrier_semaphore()
    for peer in peers:
        pl.semaphore_signal(barrier, inc=1, device_id=peer, device_id_type=MESH)
    pl.semaphore_wait(barrier, len(peers))


def torus_peers(z, x):
    return [{"tensor": place(z + a, x + b)} for a, b in ((0, 1), (0, -1), (1, 0), (-1, 0))]


def remote(src, dst, send_sem, recv_sem, peer):
    return pltpu.make_async_remote_copy(
        src_ref=src, dst_ref=dst, send_sem=send_sem, recv_sem=recv_sem,
        device_id=peer, device_id_type=MESH,
    )


def ring_gather(buf, ssem, rsem, z, x):
    half = buf.shape[-1] // 2
    quarter = half // 2
    started = []

    def block(h, first, second):
        return place(z + second, x + first) if h == 0 else place(z + first, x + second)

    def view(h, first, second, part):
        start, size = (h * half, half) if part == 0 else (h * half + (part - 1) * quarter, quarter)
        return buf.at[block(h, first, second), :, pl.ds(start, size)]

    def send(h, n, first, second, part, axis, d):
        ref = view(h, first, second, part)
        peer = {"tensor": block(h, d, 0) if axis == 0 else block(h, 0, d)}
        copy = remote(ref, ref, ssem.at[h, n], rsem.at[h, n], peer)
        copy.start()
        started.append(copy)

    def recv(h, n, first, second, part):
        ref = view(h, first, second, part)
        remote(ref, ref, ssem.at[h, n], rsem.at[h, n], {"tensor": block(h, 1, 0)}).wait_recv()

    offsets = (0, -1, 1, 2)
    for h in range(2):
        send(h, 0, 0, 0, 0, 0, 1)
        send(h, 1, 0, 0, 0, 0, -1)
    for h in range(2):
        send(h, 4, 0, 0, 0, 1, 1)
        send(h, 5, 0, 0, 0, 1, -1)
    for h in range(2):
        recv(h, 0, -1, 0, 0)
        send(h, 2, -1, 0, 1, 0, 1)
        recv(h, 1, 1, 0, 0)
        send(h, 3, 1, 0, 2, 0, -1)
        for n in (1, 2):
            send(h, 4 + 2 * n, offsets[n], 0, 0, 1, 1)
            send(h, 5 + 2 * n, offsets[n], 0, 0, 1, -1)

    def relay(n):
        k = offsets[n]
        for h in range(2):
            recv(h, 4 + 2 * n, k, -1, 0)
            send(h, 12 + 2 * n, k, -1, 1, 1, 1)
            recv(h, 5 + 2 * n, k, 1, 0)
            send(h, 13 + 2 * n, k, 1, 2, 1, -1)

    relay(0)
    for h in range(2):
        recv(h, 2, 2, 0, 1)
        recv(h, 3, 2, 0, 2)
        send(h, 10, 2, 0, 0, 1, 1)
        send(h, 11, 2, 0, 0, 1, -1)
    for n in (1, 2, 3):
        relay(n)
    for n in range(4):
        for h in range(2):
            recv(h, 12 + 2 * n, offsets[n], 2, 1)
            recv(h, 13 + 2 * n, offsets[n], 2, 2)
    for copy in started:
        copy.wait_send()


GATHER_SEMS = [DMA((2, 20)), DMA((2, 20))]


def ring_reduce(part, r1, r2, held, s1, e1, s2, e2, z, x, make, finish):
    half = part.shape[-1] // 2
    quarter = half // 2
    started = []

    def at(h, k, j):
        return (wrap(z + k), wrap(x + j)) if h == 0 else (wrap(z + j), wrap(x + k))

    def mine(h, k, j, q):
        a, b = at(h, k, j)
        return part.at[a, b, :, pl.ds(h * half + q * quarter, quarter)]

    def peer(h, axis, d):
        a, b = at(h, d, 0) if axis == 0 else at(h, 0, d)
        return {"tensor": a * SIDE + b}

    def send1(h, slot, j, src, d):
        copy = remote(src, r1.at[h, slot, j], s1.at[h, slot, j], e1.at[h, slot, j], peer(h, 0, d))
        copy.start()
        started.append(copy)

    def recv1(h, slot, j):
        ref = r1.at[h, slot, j]
        remote(ref, ref, s1.at[h, slot, j], e1.at[h, slot, j], peer(h, 0, 1)).wait_recv()

    def send2(h, slot, src, d):
        copy = remote(src, r2.at[h, slot], s2.at[h, slot], e2.at[h, slot], peer(h, 1, d))
        copy.start()
        started.append(copy)

    def recv2(h, slot):
        ref = r2.at[h, slot]
        remote(ref, ref, s2.at[h, slot], e2.at[h, slot], peer(h, 0, 1)).wait_recv()

    def load(ref):
        return ref[...].astype(F32)

    order = (2, 1, 3, 0)
    for h in range(2):
        make(h, 2)
        for j in order:
            send1(h, 0, j, mine(h, 2, j, 0), 1)
            send1(h, 3, j, mine(h, 2, j, 1), -1)
    for h in range(2):
        make(h, 1)
        for j in order:
            send1(h, 1, j, mine(h, 1, j, 1), 1)
        make(h, 3)
        for j in order:
            send1(h, 4, j, mine(h, 3, j, 0), -1)
    for j in order:
        for h in range(2):
            recv1(h, 0, j)
            r1[h, 0, j] = (load(r1.at[h, 0, j]) + load(mine(h, 1, j, 0))).astype(BF16)
            send1(h, 2, j, r1.at[h, 0, j], 1)
            recv1(h, 3, j)
            r1[h, 3, j] = (load(r1.at[h, 3, j]) + load(mine(h, 3, j, 1))).astype(BF16)
            send1(h, 5, j, r1.at[h, 3, j], -1)
    for h in range(2):
        make(h, 0)

    def arrived(h, j):
        for slot in (1, 4, 2, 5):
            recv1(h, slot, j)

    def summed(h, j, q):
        a, b = ((2, 4), (1, 5))[q]
        return load(mine(h, 0, j, q)) + load(r1.at[h, a, j]) + load(r1.at[h, b, j])

    for h in range(2):
        arrived(h, 2)
        for q, slot, d in ((0, 0, 1), (1, 3, -1)):
            held[h, 0, q] = summed(h, 2, q).astype(BF16)
            send2(h, slot, held.at[h, 0, q], d)
    for h in range(2):
        arrived(h, 1)
        held[h, 1, 1] = summed(h, 1, 1).astype(BF16)
        send2(h, 1, held.at[h, 1, 1], 1)
        arrived(h, 3)
        held[h, 2, 0] = summed(h, 3, 0).astype(BF16)
        send2(h, 4, held.at[h, 2, 0], -1)
    for h in range(2):
        recv2(h, 0)
        held[h, 1, 0] = (summed(h, 1, 0) + load(r2.at[h, 0])).astype(BF16)
        send2(h, 2, held.at[h, 1, 0], 1)
        recv2(h, 3)
        held[h, 2, 1] = (summed(h, 3, 1) + load(r2.at[h, 3])).astype(BF16)
        send2(h, 5, held.at[h, 2, 1], -1)
    for h in range(2):
        arrived(h, 0)
        for slot in (1, 4, 2, 5):
            recv2(h, slot)
        for q in range(2):
            a, b = ((2, 4), (1, 5))[q]
            value = summed(h, 0, q) + load(r2.at[h, a]) + load(r2.at[h, b])
            finish(pl.ds(h * half + q * quarter, quarter), value)
    for copy in started:
        copy.wait_send()


def reduce_scratch(rows, width):
    quarter = width // 4
    return [
        VMEM((SIDE, SIDE, rows, width), BF16),
        VMEM((2, 6, SIDE, rows, quarter), BF16),
        VMEM((2, 6, rows, quarter), BF16),
        VMEM((2, 3, 2, rows, quarter), BF16),
        DMA((2, 6, SIDE)), DMA((2, 6, SIDE)), DMA((2, 6)), DMA((2, 6)),
    ]


def products(a_ref, w_ref, part, z, x):
    rows, width = part.shape[2], part.shape[3]
    half = width // 2
    step = min(512, half)

    def make(h, k):
        def run(blocks):
            lhs = jnp.concatenate(
                [a_ref[pl.ds(pl.multiple_of((a * SIDE + b) * rows, 16), rows), :] for a, b in blocks], axis=0
            )

            def column(c, carry):
                cols = pl.ds(pl.multiple_of(h * half + c * step, step), step)
                out = jnp.dot(lhs, w_ref[:, cols], preferred_element_type=F32).astype(BF16)
                for n, (a, b) in enumerate(blocks):
                    part[a, b, :, cols] = out[n * rows:(n + 1) * rows]
                return carry

            lax.fori_loop(0, half // step, column, 0)

        if h == 0:
            run([(wrap(z + k), b) for b in range(SIDE)])
        else:
            run([(a, wrap(x + k)) for a in range(SIDE)])

    return make


def normalize(rows, gain):
    scale = lax.rsqrt(jnp.mean(rows * rows, axis=-1, keepdims=True) + EPSILON)
    return (rows * scale * gain).astype(BF16)


def share_ids_kernel(ids_ref, out_ref, ssem, rsem):
    t = lax.axis_index("tensor")
    peers = [lax.rem(t + n, GROUP) for n in range(1, GROUP)]
    greet([{"tensor": p} for p in peers])
    copies = []
    for n, p in enumerate(peers):
        copy = remote(ids_ref, out_ref.at[t], ssem.at[n], rsem.at[n], {"tensor": p})
        copy.start()
        copies.append(copy)
    out_ref[t] = ids_ref[...]
    for n in range(GROUP - 1):
        source = lax.rem(t + GROUP - 1 - n, GROUP)
        remote(ids_ref, out_ref.at[source], ssem.at[n], rsem.at[n], {"tensor": source}).wait_recv()
    for copy in copies:
        copy.wait_send()


def share_ids(ids):
    rows = ids.shape[0]
    padded = jnp.pad(ids.reshape(1, rows), ((0, 7), (0, 128 - rows)))
    out = pl.pallas_call(
        share_ids_kernel,
        out_shape=jax.ShapeDtypeStruct((GROUP, 8, 128), jnp.int32),
        in_specs=[pl.BlockSpec(memory_space=VMEM)],
        out_specs=pl.BlockSpec(memory_space=VMEM),
        scratch_shapes=[DMA((GROUP - 1,)), DMA((GROUP - 1,))],
        compiler_params=pltpu.CompilerParams(collective_id=0, has_side_effects=True),
        name="share_ids",
    )(padded)
    return out[:, 0, :rows]


def embed_kernel(found_ref, source_ref, gain_ref, emb_ref, all_ref, recv, xs, xr, gs, gr):
    z, x = here()
    t = lax.axis_index("tensor")
    peers = [lax.rem(t + n, GROUP) for n in range(1, GROUP)]
    greet([{"tensor": p} for p in peers])
    copies = []
    for n, p in enumerate(peers):
        copy = remote(found_ref.at[p], recv.at[t], xs.at[n], xr.at[n], {"tensor": p})
        copy.start()
        copies.append(copy)
    recv[t] = found_ref[t]
    for n in range(GROUP - 1):
        source = lax.rem(t + GROUP - 1 - n, GROUP)
        remote(found_ref.at[source], recv.at[source], xs.at[n], xr.at[n], {"tensor": source}).wait_recv()
    rows, width = emb_ref.shape
    lanes = lax.broadcasted_iota(jnp.int32, (rows, GROUP * SLOTS), 1)
    chosen = jnp.where(source_ref[...] == lanes, 1.0, 0.0).astype(BF16)
    step = width // 4
    total = jnp.zeros((rows, 1), F32)
    for c in range(4):
        cols = pl.ds(c * step, step)
        block = recv[:, :, cols].reshape(GROUP * SLOTS, step)
        picked = jnp.dot(chosen, block, preferred_element_type=F32)
        emb_ref[:, cols] = picked.astype(BF16)
        total += jnp.sum(picked * picked, axis=-1, keepdims=True)
    scale = lax.rsqrt(total / width + EPSILON)
    for c in range(4):
        cols = pl.ds(c * step, step)
        all_ref[t, :, cols] = (emb_ref[:, cols].astype(F32) * scale * gain_ref[:, cols]).astype(BF16)
    ring_gather(all_ref, gs, gr, z, x)
    for copy in copies:
        copy.wait_send()


def embed_and_gather(found, source, gain):
    width = found.shape[-1]
    rows = source.shape[0]
    return pl.pallas_call(
        embed_kernel,
        out_shape=(
            jax.ShapeDtypeStruct((rows, width), BF16),
            jax.ShapeDtypeStruct((GROUP, rows, width), BF16),
        ),
        in_specs=[pl.BlockSpec(memory_space=VMEM)] * 3,
        out_specs=(pl.BlockSpec(memory_space=VMEM),) * 2,
        scratch_shapes=[
            VMEM((GROUP, SLOTS, width), BF16), DMA((GROUP - 1,)), DMA((GROUP - 1,)), *GATHER_SEMS,
        ],
        compiler_params=pltpu.CompilerParams(
            collective_id=1, has_side_effects=True, vmem_limit_bytes=40 * 2**20
        ),
        name="embed_and_gather",
    )(found, source, gain)


def share_kv_kernel(own_ref, win_ref, relay, ssem, rsem):
    t = lax.axis_index("tensor")
    r = lax.axis_index("dp")
    y, c = r // 2, lax.rem(r, 2)
    kind = lax.rem(t, 2)
    partner = {"tensor": t + 1 - 2 * kind}
    up = {"dp": lax.rem(y + 1, SIDE) * 2 + c}
    down = {"dp": lax.rem(y + SIDE - 1, SIDE) * 2 + c}
    other = {"dp": y * 2 + 1 - c}
    greet([partner, up, down, other])

    def copy(n, src, dst, peer):
        return remote(src, dst, ssem.at[n], rsem.at[n], peer)

    swap = copy(0, own_ref, win_ref.at[4, kind], partner)
    swap.start()
    win_ref[4, kind] = own_ref[...]
    swap_in = copy(0, own_ref, win_ref.at[4, 1 - kind], partner)
    up_key = copy(1, win_ref.at[4, 0], win_ref.at[2, 0], up)
    up_value = copy(2, win_ref.at[4, 1], win_ref.at[2, 1], up)
    far_key = copy(3, win_ref.at[2, 0], win_ref.at[0, 0], up)
    down_value = copy(4, win_ref.at[4, 1], relay, down)
    far_value = copy(5, relay, win_ref.at[0, 1], down)
    has_up, has_far = y < SIDE - 1, y < SIDE - 2
    got_up, got_far = y > 0, y > 1
    relays = (y == SIDE - 1) | (y == 0)
    swap_in.wait_recv()

    @pl.when(has_far)
    def _():
        down_value.start()

    @pl.when(has_up)
    def _():
        up_key.start()
        up_value.start()

    near = [copy(6 + k, win_ref.at[4, k], win_ref.at[3, k], other) for k in range(2)]
    for k in range(2):
        @pl.when(c == 0)
        def _():
            near[k].start()

    @pl.when(relays)
    def _():
        down_value.wait_recv()
        far_value.start()

    @pl.when(got_up)
    def _():
        up_key.wait_recv()

        @pl.when(has_up)
        def _():
            far_key.start()

        up_value.wait_recv()

    cross0 = [copy(8 + k, win_ref.at[2, k], win_ref.at[1, k], other) for k in range(2)]
    cross1 = [copy(8 + k, win_ref.at[2, k], win_ref.at[3, k], other) for k in range(2)]

    @pl.when(got_up & (c == 0))
    def _():
        for k in range(2):
            cross0[k].start()

    @pl.when(got_up & (c == 1))
    def _():
        for k in range(2):
            cross1[k].start()

    far1 = [copy(10 + k, win_ref.at[0, k], win_ref.at[1, k], other) for k in range(2)]

    @pl.when(got_far)
    def _():
        far_key.wait_recv()
        far_value.wait_recv()

        @pl.when(c == 1)
        def _():
            for k in range(2):
                far1[k].start()

        @pl.when(c == 0)
        def _():
            for k in range(2):
                far1[k].wait_recv()

        @pl.when(c == 1)
        def _():
            for k in range(2):
                far1[k].wait_send()

    @pl.when(c == 1)
    def _():
        for k in range(2):
            near[k].wait_recv()

    @pl.when(c == 0)
    def _():
        for k in range(2):
            near[k].wait_send()

    @pl.when(got_up & (c == 0))
    def _():
        for k in range(2):
            cross1[k].wait_recv()
            cross0[k].wait_send()

    @pl.when(got_up & (c == 1))
    def _():
        for k in range(2):
            cross0[k].wait_recv()
            cross1[k].wait_send()

    @pl.when(has_far)
    def _():
        down_value.wait_send()

    @pl.when(has_up)
    def _():
        up_key.wait_send()
        up_value.wait_send()

    @pl.when(relays)
    def _():
        far_value.wait_send()

    @pl.when(got_up & has_up)
    def _():
        far_key.wait_send()

    swap.wait_send()


def share_kv(own):
    rows, width = own.shape
    return pl.pallas_call(
        share_kv_kernel,
        out_shape=jax.ShapeDtypeStruct((5, 2, rows, width), BF16),
        in_specs=[pl.BlockSpec(memory_space=VMEM)],
        out_specs=pl.BlockSpec(memory_space=VMEM),
        scratch_shapes=[VMEM((rows, width), BF16), DMA((12,)), DMA((12,))],
        compiler_params=pltpu.CompilerParams(
            collective_id=2, has_side_effects=True, vmem_limit_bytes=24 * 2**20
        ),
        name="share_kv",
    )(own)


QB = 256
KB = 256


def attention_kernel(low_ref, q_ref, first_ref, win_ref, out_ref, m_ref, l_ref, acc_ref):
    rows = q_ref.shape[0]
    per_range = rows // KB
    scale = HD ** (-0.5)
    for i in range(rows // QB):
        span = pl.ds(i * QB, QB)
        q = jnp.concatenate([q_ref[span, :HD], q_ref[span, HD:]], axis=0)
        first = first_ref[span, :]
        first = jnp.concatenate([first, first], axis=0)
        place_q = lax.broadcasted_iota(jnp.int32, (QB, 1), 0) + (4 * rows + i * QB)
        place_q = jnp.concatenate([place_q, place_q], axis=0)
        m_ref[...] = jnp.full_like(m_ref, NEGATIVE)
        l_ref[...] = jnp.zeros_like(l_ref)
        acc_ref[...] = jnp.zeros_like(acc_ref)

        def body(b, carry):
            w = b // per_range
            keys = pl.ds(pl.multiple_of((b - w * per_range) * KB, KB), KB)
            k = win_ref[w, 0, keys, :]
            v = win_ref[w, 1, keys, :]
            s = lax.dot_general(q, k, (((1,), (1,)), ((), ())), preferred_element_type=F32) * scale
            place_k = lax.broadcasted_iota(jnp.int32, (1, KB), 1) + b * KB
            s = jnp.where((place_k <= place_q) & (place_k >= first), s, NEGATIVE)
            m_old = m_ref[...]
            m_new = jnp.maximum(m_old, jnp.max(s, axis=-1, keepdims=True))
            decay = jnp.exp(m_old - m_new)
            p = jnp.exp(s - m_new)
            l_ref[...] = l_ref[...] * decay + jnp.sum(p, axis=-1, keepdims=True)
            acc_ref[...] = acc_ref[...] * decay + jnp.dot(p.astype(BF16), v, preferred_element_type=F32)
            m_ref[...] = m_new
            return carry

        lax.fori_loop(low_ref[i], 4 * per_range + (i + 1) * QB // KB, body, 0)
        out = (acc_ref[...] / l_ref[...]).astype(BF16)
        out_ref[span, :HD] = out[:QB]
        out_ref[span, HD:] = out[QB:]


def attend(low, queries, first, window):
    rows, width = queries.shape
    return pl.pallas_call(
        attention_kernel,
        out_shape=jax.ShapeDtypeStruct((rows, width), BF16),
        in_specs=[pl.BlockSpec(memory_space=pltpu.SMEM)] + [pl.BlockSpec(memory_space=VMEM)] * 3,
        out_specs=pl.BlockSpec(memory_space=VMEM),
        scratch_shapes=[VMEM((2 * QB, 1), F32), VMEM((2 * QB, 1), F32), VMEM((2 * QB, HD), F32)],
        compiler_params=pltpu.CompilerParams(vmem_limit_bytes=32 * 2**20),
        name="attend",
    )(low, queries, first, window)


def mix_kernel(att_ref, wo_ref, emb_ref, gain_ref, stream_ref, all_ref, part, r1, r2, held, s1, e1, s2, e2, gs, gr):
    z, x = here()
    t = lax.axis_index("tensor")
    greet(torus_peers(z, x))

    def finish(cols, value):
        stream_ref[:, cols] = (emb_ref[:, cols].astype(F32) + value).astype(BF16)

    ring_reduce(part, r1, r2, held, s1, e1, s2, e2, z, x, products(att_ref, wo_ref, part, z, x), finish)
    all_ref[t] = normalize(stream_ref[...].astype(F32), gain_ref[...])
    ring_gather(all_ref, gs, gr, z, x)


def mix_and_gather(attended, wo, embedded, gain):
    rows, width = embedded.shape
    return pl.pallas_call(
        mix_kernel,
        out_shape=(
            jax.ShapeDtypeStruct((rows, width), BF16),
            jax.ShapeDtypeStruct((GROUP, rows, width), BF16),
        ),
        in_specs=[pl.BlockSpec(memory_space=VMEM)] * 4,
        out_specs=(pl.BlockSpec(memory_space=VMEM),) * 2,
        scratch_shapes=[*reduce_scratch(rows, width), *GATHER_SEMS],
        compiler_params=pltpu.CompilerParams(
            collective_id=3, has_side_effects=True, vmem_limit_bytes=48 * 2**20
        ),
        name="mix_and_gather",
    )(attended, wo, embedded, gain)


def down_kernel(hid_ref, w_ref, stream_ref, out_ref, part, r1, r2, held, s1, e1, s2, e2):
    z, x = here()
    greet(torus_peers(z, x))

    def finish(cols, value):
        out_ref[:, cols] = (stream_ref[:, cols].astype(F32) + value).astype(BF16)

    ring_reduce(part, r1, r2, held, s1, e1, s2, e2, z, x, products(hid_ref, w_ref, part, z, x), finish)


def down_and_add(hidden, w_down, stream):
    rows, width = stream.shape
    return pl.pallas_call(
        down_kernel,
        out_shape=jax.ShapeDtypeStruct((rows, width), BF16),
        in_specs=[pl.BlockSpec(memory_space=VMEM)] * 3,
        out_specs=pl.BlockSpec(memory_space=VMEM),
        scratch_shapes=reduce_scratch(rows, width),
        compiler_params=pltpu.CompilerParams(
            collective_id=4, has_side_effects=True, vmem_limit_bytes=48 * 2**20
        ),
        name="down_and_add",
    )(hidden, w_down, stream)


def find_rows(ids, range_ids, table):
    t = lax.axis_index("tensor")
    owned = table.shape[0]
    count = ids.shape[0]
    inside = range_ids // owned == t
    earlier = jnp.arange(count)[:, None] < jnp.arange(count)[None, :]
    rank = jnp.sum(jnp.where(inside[:, :, None] & earlier[None], 1, 0), axis=1)
    local_rows = range_ids - t * owned
    wanted = inside[:, None, :] & (rank[:, None, :] == jnp.arange(SLOTS)[None, :, None])
    rows = jnp.sum(jnp.where(wanted, local_rows[:, None, :], 0), axis=2)
    owner = ids // owned
    own_rank = jnp.sum(jnp.where((owner[:, None] == owner[None, :]) & earlier, 1, 0), axis=0)
    found = jnp.take(table, rows.reshape(-1), axis=0).reshape(GROUP, SLOTS, -1)
    return found, (owner * SLOTS + own_rank)[:, None]


def local(ids, doc_lengths, table, attn_gain, wq, wkv, wo, mlp_gain, w_gate, w_up, w_down):
    t = lax.axis_index("tensor")
    r = lax.axis_index("dp")
    own_rows = ids.shape[0]
    width = table.shape[1]
    tok_range = own_rows * GROUP
    q_width = wq.shape[1]
    found, source = find_rows(ids, share_ids(ids), table)
    embedded, normed = embed_and_gather(found, source, attn_gain[None, :])
    normed = normed.reshape(tok_range, width)
    positions = r * tok_range + jnp.arange(tok_range, dtype=jnp.int32)
    first_pos, offsets = document_info(positions, doc_lengths)
    queries = jnp.dot(normed, wq, preferred_element_type=F32).reshape(tok_range, -1, HD)
    queries = rotate(queries, offsets).reshape(tok_range, q_width).astype(BF16)
    pairs = jnp.dot(normed, wkv, preferred_element_type=F32)
    turned = rotate(pairs[:, None, :], offsets)[:, 0, :]
    pairs = jnp.where(t % 2 == 0, turned, pairs).astype(BF16)
    window = share_kv(pairs)
    first = first_pos - (r - 4) * tok_range
    low = first[::QB] // KB
    attended = attend(low, queries, first[:, None], window)
    stream, normed_mlp = mix_and_gather(attended, wo, embedded, mlp_gain[None, :])
    normed_mlp = normed_mlp.reshape(tok_range, width)
    gate_part = jnp.dot(normed_mlp, w_gate, preferred_element_type=F32)
    up_part = jnp.dot(normed_mlp, w_up, preferred_element_type=F32)
    hidden = (jax.nn.silu(gate_part) * up_part).astype(BF16)
    return down_and_add(hidden, w_down, stream)


def solution(mesh):
    placed = (
        P(("dp", "tensor")),
        P(),
        P("tensor", None),
        P(),
        P(None, "tensor"),
        P(None, "tensor"),
        P("tensor", None),
        P(),
        P(None, "tensor"),
        P(None, "tensor"),
        P("tensor", None),
    )
    return jax.shard_map(
        local, mesh=mesh, in_specs=placed, out_specs=P(("dp", "tensor"), None), check_vma=False
    )
```

time: 552 us -> 270 us (0.49)
  waiting for transfers between devices: 383 us -> 0 us
  Pallas kernels: 0 us -> 218 us
  matrix products: 73.8 us -> 16.7 us
  other arithmetic: 42 us -> 10 us
  blocking collectives: 17.6 us -> 0 us
  between operations: 14.3 us -> 0.45 us
    reduce_scatter x3 -> x0, waiting for transfers between devices: 243 us -> none  [the longest x1 83.1 us: local(): lax.psum_scatter(jnp.dot(selected, wo, preferred_element_type=jnp.float32...]
    pallas_call x0 -> x6, Pallas kernels: none -> 218 us  [the longest x1 62.6 us: mix_and_gather(): pl.pallas_call(mix_kernel, out_shape=(jax.ShapeDtypeStruct((rows, width),...]
    all_gather x3 -> x0, waiting for transfers between devices: 135 us -> none  [the longest x1 60.8 us: local(): shard_rows = lax.all_gather(normed_mlp, 'tensor', axis=0, tiled=True)]
    dot_general x7 -> x4, matrix products: 73.8 us -> 16.7 us  [the longest x1 5.99 us: local(): gate_part = jnp.dot(normed_mlp, w_gate, preferred_element_type=F32)]
    reduce_sum x5 -> x3, other arithmetic: 20.4 us -> 0.62 us  [the longest x1 0.35 us: find_rows(): rows = jnp.sum(jnp.where(wanted, local_rows[:, None, :], 0), axis=2)]
    unnamed x1 -> x0, blocking collectives: 17.6 us -> none
    convert_element_type x6 -> x2, other arithmetic: 14 us -> 3.42 us  [the longest x1 2.02 us: local(): queries = rotate(queries, offsets).reshape(tok_range, q_width).astype(BF16)]
    gather x1, local copies, waits for them, and re-layouts: 16.4 us -> 6.67 us  [find_rows(): found = jnp.take(table, rows.reshape(-1), axis=0).reshape(GROUP, SLOTS, -1)]
  transfers between devices with their start and end apart: 7 -> 0, of which waited for: 7 -> 0; matrix products, arithmetic and copies ran while one was open for 2% -> 0% of each run, Pallas kernels for 0% -> 0%
where the time goes in v1:
time: 270 us; the launch traced here: 269 us
  Pallas kernels  218 us (81%)
  local copies, waits for them, and re-layouts  23.5 us (9%)
  matrix products  16.7 us (6%)
  other arithmetic  10 us (4%)
    pallas_call x1, Pallas kernels, mix_and_gather(): pl.pallas_call(mix_kernel, out_shape=(jax.ShapeDtypeStruct((rows, width),...  62.6 us
    pallas_call x1, Pallas kernels, embed_and_gather(): pl.pallas_call(embed_kernel, out_shape=(jax.ShapeDtypeStruct((rows, width...  52.5 us
    pallas_call x1, Pallas kernels, attend(): pl.pallas_call(attention_kernel, out_shape=jax.ShapeDtypeStruct((rows, wi...  45.3 us
    pallas_call x1, Pallas kernels, down_and_add(): pl.pallas_call(down_kernel, out_shape=jax.ShapeDtypeStruct((rows, width),...  27.5 us
    pallas_call x1, Pallas kernels, share_kv(): pl.pallas_call(share_kv_kernel, out_shape=jax.ShapeDtypeStruct((5, 2, row...  18.4 us
    pallas_call x1, Pallas kernels, share_ids(): pl.pallas_call(share_ids_kernel, out_shape=jax.ShapeDtypeStruct((GROUP, 8...  11.9 us
    gather x1, local copies, waits for them, and re-layouts, find_rows(): found = jnp.take(table, rows.reshape(-1), axis=0).reshape(GROUP, SLOTS, -1)  6.67 us
    dot_general x1, matrix products, local(): gate_part = jnp.dot(normed_mlp, w_gate, preferred_element_type=F32)  5.99 us

profile of v1, /device:TPU:16, one launch (start us, length us, event | category | flops | bytes accessed | tf_op | source)
XLA Modules:
  0.0 269.1 jit_solution(2328126919653895475)
XLA Ops:
  2.3 1.3 pad.4.ids_ref
  3.6 11.9 %share_ids.1 = s32[16,8,128]{2,1,0:T(8,128)} custom-call(s32[8,128]{1,0:T(8,128)} %pad.4.ids_ref), custom_call_target="tpu_custom_call" | custom-call | tf_op jit(solution)/shard_map/share_ids/pallas_call | solution.py:305
  15.5 0.9 fusion.12
  16.6 0.9 fusion.9
  18.0 6.7 %gather_fusion = bf16[128,4096]{1,0:T(8,128)(2,1)S(1)} fusion(bf16[1024,4096]{1,0:T(8,128)(2,1)} %param.13, s32[1024]{0:T(1024)S(1)} %pad_clamp_fusion), kind=kCustom, calls=%fused_computation | custom fusion | bytes 2097664 | tf_op jit(solution)/shard_map/jit(_take)/gather | solution.py:645
  25.1 52.5 %embed_and_gather.1 = (bf16[48,4096]{1,0:T(8,128)(2,1)S(1)}, bf16[16,48,4096]{2,1,0:T(8,128)(2,1)S(1)}) custom-call(bf16[16,8,4096]{2,1,0:T(8,128)(2,1)S(1)} %bitcast_select_fusion.found_ref, s32[48,1]{1,0:T(8,128)S(1)} %copy.51.source_ref, f32[1,4096]{1,0:T(1,128)S(1)} %bitcast.35), custom_call_target="tpu_custom_call" | custom-call | tf_op jit(solution)/shard_map/embed_and_gather/pallas_call | solution.py:354
  78.4 2.7 copy-done.9
  81.1 4.3 %copy.68 = bf16[256,4096]{1,0:T(8,128)(2,1)} copy(bf16[256,4096]{0,1:T(8,128)(2,1)} %bitcast.42) | data formatting | bytes 4194304 | tf_op jit(solution)/shard_map/dot_general | solution.py:661
  85.4 5.4 %fusion.13 = f32[768,2,128]{0,2,1:T(8,128)S(1)} fusion(bf16[768,4096,1]{1,0,2:T(8,128)(2,1)} %bitcast.37, bf16[2,128,4096]{2,1,0:T(8,128)(2,1)} %bitcast.43), kind=kOutput, calls=%fused_computation.59 | convolution fusion | flops 1610612736 | bytes 9175040 | tf_op jit(solution)/shard_map/dot_general | solution.py:661
  90.8 1.0 slice_negate_fusion.1
  91.8 1.8 fusion.14
  93.9 1.4 multiply_cosine_fusion
  95.3 1.4 fusion.5
  96.7 1.2 copy.54
  97.9 1.2 copy.53
  99.0 2.0 fusion.1
  101.1 1.3 copy.69.q_ref
  103.2 0.9 copy-done.3
  104.2 18.4 %share_kv.1.win_ref = bf16[5,2,768,128]{3,2,1,0:T(8,128)(2,1)S(1)} custom-call(bf16[768,128]{1,0:T(8,128)(2,1)S(1)} %copy-done.3), custom_call_target="tpu_custom_call" | custom-call | tf_op jit(solution)/shard_map/share_kv/pallas_call | solution.py:509
  123.1 45.3 %attend.1.att_ref = bf16[768,256]{1,0:T(8,128)(2,1)S(1)} custom-call(s32[3]{0:T(128)S(1)} %copy-done.8, bf16[768,256]{1,0:T(8,128)(2,1)S(1)} %copy.69.q_ref, s32[768,1]{1,0:T(8,128)S(1)} %sub.66.first_ref, bf16[5,2,768,128]{3,2,1,0:T(8,128)(2,1)S(1)} %share_kv.1.win_ref), custom_call_target="tpu_custom_call" | custom-call | tf_op jit(solution)/shard_map/attend/pallas_call | solution.py:566
  168.5 62.6 %mix_and_gather.1 = (bf16[48,4096]{1,0:T(8,128)(2,1)S(1)}, bf16[16,48,4096]{2,1,0:T(8,128)(2,1)}) custom-call(bf16[768,256]{1,0:T(8,128)(2,1)S(1)} %attend.1.att_ref, bf16[256,4096]{1,0:T(8,128)(2,1)S(1)} %copy-done.2, bf16[48,4096]{1,0:T(8,128)(2,1)S(1)} %copy-done.5, f32[1,4096]{1,0:T(1,128)S(1)} %bitcast.36), custom_call_target="tpu_custom_call" | custom-call | tf_op jit(solution)/shard_map/mix_and_gather/pallas_call | solution.py:592
  231.1 6.0 %fusion.15 = f32[768,448]{1,0:T(8,128)S(1)} fusion(bf16[768,4096]{1,0:T(8,128)(2,1)} %bitcast.50, bf16[4096,448]{0,1:T(8,128)(2,1)S(1)} %copy-done.15), kind=kOutput, calls=%fused_computation.61 | convolution fusion | flops 2818572288 | bytes 11337728 | tf_op jit(solution)/shard_map/dot_general | solution.py:672
  237.2 3.6 %multiply_convert_fusion.hid_ref = bf16[768,448]{1,0:T(8,128)(2,1)S(1)} fusion(f32[768,448]{1,0:T(8,128)S(1)} %fusion.15, bf16[768,4096]{1,0:T(8,128)(2,1)S(1)} %bitcast.51, bf16[4096,448]{0,1:T(8,128)(2,1)S(1)} %copy-done.16), kind=kOutput, calls=%fused_computation.1 | convolution fusion | flops 2820636672 | bytes 12025856 | tf_op jit(solution)/shard_map/dot_general | solution.py:673
  240.8 27.5 %down_and_add.1 = bf16[48,4096]{1,0:T(8,128)(2,1)S(1)} custom-call(bf16[768,448]{1,0:T(8,128)(2,1)S(1)} %multiply_convert_fusion.hid_ref, bf16[448,4096]{1,0:T(8,128)(2,1)S(1)} %copy-done.1, bf16[48,4096]{1,0:T(8,128)(2,1)S(1)} %get-tuple-element.12.stream_ref), custom_call_target="tpu_custom_call" | custom-call | tf_op jit(solution)/shard_map/down_and_add/pallas_call | solution.py:620
  (64 shorter events, 6.5 us)
Async XLA Ops:
  0.0 91.8 %copy-start = (bf16[4096,128]{1,0:T(8,128)(2,1)S(1)}, bf16[4096,128]{1,0:T(8,128)(2,1)}, u32[]{:S(2)}) copy-start(bf16[4096,128]{1,0:T(8,128)(2,1)} %param.16) | copy-start | bytes 3145732
  1.8 16.2 %copy-start.12 = (s32[768]{0:T(1024)}, s32[768]{0:T(1024)S(1)}, u32[]{:S(2)}) copy-start(s32[768]{0:T(1024)S(1)} %get-tuple-element.25) | copy-start | bytes 9220
  18.0 6.9 %copy-start.13 = (s32[48]{0:T(128)S(1)}, s32[48]{0:T(128)}, u32[]{:S(2)}) copy-start(s32[48]{0:T(128)} %param.11) | copy-start | bytes 580
  18.0 7.1 %copy-start.6 = (f32[4096]{0:T(1024)S(1)}, f32[4096]{0:T(1024)}, u32[]{:S(2)}) copy-start(f32[4096]{0:T(1024)} %param.14) | copy-start | bytes 49156
  77.7 0.8 copy-start.4
  78.4 2.7 copy-start.9
  81.1 10.7 %slice-start = ((s8[6291456]{0:T(1024)(128)(4,1)}), s8[2097152]{0:T(1024)(128)(4,1)S(1)}, s32[]{:S(2)}) async-start(s8[6291456]{0:T(1024)(128)(4,1)} %bitcast.38), calls=%async_computation | async-start | bytes 4194304
  85.4 6.4 %slice-start.1 = ((s8[6291456]{0:T(1024)(128)(4,1)}), s8[4194304]{0:T(1024)(128)(4,1)S(1)}, s32[]{:S(2)}) async-start(s8[6291456]{0:T(1024)(128)(4,1)} %bitcast.38), calls=%async_computation.1 | async-start | bytes 8388608
  90.8 2.8 %copy-start.10 = (f32[768,2,128]{0,2,1:T(8,128)}, f32[768,2,128]{0,2,1:T(8,128)S(1)}, u32[]{:S(2)}) copy-start(f32[768,2,128]{0,2,1:T(8,128)S(1)} %fusion.13) | copy-start | bytes 2359300
  93.6 5.4 %copy-start.11 = (f32[768,2,128]{0,2,1:T(8,128)S(1)}, f32[768,2,128]{0,2,1:T(8,128)}, u32[]{:S(2)}) copy-start(f32[768,2,128]{0,2,1:T(8,128)} %copy-done.10) | copy-start | bytes 2359300
  99.0 69.4 %copy-start.7 = (f32[4096]{0:T(1024)S(1)}, f32[4096]{0:T(1024)}, u32[]{:S(2)}) copy-start(f32[4096]{0:T(1024)} %param.18) | copy-start | bytes 49156
  101.1 67.4 %copy-start.2 = (bf16[256,4096]{1,0:T(8,128)(2,1)S(1)}, bf16[256,4096]{1,0:T(8,128)(2,1)}, u32[]{:S(2)}) copy-start(bf16[256,4096]{1,0:T(8,128)(2,1)} %wo_ref.1) | copy-start | bytes 6291460
  103.2 0.9 copy-start.3
  104.2 64.3 %copy-start.5 = (bf16[48,4096]{1,0:T(8,128)(2,1)S(1)}, bf16[48,4096]{1,0:T(8,128)(2,1)}, u32[]{:S(2)}) copy-start(bf16[48,4096]{1,0:T(8,128)(2,1)} %copy-done.4) | copy-start | bytes 1179652
  122.5 0.6 copy-start.8
  123.1 108.0 %copy-start.15 = (bf16[4096,448]{0,1:T(8,128)(2,1)S(1)}, bf16[4096,448]{0,1:T(8,128)(2,1)}, u32[]{:S(2)}) copy-start(bf16[4096,448]{0,1:T(8,128)(2,1)} %param.19) | copy-start | bytes 11010052
  231.1 6.0 %copy-start.14 = (bf16[16,48,4096]{2,1,0:T(8,128)(2,1)S(1)}, bf16[16,48,4096]{2,1,0:T(8,128)(2,1)}, u32[]{:S(2)}) copy-start(bf16[16,48,4096]{2,1,0:T(8,128)(2,1)} %get-tuple-element.11) | copy-start | bytes 18874372
  231.1 6.0 %copy-start.16 = (bf16[4096,448]{0,1:T(8,128)(2,1)S(1)}, bf16[4096,448]{0,1:T(8,128)(2,1)}, u32[]{:S(2)}) copy-start(bf16[4096,448]{0,1:T(8,128)(2,1)} %param.20) | copy-start | bytes 11010052
  237.2 3.6 %copy-start.1 = (bf16[448,4096]{1,0:T(8,128)(2,1)S(1)}, bf16[448,4096]{1,0:T(8,128)(2,1)}, u32[]{:S(2)}) copy-start(bf16[448,4096]{1,0:T(8,128)(2,1)} %w_ref.1) | copy-start | bytes 11010052

commit v2 on v1

v2 whole, which is shorter than its diff:
```python
import jax
import jax.numpy as jnp
from jax import lax
from jax.experimental import pallas as pl
from jax.experimental.pallas import tpu as pltpu
from jax.sharding import PartitionSpec as P

HD = 128
SIDE = 4
GROUP = SIDE * SIDE
SLOTS = 8

EPSILON = 1e-05
ROPE_BASE = 500000.0
NEGATIVE = -1e30
EXP_SCALE = HD ** (-0.5) * 1.4426950408889634
MESH = pl.DeviceIdType.MESH
VMEM = pltpu.VMEM
DMA = pltpu.SemaphoreType.DMA
BF16 = jnp.bfloat16
F32 = jnp.float32


def document_info(positions, doc_lengths):
    ends = jnp.cumsum(doc_lengths)
    starts = ends - doc_lengths
    began = starts[None, :] <= positions[:, None]
    first_pos = jnp.max(jnp.where(began, starts[None, :], 0), axis=1)
    return first_pos, positions - first_pos


def turns(offsets):
    half_dim = HD // 2
    inverse = ROPE_BASE ** (-jnp.arange(half_dim, dtype=jnp.float32) * 2.0 / HD)
    angle = offsets.astype(jnp.float32)[:, None] * inverse[None, :]
    cosine, sine = jnp.cos(angle), jnp.sin(angle)
    return jnp.concatenate([cosine, cosine], axis=-1), jnp.concatenate([-sine, sine], axis=-1)


def wrap(v):
    return lax.rem(v + 2 * SIDE, SIDE)


def place(z, x):
    return wrap(z) * SIDE + wrap(x)


def here():
    t = lax.axis_index("tensor")
    return t // SIDE, lax.rem(t, SIDE)


def greet(peers):
    barrier = pltpu.get_barrier_semaphore()
    for peer in peers:
        pl.semaphore_signal(barrier, inc=1, device_id=peer, device_id_type=MESH)
    pl.semaphore_wait(barrier, len(peers))


def torus_peers(z, x):
    return [{"tensor": place(z + a, x + b)} for a, b in ((0, 1), (0, -1), (1, 0), (-1, 0))]


def remote(src, dst, send_sem, recv_sem, peer):
    return pltpu.make_async_remote_copy(
        src_ref=src, dst_ref=dst, send_sem=send_sem, recv_sem=recv_sem,
        device_id=peer, device_id_type=MESH,
    )


def ring_gather(buf, ssem, rsem, z, x, ready):
    half = buf.shape[-1] // 2
    quarter = half // 2
    started = []

    def block(h, first, second):
        return place(z + second, x + first) if h == 0 else place(z + first, x + second)

    def view(h, first, second, part):
        start, size = (h * half, half) if part == 0 else (h * half + (part - 1) * quarter, quarter)
        return buf.at[block(h, first, second), :, pl.ds(start, size)]

    def send(h, n, first, second, part, axis, d):
        ref = view(h, first, second, part)
        peer = {"tensor": block(h, d, 0) if axis == 0 else block(h, 0, d)}
        copy = remote(ref, ref, ssem.at[h, n], rsem.at[h, n], peer)
        copy.start()
        started.append(copy)

    def recv(h, n, first, second, part):
        ref = view(h, first, second, part)
        remote(ref, ref, ssem.at[h, n], rsem.at[h, n], {"tensor": block(h, 1, 0)}).wait_recv()

    offsets = (0, -1, 1, 2)
    for h in range(2):
        send(h, 0, 0, 0, 0, 0, 1)
        send(h, 1, 0, 0, 0, 0, -1)
    for h in range(2):
        send(h, 4, 0, 0, 0, 1, 1)
        send(h, 5, 0, 0, 0, 1, -1)
    for h in range(2):
        recv(h, 0, -1, 0, 0)
        send(h, 2, -1, 0, 1, 0, 1)
        recv(h, 1, 1, 0, 0)
        send(h, 3, 1, 0, 2, 0, -1)
        for n in (1, 2):
            send(h, 4 + 2 * n, offsets[n], 0, 0, 1, 1)
            send(h, 5 + 2 * n, offsets[n], 0, 0, 1, -1)

    def relay(n):
        k = offsets[n]
        for h in range(2):
            recv(h, 4 + 2 * n, k, -1, 0)
            send(h, 12 + 2 * n, k, -1, 1, 1, 1)
            recv(h, 5 + 2 * n, k, 1, 0)
            send(h, 13 + 2 * n, k, 1, 2, 1, -1)

    relay(0)
    for h in range(2):
        recv(h, 2, 2, 0, 1)
        recv(h, 3, 2, 0, 2)
        send(h, 10, 2, 0, 0, 1, 1)
        send(h, 11, 2, 0, 0, 1, -1)
    relay(1)
    relay(2)

    def far(h, n):
        recv(h, 12 + 2 * n, offsets[n], 2, 1)
        recv(h, 13 + 2 * n, offsets[n], 2, 2)

    far(1, 0)
    ready(0)
    relay(3)
    far(1, 1)
    ready(-1)
    far(1, 2)
    ready(1)
    for n in range(4):
        far(0, n)
    far(1, 3)
    ready(2)
    for copy in started:
        copy.wait_send()


GATHER_SEMS = [DMA((2, 20)), DMA((2, 20))]


def ring_reduce(part, r1, r2, held, s1, e1, s2, e2, z, x, make, finish):
    half = part.shape[-1] // 2
    quarter = half // 2
    started = []

    def at(h, k, j):
        return (wrap(z + k), wrap(x + j)) if h == 0 else (wrap(z + j), wrap(x + k))

    def mine(h, k, j, q):
        a, b = at(h, k, j)
        return part.at[a, b, :, pl.ds(h * half + q * quarter, quarter)]

    def peer(h, axis, d):
        a, b = at(h, d, 0) if axis == 0 else at(h, 0, d)
        return {"tensor": a * SIDE + b}

    def send1(h, slot, j, src, d):
        copy = remote(src, r1.at[h, slot, j], s1.at[h, slot, j], e1.at[h, slot, j], peer(h, 0, d))
        copy.start()
        started.append(copy)

    def recv1(h, slot, j):
        ref = r1.at[h, slot, j]
        remote(ref, ref, s1.at[h, slot, j], e1.at[h, slot, j], peer(h, 0, 1)).wait_recv()

    def send2(h, slot, src, d):
        copy = remote(src, r2.at[h, slot], s2.at[h, slot], e2.at[h, slot], peer(h, 1, d))
        copy.start()
        started.append(copy)

    def recv2(h, slot):
        ref = r2.at[h, slot]
        remote(ref, ref, s2.at[h, slot], e2.at[h, slot], peer(h, 0, 1)).wait_recv()

    def load(ref):
        return ref[...].astype(F32)

    order = (2, 1, 3, 0)
    for h in range(2):
        make(h, 2)
        for j in order:
            send1(h, 0, j, mine(h, 2, j, 0), 1)
            send1(h, 3, j, mine(h, 2, j, 1), -1)
    for h in range(2):
        make(h, 1)
        for j in order:
            send1(h, 1, j, mine(h, 1, j, 1), 1)
        make(h, 3)
        for j in order:
            send1(h, 4, j, mine(h, 3, j, 0), -1)
    for j in order:
        for h in range(2):
            recv1(h, 0, j)
            r1[h, 0, j] = (load(r1.at[h, 0, j]) + load(mine(h, 1, j, 0))).astype(BF16)
            send1(h, 2, j, r1.at[h, 0, j], 1)
            recv1(h, 3, j)
            r1[h, 3, j] = (load(r1.at[h, 3, j]) + load(mine(h, 3, j, 1))).astype(BF16)
            send1(h, 5, j, r1.at[h, 3, j], -1)
    for h in range(2):
        make(h, 0)

    def arrived(h, j):
        for slot in (1, 4, 2, 5):
            recv1(h, slot, j)

    def summed(h, j, q):
        a, b = ((2, 4), (1, 5))[q]
        return load(mine(h, 0, j, q)) + load(r1.at[h, a, j]) + load(r1.at[h, b, j])

    for h in range(2):
        arrived(h, 2)
        for q, slot, d in ((0, 0, 1), (1, 3, -1)):
            held[h, 0, q] = summed(h, 2, q).astype(BF16)
            send2(h, slot, held.at[h, 0, q], d)
    for h in range(2):
        arrived(h, 1)
        held[h, 1, 1] = summed(h, 1, 1).astype(BF16)
        send2(h, 1, held.at[h, 1, 1], 1)
        arrived(h, 3)
        held[h, 2, 0] = summed(h, 3, 0).astype(BF16)
        send2(h, 4, held.at[h, 2, 0], -1)
    for h in range(2):
        recv2(h, 0)
        held[h, 1, 0] = (summed(h, 1, 0) + load(r2.at[h, 0])).astype(BF16)
        send2(h, 2, held.at[h, 1, 0], 1)
        recv2(h, 3)
        held[h, 2, 1] = (summed(h, 3, 1) + load(r2.at[h, 3])).astype(BF16)
        send2(h, 5, held.at[h, 2, 1], -1)
    for h in range(2):
        arrived(h, 0)
        for slot in (1, 4, 2, 5):
            recv2(h, slot)
        for q in range(2):
            a, b = ((2, 4), (1, 5))[q]
            value = summed(h, 0, q) + load(r2.at[h, a]) + load(r2.at[h, b])
            finish(pl.ds(h * half + q * quarter, quarter), value)
    for copy in started:
        copy.wait_send()


def reduce_scratch(rows, width):
    quarter = width // 4
    return [
        VMEM((SIDE, SIDE, rows, width), BF16),
        VMEM((2, 6, SIDE, rows, quarter), BF16),
        VMEM((2, 6, rows, quarter), BF16),
        VMEM((2, 3, 2, rows, quarter), BF16),
        DMA((2, 6, SIDE)), DMA((2, 6, SIDE)), DMA((2, 6)), DMA((2, 6)),
    ]


def products(a_ref, w_ref, part, z, x):
    rows, width = part.shape[2], part.shape[3]
    half = width // 2
    step = min(512, half)

    def make(h, k):
        def run(blocks):
            lhs = jnp.concatenate(
                [a_ref[pl.ds(pl.multiple_of((a * SIDE + b) * rows, 16), rows), :] for a, b in blocks], axis=0
            )

            def column(c, carry):
                cols = pl.ds(pl.multiple_of(h * half + c * step, step), step)
                out = jnp.dot(lhs, w_ref[:, cols], preferred_element_type=F32).astype(BF16)
                for n, (a, b) in enumerate(blocks):
                    part[a, b, :, cols] = out[n * rows:(n + 1) * rows]
                return carry

            lax.fori_loop(0, half // step, column, 0)

        if h == 0:
            run([(wrap(z + k), b) for b in range(SIDE)])
        else:
            run([(a, wrap(x + k)) for a in range(SIDE)])

    return make


def normalize(rows, gain):
    scale = lax.rsqrt(jnp.mean(rows * rows, axis=-1, keepdims=True) + EPSILON)
    return (rows * scale * gain).astype(BF16)


def row_group(all_ref, z, dz):
    rows, width = all_ref.shape[1:]
    zz = wrap(z + dz)
    lhs = all_ref[pl.ds(zz * SIDE, SIDE)].reshape(SIDE * rows, width)
    return lhs, pl.ds(pl.multiple_of(zz * SIDE * rows, 16), SIDE * rows)


def front_kernel(ids_ref, source_ref, gain_ref, cos_ref, sin_ref, table_hbm, wq_hbm, wkv_hbm,
                 emb_ref, q_ref, pair_ref,
                 table, wq, wkv, all_ids, found, recv, all_ref, load_sem, ks, kr, xs, xr, gs, gr):
    z, x = here()
    t = lax.axis_index("tensor")
    loads = [
        pltpu.make_async_copy(src, dst, load_sem.at[n])
        for n, (src, dst) in enumerate(((table_hbm, table), (wq_hbm, wq), (wkv_hbm, wkv)))
    ]
    for load in loads:
        load.start()
    peers = [lax.rem(t + n, GROUP) for n in range(1, GROUP)]
    sources = [lax.rem(t + GROUP - n, GROUP) for n in range(1, GROUP)]
    greet([{"tensor": p} for p in peers])
    copies = []
    for n, p in enumerate(peers):
        copy = remote(ids_ref, all_ids.at[t], ks.at[n], kr.at[n], {"tensor": p})
        copy.start()
        copies.append(copy)
    all_ids[t] = ids_ref[...]
    for n, p in enumerate(sources):
        remote(ids_ref, all_ids.at[p], ks.at[n], kr.at[n], {"tensor": p}).wait_recv()
    slots = GROUP * SLOTS
    owned, width = table.shape
    ids = all_ids[...].reshape(slots, 128)
    local_rows = ids - t * owned
    inside = (local_rows >= 0) & (local_rows < owned)
    square = (128, 128)
    earlier = lax.broadcasted_iota(jnp.int32, square, 0) < lax.broadcasted_iota(jnp.int32, square, 1)
    rank = jnp.dot(
        jnp.where(inside, 1.0, 0.0).astype(BF16), jnp.where(earlier, 1.0, 0.0).astype(BF16),
        preferred_element_type=F32,
    )
    slot = lax.rem(lax.broadcasted_iota(jnp.int32, (slots, 128), 0), SLOTS).astype(F32)
    wanted = jnp.sum(
        jnp.where(inside & (rank == slot), local_rows.astype(F32), 0.0), axis=1, keepdims=True
    )
    pick = lax.broadcasted_iota(jnp.int32, (slots, owned), 1).astype(F32) == wanted
    pick = jnp.where(pick, 1.0, 0.0).astype(BF16)
    loads[0].wait()
    parts = 2
    step = width // parts
    for c in range(parts):
        def fetch(b, carry):
            cols = pl.ds(pl.multiple_of(c * step + b * 512, 512), 512)
            rows = jnp.dot(pick, table[:, cols], preferred_element_type=F32).astype(BF16)
            found[:, :, cols] = rows.reshape(GROUP, SLOTS, 512)
            return carry

        lax.fori_loop(0, step // 512, fetch, 0)
        cols = pl.ds(c * step, step)
        for n, p in enumerate(peers):
            copy = remote(found.at[p, :, cols], recv.at[t, :, cols], xs.at[c, n], xr.at[c, n], {"tensor": p})
            copy.start()
            copies.append(copy)
        recv[t, :, cols] = found[t, :, cols]
    rows = emb_ref.shape[0]
    lanes = lax.broadcasted_iota(jnp.int32, (rows, slots), 1)
    chosen = jnp.where(source_ref[...] == lanes, 1.0, 0.0).astype(BF16)
    total = jnp.zeros((rows, 1), F32)
    for c in range(parts):
        cols = pl.ds(c * step, step)
        for n, p in enumerate(sources):
            ref = recv.at[p, :, cols]
            remote(ref, ref, xs.at[c, n], xr.at[c, n], {"tensor": p}).wait_recv()
        for b in range(step // 1024):
            cols = pl.ds(c * step + b * 1024, 1024)
            picked = jnp.dot(chosen, recv[:, :, cols].reshape(slots, 1024), preferred_element_type=F32)
            emb_ref[:, cols] = picked.astype(BF16)
            total += jnp.sum(picked * picked, axis=-1, keepdims=True)
    scale = lax.rsqrt(total / width + EPSILON)
    for b in range(width // 1024):
        cols = pl.ds(b * 1024, 1024)
        all_ref[t, :, cols] = (emb_ref[:, cols].astype(F32) * scale * gain_ref[:, cols]).astype(BF16)
    loads[1].wait()
    loads[2].wait()
    keys_here = lax.rem(t, 2) == 0

    def project(dz):
        lhs, span = row_group(all_ref, z, dz)
        cos, sin = cos_ref[span, :], sin_ref[span, :]
        queries = jnp.dot(lhs, wq[...], preferred_element_type=F32)
        for h in range(queries.shape[1] // HD):
            head = queries[:, h * HD:(h + 1) * HD]
            q_ref[span, h * HD:(h + 1) * HD] = (head * cos + pltpu.roll(head, HD // 2, 1) * sin).astype(BF16)
        pair = jnp.dot(lhs, wkv[...], preferred_element_type=F32)
        turned = pair * cos + pltpu.roll(pair, HD // 2, 1) * sin
        pair_ref[span, :] = jnp.where(keys_here, turned, pair).astype(BF16)

    ring_gather(all_ref, gs, gr, z, x, project)
    for copy in copies:
        copy.wait_send()


def front(ids, source, gain, cos, sin, table, wq, wkv):
    rows, width = ids.shape[0], table.shape[1]
    span = rows * GROUP
    padded = jnp.broadcast_to(jnp.pad(ids, (0, 128 - rows), constant_values=-1)[None, :], (8, 128))
    whole = pl.BlockSpec(memory_space=VMEM)
    outside = pl.BlockSpec(memory_space=pl.ANY)
    return pl.pallas_call(
        front_kernel,
        out_shape=(
            jax.ShapeDtypeStruct((rows, width), BF16),
            jax.ShapeDtypeStruct((span, wq.shape[1]), BF16),
            jax.ShapeDtypeStruct((span, wkv.shape[1]), BF16),
        ),
        in_specs=[whole] * 5 + [outside] * 3,
        out_specs=(whole,) * 3,
        scratch_shapes=[
            VMEM(table.shape, BF16), VMEM(wq.shape, BF16), VMEM(wkv.shape, BF16),
            VMEM((GROUP, 8, 128), jnp.int32),
            VMEM((GROUP, SLOTS, width), BF16), VMEM((GROUP, SLOTS, width), BF16),
            VMEM((GROUP, rows, width), BF16),
            DMA((3,)), DMA((GROUP - 1,)), DMA((GROUP - 1,)), DMA((2, GROUP - 1)), DMA((2, GROUP - 1)),
            *GATHER_SEMS,
        ],
        compiler_params=pltpu.CompilerParams(
            collective_id=0, has_side_effects=True, vmem_limit_bytes=48 * 2**20
        ),
        name="front",
    )(padded, source, gain, cos, sin, table, wq, wkv)


QB = 256


def attention(q_ref, first_ref, pair_ref, att_ref, win_ref, relay, m_ref, l_ref, acc_ref, ssem, rsem):
    t = lax.axis_index("tensor")
    r = lax.axis_index("dp")
    y, c = r // 2, lax.rem(r, 2)
    kind = lax.rem(t, 2)
    rows = q_ref.shape[0]
    blocks = rows // QB
    partner = {"tensor": t + 1 - 2 * kind}
    up = {"dp": lax.rem(y + 1, SIDE) * 2 + c}
    down = {"dp": lax.rem(y + SIDE - 1, SIDE) * 2 + c}
    other = {"dp": y * 2 + 1 - c}

    def copy(n, src, dst, peer):
        return remote(src, dst, ssem.at[n], rsem.at[n], peer)

    def step(w, i, count, causal):
        span = pl.ds(i * QB, QB)
        q = jnp.concatenate([q_ref[span, :HD], q_ref[span, HD:]], axis=0)
        first = first_ref[:, span]
        first = jnp.concatenate([first, first], axis=1)
        scores = lax.dot_general(
            win_ref[w, 0, :count, :], q, (((1,), (1,)), ((), ())), preferred_element_type=F32
        )
        at = lax.broadcasted_iota(jnp.int32, (count, 1), 0) + w * rows
        allowed = at >= first
        if causal:
            query = lax.broadcasted_iota(jnp.int32, (1, QB), 1) + (4 * rows + i * QB)
            allowed &= at <= jnp.concatenate([query, query], axis=1)
        scores = jnp.where(allowed, scores, NEGATIVE)
        top = jnp.max(scores, axis=0, keepdims=True) * EXP_SCALE
        if not causal:
            old = m_ref[i]
            top = jnp.maximum(old, top)
            decay = jnp.exp2(old - top)
        weights = jnp.exp2(scores * EXP_SCALE - top)
        total = jnp.sum(weights, axis=0, keepdims=True)
        added = lax.dot_general(
            win_ref[w, 1, :count, :], weights.astype(BF16), (((0,), (0,)), ((), ())),
            preferred_element_type=F32,
        )
        l_ref[i] = total if causal else l_ref[i] * decay + total
        acc_ref[i] = added if causal else acc_ref[i] * decay + added
        m_ref[i] = top

    def earlier(w):
        @pl.when(r + w >= 4)
        def _():
            for i in range(blocks):
                step(w, i, rows, False)

    swap = copy(0, pair_ref, win_ref.at[4, kind], partner)
    swap.start()
    win_ref[4, kind] = pair_ref[...]
    swap_in = copy(0, pair_ref, win_ref.at[4, 1 - kind], partner)
    up_key = copy(1, win_ref.at[4, 0], win_ref.at[2, 0], up)
    up_value = copy(2, win_ref.at[4, 1], win_ref.at[2, 1], up)
    far_key = copy(3, win_ref.at[2, 0], win_ref.at[0, 0], up)
    down_value = copy(4, win_ref.at[4, 1], relay, down)
    far_value = copy(5, relay, win_ref.at[0, 1], down)
    near = [copy(6 + k, win_ref.at[4, k], win_ref.at[3, k], other) for k in range(2)]
    cross0 = [copy(8 + k, win_ref.at[2, k], win_ref.at[1, k], other) for k in range(2)]
    cross1 = [copy(8 + k, win_ref.at[2, k], win_ref.at[3, k], other) for k in range(2)]
    far1 = [copy(10 + k, win_ref.at[0, k], win_ref.at[1, k], other) for k in range(2)]
    has_up, has_far = y < SIDE - 1, y < SIDE - 2
    got_up, got_far = y > 0, y > 1
    relays = (y == SIDE - 1) | (y == 0)
    swap_in.wait_recv()

    @pl.when(has_far)
    def _():
        down_value.start()

    @pl.when(has_up)
    def _():
        up_key.start()
        up_value.start()

    @pl.when(c == 0)
    def _():
        for k in range(2):
            near[k].start()

    for i in range(blocks):
        step(4, i, (i + 1) * QB, True)

    @pl.when(relays)
    def _():
        down_value.wait_recv()
        far_value.start()

    @pl.when(got_up)
    def _():
        up_key.wait_recv()

        @pl.when(has_up)
        def _():
            far_key.start()

        up_value.wait_recv()

        @pl.when(c == 0)
        def _():
            for k in range(2):
                cross0[k].start()

        @pl.when(c == 1)
        def _():
            for k in range(2):
                cross1[k].start()

    @pl.when(c == 1)
    def _():
        for k in range(2):
            near[k].wait_recv()

    earlier(2 + c)

    @pl.when(got_up & (c == 0))
    def _():
        for k in range(2):
            cross1[k].wait_recv()

    earlier(3 - c)

    @pl.when(got_far)
    def _():
        far_key.wait_recv()
        far_value.wait_recv()

        @pl.when(c == 1)
        def _():
            for k in range(2):
                far1[k].start()

    @pl.when(got_up & (c == 1))
    def _():
        for k in range(2):
            cross0[k].wait_recv()

    earlier(c)

    @pl.when(got_far & (c == 0))
    def _():
        for k in range(2):
            far1[k].wait_recv()

    earlier(1 - c)
    for i in range(blocks):
        span = pl.ds(i * QB, QB)
        out = acc_ref[i] / l_ref[i]
        att_ref[span, :HD] = out[:, :QB].T.astype(BF16)
        att_ref[span, HD:] = out[:, QB:].T.astype(BF16)

    @pl.when(c == 0)
    def _():
        for k in range(2):
            near[k].wait_send()

    @pl.when(got_up & (c == 0))
    def _():
        for k in range(2):
            cross0[k].wait_send()

    @pl.when(got_up & (c == 1))
    def _():
        for k in range(2):
            cross1[k].wait_send()

    @pl.when(got_far & (c == 1))
    def _():
        for k in range(2):
            far1[k].wait_send()

    @pl.when(has_far)
    def _():
        down_value.wait_send()

    @pl.when(has_up)
    def _():
        up_key.wait_send()
        up_value.wait_send()

    @pl.when(relays)
    def _():
        far_value.wait_send()

    @pl.when(got_up & has_up)
    def _():
        far_key.wait_send()

    swap.wait_send()


def back_kernel(pair_ref, q_ref, first_ref, emb_ref, gain_ref, wo_hbm, wg_hbm, wu_hbm, wd_hbm, out_ref,
                wo, wg, wu, wd, win, relay, m_ref, l_ref, acc_ref, att, stream, all_ref, hid, load_sem, as_, ar,
                part, r1, r2, held, s1, e1, s2, e2, part_b, r1b, r2b, held_b, s1b, e1b, s2b, e2b, gs, gr):
    z, x = here()
    t = lax.axis_index("tensor")
    r = lax.axis_index("dp")
    y, c = r // 2, lax.rem(r, 2)
    loads = [
        pltpu.make_async_copy(src, dst, load_sem.at[n])
        for n, (src, dst) in enumerate(((wo_hbm, wo), (wg_hbm, wg), (wu_hbm, wu), (wd_hbm, wd)))
    ]
    for load in loads:
        load.start()
    greet(torus_peers(z, x) + [
        {"dp": lax.rem(y + 1, SIDE) * 2 + c}, {"dp": lax.rem(y + SIDE - 1, SIDE) * 2 + c}, {"dp": y * 2 + 1 - c},
    ])
    attention(q_ref, first_ref, pair_ref, att, win, relay, m_ref, l_ref, acc_ref, as_, ar)

    def mixed(cols, value):
        stream[:, cols] = (emb_ref[:, cols].astype(F32) + value).astype(BF16)

    loads[0].wait()
    ring_reduce(part, r1, r2, held, s1, e1, s2, e2, z, x, products(att, wo, part, z, x), mixed)
    all_ref[t] = normalize(stream[...].astype(F32), gain_ref[...])
    loads[1].wait()
    loads[2].wait()

    def gate(dz):
        lhs, span = row_group(all_ref, z, dz)
        gated = jnp.dot(lhs, wg[...], preferred_element_type=F32)
        upper = jnp.dot(lhs, wu[...], preferred_element_type=F32)
        hid[span, :] = (gated / (1.0 + jnp.exp(-gated)) * upper).astype(BF16)

    ring_gather(all_ref, gs, gr, z, x, gate)

    def added(cols, value):
        out_ref[:, cols] = (stream[:, cols].astype(F32) + value).astype(BF16)

    loads[3].wait()
    ring_reduce(part_b, r1b, r2b, held_b, s1b, e1b, s2b, e2b, z, x, products(hid, wd, part_b, z, x), added)


def back(pair, queries, first, embedded, gain, wo, w_gate, w_up, w_down):
    rows, width = embedded.shape
    span = rows * GROUP
    blocks = span // QB
    whole = pl.BlockSpec(memory_space=VMEM)
    outside = pl.BlockSpec(memory_space=pl.ANY)
    return pl.pallas_call(
        back_kernel,
        out_shape=jax.ShapeDtypeStruct((rows, width), BF16),
        in_specs=[whole] * 5 + [outside] * 4,
        out_specs=whole,
        scratch_shapes=[
            VMEM(wo.shape, BF16), VMEM(w_gate.shape, BF16), VMEM(w_up.shape, BF16), VMEM(w_down.shape, BF16),
            VMEM((5, 2, span, HD), BF16), VMEM((span, HD), BF16),
            VMEM((blocks, 1, 2 * QB), F32), VMEM((blocks, 1, 2 * QB), F32), VMEM((blocks, HD, 2 * QB), F32),
            VMEM((span, 2 * HD), BF16), VMEM((rows, width), BF16),
            VMEM((GROUP, rows, width), BF16), VMEM((span, w_gate.shape[1]), BF16),
            DMA((4,)), DMA((12,)), DMA((12,)),
            *reduce_scratch(rows, width), *reduce_scratch(rows, width), *GATHER_SEMS,
        ],
        compiler_params=pltpu.CompilerParams(
            collective_id=1, has_side_effects=True, vmem_limit_bytes=62 * 2**20
        ),
        name="back",
    )(pair, queries, first, embedded, gain, wo, w_gate, w_up, w_down)


def local(ids, doc_lengths, table, attn_gain, wq, wkv, wo, mlp_gain, w_gate, w_up, w_down):
    r = lax.axis_index("dp")
    own_rows = ids.shape[0]
    tok_range = own_rows * GROUP
    owner = ids // table.shape[0]
    earlier = jnp.arange(own_rows)[:, None] < jnp.arange(own_rows)[None, :]
    own_rank = jnp.sum(jnp.where((owner[:, None] == owner[None, :]) & earlier, 1, 0), axis=0)
    source = (owner * SLOTS + own_rank)[:, None]
    positions = r * tok_range + jnp.arange(tok_range, dtype=jnp.int32)
    first_pos, offsets = document_info(positions, doc_lengths)
    cos, sin = turns(offsets)
    embedded, queries, pair = front(ids, source, attn_gain[None, :], cos, sin, table, wq, wkv)
    first = (first_pos - (r - 4) * tok_range)[None, :]
    return back(pair, queries, first, embedded, mlp_gain[None, :], wo, w_gate, w_up, w_down)


def solution(mesh):
    placed = (
        P(("dp", "tensor")),
        P(),
        P("tensor", None),
        P(),
        P(None, "tensor"),
        P(None, "tensor"),
        P("tensor", None),
        P(),
        P(None, "tensor"),
        P(None, "tensor"),
        P("tensor", None),
    )
    return jax.shard_map(
        local, mesh=mesh, in_specs=placed, out_specs=P(("dp", "tensor"), None), check_vma=False
    )
```

time: 270 us -> 220 us (0.81)
  Pallas kernels: 218 us -> 195 us
  matrix products: 16.7 us -> 0 us
  other arithmetic: 10 us -> 4.21 us
  local copies, waits for them, and re-layouts: 23.5 us -> 19.8 us
    pallas_call x6 -> x2, Pallas kernels: 218 us -> 195 us  [the longest x1 133 us: back(): pl.pallas_call(back_kernel, out_shape=jax.ShapeDtypeStruct((rows, width),...]
    dot_general x4 -> x0, matrix products: 16.7 us -> none  [the longest x1 5.99 us: local(): gate_part = jnp.dot(normed_mlp, w_gate, preferred_element_type=F32)]
    unnamed x40 -> x15, local copies, waits for them, and re-layouts: 5.73 us -> 17.6 us
    gather x1 -> x0, local copies, waits for them, and re-layouts: 6.67 us -> none  [find_rows(): found = jnp.take(table, rows.reshape(-1), axis=0).reshape(GROUP, SLOTS, -1)]
    dot_general x1 -> x0, local copies, waits for them, and re-layouts: 4.32 us -> none  [local(): jnp.dot(normed, wq, preferred_element_type=F32).reshape(tok_range, -1, HD)]
    convert_element_type x3 -> x0, other arithmetic: 3.43 us -> none  [the longest x1 2.02 us: local(): queries = rotate(queries, offsets).reshape(tok_range, q_width).astype(BF16)]
where the time goes in v2:
time: 220 us; the launch traced here: 219 us
  Pallas kernels  195 us (89%)
  local copies, waits for them, and re-layouts  19.8 us (9%)
  other arithmetic  4.21 us (2%)
    pallas_call x1, Pallas kernels, back(): pl.pallas_call(back_kernel, out_shape=jax.ShapeDtypeStruct((rows, width),...  133 us
    pallas_call x1, Pallas kernels, front(): pl.pallas_call(front_kernel, out_shape=(jax.ShapeDtypeStruct((rows, width...  61.9 us
    unnamed x15, local copies, waits for them, and re-layouts  17.6 us

profile of v2, /device:TPU:16, one launch (start us, length us, event | category | flops | bytes accessed | tf_op | source)
XLA Modules:
  0.0 218.7 jit_solution(1920384417055965197)
XLA Ops:
  0.0 0.8 pad.4
  0.8 0.8 and_select_fusion
  1.6 0.1 select_reduce_fusion.1
  1.7 0.7 add_bitcast_fusion
  2.4 0.7 copy.20
  3.2 0.1 reduce
  3.3 0.7 sub.36
  4.0 0.1 select_reduce_fusion
  4.1 0.6 sub.41.first_ref
  4.7 0.1 copy.21.source_ref
  4.8 1.4 fusion
  6.2 0.3 pad_maximum_fusion
  6.5 0.0 copy-done.1
  6.5 0.0 copy-done
  6.5 0.0 copy-start.5
  6.5 0.7 copy-done.5
  7.2 61.9 %front.1 = (bf16[48,4096]{1,0:T(8,128)(2,1)S(1)}, bf16[768,256]{1,0:T(8,128)(2,1)S(1)}, bf16[768,128]{1,0:T(8,128)(2,1)S(1)}) custom-call(s32[8,128]{1,0:T(8,128)S(1)} %broadcast_in_dim.26.ids_ref, s32[48,1]{1,0:T(8,128)S(1)} %copy.21.source_ref, f32[1,4096]{1,0:T(1,128)S(1)} %bitcast.5, f32[768,128]{1,0:T(8,128)S(1)} %get-tuple-element.16.cos_ref, ...), custom_call_target="tpu_custom_call" | custom-call | tf_op jit(solution)/shard_map/front/pallas_call | solution.py:400
  69.1 0.8 copy-done.2
  69.9 0.7 copy-done.3
  70.7 0.7 copy-done.4
  71.4 6.4 %copy.22.wg_hbm = bf16[4096,448]{1,0:T(8,128)(2,1)} copy(bf16[4096,448]{0,1:T(8,128)(2,1)} %param.19) | data formatting | bytes 7340032 | tf_op args[8]
  77.8 6.5 %copy.23.wu_hbm = bf16[4096,448]{1,0:T(8,128)(2,1)} copy(bf16[4096,448]{0,1:T(8,128)(2,1)} %param.20) | data formatting | bytes 7340032 | tf_op args[9]
  84.2 132.7 %back.1 = bf16[48,4096]{1,0:T(8,128)(2,1)} custom-call(bf16[768,128]{1,0:T(8,128)(2,1)} %copy-done.4, bf16[768,256]{1,0:T(8,128)(2,1)} %copy-done.3, s32[1,768]{1,0:T(1,128)} %sub.41.first_ref, bf16[48,4096]{1,0:T(8,128)(2,1)} %copy-done.2, f32[1,4096]{1,0:T(1,128)} %bitcast.6, bf16[256,4096]{1,0:T(8,128)(2,1)} %wo_hbm.1, bf16[4096,448]{1,0:T(8,128)(2,1)} %copy.22.wg_hbm, ...), custom_call_target="tpu_custom_call" | custom-call | tf_op jit(solution)/shard_map/back/pallas_call | solution.py:668
  217.0 1.8 copy.25
  (10 shorter events, 0.1 us)
Async XLA Ops:
  0.0 6.5 %copy-start.1 = (bf16[4096,128]{1,0:T(8,128)(2,1)S(1)}, bf16[4096,128]{1,0:T(8,128)(2,1)}, u32[]{:S(2)}) copy-start(bf16[4096,128]{1,0:T(8,128)(2,1)} %wkv_hbm.1) | copy-start | bytes 3145732
  0.0 6.5 %copy-start = (bf16[4096,256]{1,0:T(8,128)(2,1)S(1)}, bf16[4096,256]{1,0:T(8,128)(2,1)}, u32[]{:S(2)}) copy-start(bf16[4096,256]{1,0:T(8,128)(2,1)} %wq_hbm.1) | copy-start | bytes 6291460
  6.5 0.7 copy-start.5
  69.1 0.8 copy-start.2
  69.9 0.7 copy-start.3
  70.7 0.7 copy-start.4

commit v3 on v2

--- a/solution.py
+++ b/solution.py
@@ -19,22 +19,6 @@
 DMA = pltpu.SemaphoreType.DMA
 BF16 = jnp.bfloat16
 F32 = jnp.float32
-
-
-def document_info(positions, doc_lengths):
-    ends = jnp.cumsum(doc_lengths)
-    starts = ends - doc_lengths
-    began = starts[None, :] <= positions[:, None]
-    first_pos = jnp.max(jnp.where(began, starts[None, :], 0), axis=1)
-    return first_pos, positions - first_pos
-
-
-def turns(offsets):
-    half_dim = HD // 2
-    inverse = ROPE_BASE ** (-jnp.arange(half_dim, dtype=jnp.float32) * 2.0 / HD)
-    angle = offsets.astype(jnp.float32)[:, None] * inverse[None, :]
-    cosine, sine = jnp.cos(angle), jnp.sin(angle)
-    return jnp.concatenate([cosine, cosine], axis=-1), jnp.concatenate([-sine, sine], axis=-1)
 
 
 def wrap(v):
@@ -246,17 +230,6 @@
         copy.wait_send()
 
 
-def reduce_scratch(rows, width):
-    quarter = width // 4
-    return [
-        VMEM((SIDE, SIDE, rows, width), BF16),
-        VMEM((2, 6, SIDE, rows, quarter), BF16),
-        VMEM((2, 6, rows, quarter), BF16),
-        VMEM((2, 3, 2, rows, quarter), BF16),
-        DMA((2, 6, SIDE)), DMA((2, 6, SIDE)), DMA((2, 6)), DMA((2, 6)),
-    ]
-
-
 def products(a_ref, w_ref, part, z, x):
     rows, width = part.shape[2], part.shape[3]
     half = width // 2
@@ -297,53 +270,45 @@
     return lhs, pl.ds(pl.multiple_of(zz * SIDE * rows, 16), SIDE * rows)
 
 
-def front_kernel(ids_ref, source_ref, gain_ref, cos_ref, sin_ref, table_hbm, wq_hbm, wkv_hbm,
-                 emb_ref, q_ref, pair_ref,
-                 table, wq, wkv, all_ids, found, recv, all_ref, load_sem, ks, kr, xs, xr, gs, gr):
-    z, x = here()
-    t = lax.axis_index("tensor")
-    loads = [
-        pltpu.make_async_copy(src, dst, load_sem.at[n])
-        for n, (src, dst) in enumerate(((table_hbm, table), (wq_hbm, wq), (wkv_hbm, wkv)))
-    ]
-    for load in loads:
-        load.start()
-    peers = [lax.rem(t + n, GROUP) for n in range(1, GROUP)]
-    sources = [lax.rem(t + GROUP - n, GROUP) for n in range(1, GROUP)]
-    greet([{"tensor": p} for p in peers])
+def find_rows(ids_ref, all_ids, wanted_by, table, found, recv, emb_ref, t, peers, sources, load, ks, kr, xs, xr, meanwhile):
     copies = []
+    rows, width = emb_ref.shape
+    wanted_by[...] = jnp.full_like(wanted_by, -1)
+    wanted_by[:, :rows] = jnp.broadcast_to(ids_ref[...], (8, rows))
     for n, p in enumerate(peers):
-        copy = remote(ids_ref, all_ids.at[t], ks.at[n], kr.at[n], {"tensor": p})
+        copy = remote(wanted_by, all_ids.at[t], ks.at[n], kr.at[n], {"tensor": p})
         copy.start()
         copies.append(copy)
-    all_ids[t] = ids_ref[...]
+    all_ids[t] = wanted_by[...]
+    slots = GROUP * SLOTS
+    owned = table.shape[0]
+    square = (128, 128)
+    row, lane = lax.broadcasted_iota(jnp.int32, square, 0), lax.broadcasted_iota(jnp.int32, square, 1)
+    own = jnp.broadcast_to(wanted_by[:1, :], square)
+    owner = jnp.right_shift(own, owned.bit_length() - 1).astype(F32)
+    same = (owner == owner.T) & (row < lane)
+    source = owner * SLOTS + jnp.sum(jnp.where(same, 1.0, 0.0), axis=0, keepdims=True)
+    chosen = jnp.where((source == row.astype(F32)) & (own >= 0), 1.0, 0.0).T[:rows].astype(BF16)
+    before = jnp.where(row < lane, 1.0, 0.0).astype(BF16)
     for n, p in enumerate(sources):
-        remote(ids_ref, all_ids.at[p], ks.at[n], kr.at[n], {"tensor": p}).wait_recv()
-    slots = GROUP * SLOTS
-    owned, width = table.shape
-    ids = all_ids[...].reshape(slots, 128)
-    local_rows = ids - t * owned
+        remote(wanted_by, all_ids.at[p], ks.at[n], kr.at[n], {"tensor": p}).wait_recv()
+    local_rows = all_ids[...].reshape(slots, 128) - t * owned
     inside = (local_rows >= 0) & (local_rows < owned)
-    square = (128, 128)
-    earlier = lax.broadcasted_iota(jnp.int32, square, 0) < lax.broadcasted_iota(jnp.int32, square, 1)
-    rank = jnp.dot(
-        jnp.where(inside, 1.0, 0.0).astype(BF16), jnp.where(earlier, 1.0, 0.0).astype(BF16),
-        preferred_element_type=F32,
-    )
-    slot = lax.rem(lax.broadcasted_iota(jnp.int32, (slots, 128), 0), SLOTS).astype(F32)
+    rank = jnp.dot(jnp.where(inside, 1.0, 0.0).astype(BF16), before, preferred_element_type=F32)
+    slot = lax.rem(row, SLOTS).astype(F32)
     wanted = jnp.sum(
         jnp.where(inside & (rank == slot), local_rows.astype(F32), 0.0), axis=1, keepdims=True
     )
     pick = lax.broadcasted_iota(jnp.int32, (slots, owned), 1).astype(F32) == wanted
     pick = jnp.where(pick, 1.0, 0.0).astype(BF16)
-    loads[0].wait()
+    load.wait()
     parts = 2
     step = width // parts
     for c in range(parts):
         def fetch(b, carry):
             cols = pl.ds(pl.multiple_of(c * step + b * 512, 512), 512)
-            rows = jnp.dot(pick, table[:, cols], preferred_element_type=F32).astype(BF16)
-            found[:, :, cols] = rows.reshape(GROUP, SLOTS, 512)
+            out = jnp.dot(pick, table[:, cols], preferred_element_type=F32).astype(BF16)
+            found[:, :, cols] = out.reshape(GROUP, SLOTS, 512)
             return carry
 
         lax.fori_loop(0, step // 512, fetch, 0)
@@ -353,9 +318,7 @@
             copy.start()
             copies.append(copy)
         recv[t, :, cols] = found[t, :, cols]
-    rows = emb_ref.shape[0]
-    lanes = lax.broadcasted_iota(jnp.int32, (rows, slots), 1)
-    chosen = jnp.where(source_ref[...] == lanes, 1.0, 0.0).astype(BF16)
+    meanwhile()
     total = jnp.zeros((rows, 1), F32)
     for c in range(parts):
         cols = pl.ds(c * step, step)
@@ -367,58 +330,16 @@
             picked = jnp.dot(chosen, recv[:, :, cols].reshape(slots, 1024), preferred_element_type=F32)
             emb_ref[:, cols] = picked.astype(BF16)
             total += jnp.sum(picked * picked, axis=-1, keepdims=True)
-    scale = lax.rsqrt(total / width + EPSILON)
-    for b in range(width // 1024):
-        cols = pl.ds(b * 1024, 1024)
-        all_ref[t, :, cols] = (emb_ref[:, cols].astype(F32) * scale * gain_ref[:, cols]).astype(BF16)
-    loads[1].wait()
-    loads[2].wait()
-    keys_here = lax.rem(t, 2) == 0
-
-    def project(dz):
-        lhs, span = row_group(all_ref, z, dz)
-        cos, sin = cos_ref[span, :], sin_ref[span, :]
-        queries = jnp.dot(lhs, wq[...], preferred_element_type=F32)
-        for h in range(queries.shape[1] // HD):
-            head = queries[:, h * HD:(h + 1) * HD]
-            q_ref[span, h * HD:(h + 1) * HD] = (head * cos + pltpu.roll(head, HD // 2, 1) * sin).astype(BF16)
-        pair = jnp.dot(lhs, wkv[...], preferred_element_type=F32)
-        turned = pair * cos + pltpu.roll(pair, HD // 2, 1) * sin
-        pair_ref[span, :] = jnp.where(keys_here, turned, pair).astype(BF16)
-
-    ring_gather(all_ref, gs, gr, z, x, project)
-    for copy in copies:
-        copy.wait_send()
-
-
-def front(ids, source, gain, cos, sin, table, wq, wkv):
-    rows, width = ids.shape[0], table.shape[1]
-    span = rows * GROUP
-    padded = jnp.broadcast_to(jnp.pad(ids, (0, 128 - rows), constant_values=-1)[None, :], (8, 128))
-    whole = pl.BlockSpec(memory_space=VMEM)
-    outside = pl.BlockSpec(memory_space=pl.ANY)
-    return pl.pallas_call(
-        front_kernel,
-        out_shape=(
-            jax.ShapeDtypeStruct((rows, width), BF16),
-            jax.ShapeDtypeStruct((span, wq.shape[1]), BF16),
-            jax.ShapeDtypeStruct((span, wkv.shape[1]), BF16),
-        ),
-        in_specs=[whole] * 5 + [outside] * 3,
-        out_specs=(whole,) * 3,
-        scratch_shapes=[
-            VMEM(table.shape, BF16), VMEM(wq.shape, BF16), VMEM(wkv.shape, BF16),
-            VMEM((GROUP, 8, 128), jnp.int32),
-            VMEM((GROUP, SLOTS, width), BF16), VMEM((GROUP, SLOTS, width), BF16),
-            VMEM((GROUP, rows, width), BF16),
-            DMA((3,)), DMA((GROUP - 1,)), DMA((GROUP - 1,)), DMA((2, GROUP - 1)), DMA((2, GROUP - 1)),
-            *GATHER_SEMS,
-        ],
-        compiler_params=pltpu.CompilerParams(
-            collective_id=0, has_side_effects=True, vmem_limit_bytes=48 * 2**20
-        ),
-        name="front",
-    )(padded, source, gain, cos, sin, table, wq, wkv)
+    return copies, total
+
+
+def document_starts(lengths_ref, positions):
+    first = jnp.zeros_like(positions)
+    start = jnp.int32(0)
+    for d in range(lengths_ref.shape[0]):
+        first = jnp.where(positions >= start, start, first)
+        start = start + lengths_ref[d]
+    return first
 
 
 QB = 256
@@ -617,89 +538,147 @@
     swap.wait_send()
 
 
-def back_kernel(pair_ref, q_ref, first_ref, emb_ref, gain_ref, wo_hbm, wg_hbm, wu_hbm, wd_hbm, out_ref,
-                wo, wg, wu, wd, win, relay, m_ref, l_ref, acc_ref, att, stream, all_ref, hid, load_sem, as_, ar,
-                part, r1, r2, held, s1, e1, s2, e2, part_b, r1b, r2b, held_b, s1b, e1b, s2b, e2b, gs, gr):
+def layer_kernel(ids_ref, lengths_ref, inverse_ref, attn_gain_ref, mlp_gain_ref,
+                 table_hbm, wq_hbm, wkv_hbm, wo_hbm, wg_hbm, wu_hbm, wd_hbm, out_ref,
+                 table, wq, wkv, wo, wg, wu, wd, load_sem,
+                 wanted_by, all_ids, found, recv, ks, kr, xs, xr,
+                 emb, all_ref, q, pair, cos_ref, sin_ref, first_ref, gs, gr,
+                 win, relay, m_ref, l_ref, acc_ref, att, as_, ar,
+                 stream, hid, gs2, gr2,
+                 part, r1, r2, held, s1, e1, s2, e2, s1b, e1b, s2b, e2b):
     z, x = here()
     t = lax.axis_index("tensor")
     r = lax.axis_index("dp")
     y, c = r // 2, lax.rem(r, 2)
     loads = [
         pltpu.make_async_copy(src, dst, load_sem.at[n])
-        for n, (src, dst) in enumerate(((wo_hbm, wo), (wg_hbm, wg), (wu_hbm, wu), (wd_hbm, wd)))
+        for n, (src, dst) in enumerate((
+            (table_hbm, table), (wq_hbm, wq), (wkv_hbm, wkv), (wo_hbm, wo), (wg_hbm, wg), (wu_hbm, wu), (wd_hbm, wd)
+        ))
     ]
     for load in loads:
         load.start()
-    greet(torus_peers(z, x) + [
+    peers = [lax.rem(t + n, GROUP) for n in range(1, GROUP)]
+    sources = [lax.rem(t + GROUP - n, GROUP) for n in range(1, GROUP)]
+    greet([{"tensor": p} for p in peers] + [
         {"dp": lax.rem(y + 1, SIDE) * 2 + c}, {"dp": lax.rem(y + SIDE - 1, SIDE) * 2 + c}, {"dp": y * 2 + 1 - c},
     ])
-    attention(q_ref, first_ref, pair_ref, att, win, relay, m_ref, l_ref, acc_ref, as_, ar)
-
-    def mixed(cols, value):
-        stream[:, cols] = (emb_ref[:, cols].astype(F32) + value).astype(BF16)
-
-    loads[0].wait()
-    ring_reduce(part, r1, r2, held, s1, e1, s2, e2, z, x, products(att, wo, part, z, x), mixed)
-    all_ref[t] = normalize(stream[...].astype(F32), gain_ref[...])
+    rows, width = emb.shape
+    span_rows = rows * GROUP
+
+    def positions():
+        lanes = r * span_rows + lax.broadcasted_iota(jnp.int32, (1, span_rows), 1)
+        first_ref[...] = document_starts(lengths_ref, lanes) - (r - 4) * span_rows
+        sign = jnp.where(lax.broadcasted_iota(jnp.int32, (1, HD), 1) < HD // 2, -1.0, 1.0)
+
+        def turn(b, carry):
+            at = pl.ds(pl.multiple_of(b * 64, 64), 64)
+            place_of = r * span_rows + b * 64 + lax.broadcasted_iota(jnp.int32, (64, HD), 0)
+            angle = (place_of - document_starts(lengths_ref, place_of)).astype(F32) * inverse_ref[...]
+            cos_ref[at, :] = jnp.cos(angle)
+            sin_ref[at, :] = jnp.sin(angle) * sign
+            return carry
+
+        lax.fori_loop(0, span_rows // 64, turn, 0)
+
+    copies, total = find_rows(
+        ids_ref, all_ids, wanted_by, table, found, recv, emb, t, peers, sources, loads[0], ks, kr, xs, xr, positions
+    )
+    scale = lax.rsqrt(total / width + EPSILON)
+    for b in range(width // 1024):
+        cols = pl.ds(b * 1024, 1024)
+        all_ref[t, :, cols] = (emb[:, cols].astype(F32) * scale * attn_gain_ref[:, cols]).astype(BF16)
     loads[1].wait()
     loads[2].wait()
+    keys_here = lax.rem(t, 2) == 0
+
+    def project(dz):
+        lhs, span = row_group(all_ref, z, dz)
+        cos, sin = cos_ref[span, :], sin_ref[span, :]
+        queries = jnp.dot(lhs, wq[...], preferred_element_type=F32)
+        for h in range(queries.shape[1] // HD):
+            head = queries[:, h * HD:(h + 1) * HD]
+            q[span, h * HD:(h + 1) * HD] = (head * cos + pltpu.roll(head, HD // 2, 1) * sin).astype(BF16)
+        both = jnp.dot(lhs, wkv[...], preferred_element_type=F32)
+        turned = both * cos + pltpu.roll(both, HD // 2, 1) * sin
+        pair[span, :] = jnp.where(keys_here, turned, both).astype(BF16)
+
+    ring_gather(all_ref, gs, gr, z, x, project)
+    attention(q, first_ref, pair, att, win, relay, m_ref, l_ref, acc_ref, as_, ar)
+
+    def mixed(cols, value):
+        stream[:, cols] = (emb[:, cols].astype(F32) + value).astype(BF16)
+
+    loads[3].wait()
+    ring_reduce(part, r1, r2, held, s1, e1, s2, e2, z, x, products(att, wo, part, z, x), mixed)
+    all_ref[t] = normalize(stream[...].astype(F32), mlp_gain_ref[...])
+    loads[4].wait()
+    loads[5].wait()
 
     def gate(dz):
         lhs, span = row_group(all_ref, z, dz)
-        gated = jnp.dot(lhs, wg[...], preferred_element_type=F32)
-        upper = jnp.dot(lhs, wu[...], preferred_element_type=F32)
+        across = (((1,), (1,)), ((), ()))
+        gated = lax.dot_general(lhs, wg[...], across, preferred_element_type=F32)
+        upper = lax.dot_general(lhs, wu[...], across, preferred_element_type=F32)
         hid[span, :] = (gated / (1.0 + jnp.exp(-gated)) * upper).astype(BF16)
 
-    ring_gather(all_ref, gs, gr, z, x, gate)
+    ring_gather(all_ref, gs2, gr2, z, x, gate)
 
     def added(cols, value):
         out_ref[:, cols] = (stream[:, cols].astype(F32) + value).astype(BF16)
 
-    loads[3].wait()
-    ring_reduce(part_b, r1b, r2b, held_b, s1b, e1b, s2b, e2b, z, x, products(hid, wd, part_b, z, x), added)
-
-
-def back(pair, queries, first, embedded, gain, wo, w_gate, w_up, w_down):
-    rows, width = embedded.shape
+    loads[6].wait()
+    ring_reduce(part, r1, r2, held, s1b, e1b, s2b, e2b, z, x, products(hid, wd, part, z, x), added)
+    for copy in copies:
+        copy.wait_send()
+
+
+def layer(ids, lengths, inverse, attn_gain, mlp_gain, table, wq, wkv, wo, wg, wu, wd):
+    rows, width = ids.shape[1], table.shape[1]
     span = rows * GROUP
     blocks = span // QB
+    quarter = width // 4
     whole = pl.BlockSpec(memory_space=VMEM)
     outside = pl.BlockSpec(memory_space=pl.ANY)
+    peers = DMA((GROUP - 1,))
+    reduce_sems = [DMA((2, 6, SIDE)), DMA((2, 6, SIDE)), DMA((2, 6)), DMA((2, 6))]
     return pl.pallas_call(
-        back_kernel,
+        layer_kernel,
         out_shape=jax.ShapeDtypeStruct((rows, width), BF16),
-        in_specs=[whole] * 5 + [outside] * 4,
+        in_specs=[whole, pl.BlockSpec(memory_space=pltpu.SMEM)] + [whole] * 3 + [outside] * 7,
         out_specs=whole,
         scratch_shapes=[
-            VMEM(wo.shape, BF16), VMEM(w_gate.shape, BF16), VMEM(w_up.shape, BF16), VMEM(w_down.shape, BF16),
+            *[VMEM(w.shape, BF16) for w in (table, wq, wkv, wo, wg, wu, wd)], DMA((7,)),
+            VMEM((8, 128), jnp.int32), VMEM((GROUP, 8, 128), jnp.int32),
+            VMEM((GROUP, SLOTS, width), BF16), VMEM((GROUP, SLOTS, width), BF16),
+            peers, peers, DMA((2, GROUP - 1)), DMA((2, GROUP - 1)),
+            VMEM((rows, width), BF16), VMEM((GROUP, rows, width), BF16),
+            VMEM((span, wq.shape[1]), BF16), VMEM((span, HD), BF16),
+            VMEM((span, HD), F32), VMEM((span, HD), F32), VMEM((1, span), jnp.int32), *GATHER_SEMS,
             VMEM((5, 2, span, HD), BF16), VMEM((span, HD), BF16),
             VMEM((blocks, 1, 2 * QB), F32), VMEM((blocks, 1, 2 * QB), F32), VMEM((blocks, HD, 2 * QB), F32),
-            VMEM((span, 2 * HD), BF16), VMEM((rows, width), BF16),
-            VMEM((GROUP, rows, width), BF16), VMEM((span, w_gate.shape[1]), BF16),
-            DMA((4,)), DMA((12,)), DMA((12,)),
-            *reduce_scratch(rows, width), *reduce_scratch(rows, width), *GATHER_SEMS,
+            VMEM((span, 2 * HD), BF16), DMA((12,)), DMA((12,)),
+            VMEM((rows, width), BF16), VMEM((span, wg.shape[0]), BF16), *GATHER_SEMS,
+            VMEM((SIDE, SIDE, rows, width), BF16),
+            VMEM((2, 6, SIDE, rows, quarter), BF16),
+            VMEM((2, 6, rows, quarter), BF16),
+            VMEM((2, 3, 2, rows, quarter), BF16),
+            *reduce_sems, *reduce_sems,
         ],
         compiler_params=pltpu.CompilerParams(
-            collective_id=1, has_side_effects=True, vmem_limit_bytes=62 * 2**20
+            collective_id=0, has_side_effects=True, vmem_limit_bytes=63 * 2**20
         ),
-        name="back",
-    )(pair, queries, first, embedded, gain, wo, w_gate, w_up, w_down)
+        name="layer",
+    )(ids, lengths, inverse, attn_gain, mlp_gain, table, wq, wkv, wo, wg, wu, wd)
 
 
 def local(ids, doc_lengths, table, attn_gain, wq, wkv, wo, mlp_gain, w_gate, w_up, w_down):
-    r = lax.axis_index("dp")
-    own_rows = ids.shape[0]
-    tok_range = own_rows * GROUP
-    owner = ids // table.shape[0]
-    earlier = jnp.arange(own_rows)[:, None] < jnp.arange(own_rows)[None, :]
-    own_rank = jnp.sum(jnp.where((owner[:, None] == owner[None, :]) & earlier, 1, 0), axis=0)
-    source = (owner * SLOTS + own_rank)[:, None]
-    positions = r * tok_range + jnp.arange(tok_range, dtype=jnp.int32)
-    first_pos, offsets = document_info(positions, doc_lengths)
-    cos, sin = turns(offsets)
-    embedded, queries, pair = front(ids, source, attn_gain[None, :], cos, sin, table, wq, wkv)
-    first = (first_pos - (r - 4) * tok_range)[None, :]
-    return back(pair, queries, first, embedded, mlp_gain[None, :], wo, w_gate, w_up, w_down)
+    inverse = ROPE_BASE ** (-jnp.arange(HD // 2, dtype=jnp.float32) * 2.0 / HD)
+    inverse = jnp.concatenate([inverse, inverse])[None, :]
+    return layer(
+        ids[None, :], doc_lengths, inverse, attn_gain[None, :], mlp_gain[None, :],
+        table, wq, wkv, wo, w_gate.T, w_up.T, w_down,
+    )
 
 
 def solution(mesh):

time: 220 us -> 195 us (0.89)
  local copies, waits for them, and re-layouts: 19.8 us -> 1.77 us
  Pallas kernels: 195 us -> 191 us
  other arithmetic: 4.21 us -> 0.6 us
    unnamed x15 -> x1, local copies, waits for them, and re-layouts: 17.6 us -> 1.77 us
    pallas_call x2 -> x1, Pallas kernels: 195 us -> 191 us  [layer(): pl.pallas_call(layer_kernel, out_shape=jax.ShapeDtypeStruct((rows, width)...]
where the time goes in v3:
time: 195 us; the launch traced here: 193 us
  Pallas kernels  191 us (98%)
    pallas_call x1, Pallas kernels, layer(): pl.pallas_call(layer_kernel, out_shape=jax.ShapeDtypeStruct((rows, width)...  191 us

profile of v3, /device:TPU:16, one launch (start us, length us, event | category | flops | bytes accessed | tf_op | source)
XLA Modules:
  0.0 192.9 jit_solution(5433446724933570588)
XLA Ops:
  0.0 0.6 maximum_bitcast_fusion.inverse_ref
  0.6 190.6 %layer.1 = bf16[48,4096]{1,0:T(8,128)(2,1)} custom-call(s32[1,48]{1,0:T(1,128)} %bitcast.11, s32[16]{0:T(128)} %lengths_ref.1, f32[1,128]{1,0:T(1,128)} %maximum_bitcast_fusion.inverse_ref, f32[1,4096]{1,0:T(1,128)} %bitcast.9, f32[1,4096]{1,0:T(1,128)} %bitcast.10, bf16[1024,4096]{1,0:T(8,128)(2,1)} %table_hbm.1, bf16[4096,256]{1,0:T(8,128)(2,1)} %wq_hbm.1, ...), custom_call_target="tpu_custom_call" | custom-call | tf_op jit(solution)/shard_map/layer/pallas_call | solution.py:645
  191.2 1.8 copy.13
  (1 shorter events, 0.0 us)

commit v4 on v3

v4 whole, which is shorter than its diff:
```python
import jax
import jax.numpy as jnp
from jax import lax
from jax.experimental import pallas as pl
from jax.experimental.pallas import tpu as pltpu
from jax.sharding import PartitionSpec as P

HD = 128
SIDE = 4
GROUP = SIDE * SIDE
SLOTS = 8

EPSILON = 1e-05
ROPE_BASE = 500000.0
NEGATIVE = -1e30
EXP_SCALE = HD ** (-0.5) * 1.4426950408889634
MESH = pl.DeviceIdType.MESH
VMEM = pltpu.VMEM
DMA = pltpu.SemaphoreType.DMA
BF16 = jnp.bfloat16
F32 = jnp.float32


def wrap(v):
    return lax.rem(v + 2 * SIDE, SIDE)


def place(z, x):
    return wrap(z) * SIDE + wrap(x)


def here():
    t = lax.axis_index("tensor")
    return t // SIDE, lax.rem(t, SIDE)


def greet(peers):
    barrier = pltpu.get_barrier_semaphore()
    for peer in peers:
        pl.semaphore_signal(barrier, inc=1, device_id=peer, device_id_type=MESH)
    pl.semaphore_wait(barrier, len(peers))


def remote(src, dst, send_sem, recv_sem, peer):
    return pltpu.make_async_remote_copy(
        src_ref=src, dst_ref=dst, send_sem=send_sem, recv_sem=recv_sem,
        device_id=peer, device_id_type=MESH,
    )


def weave(*streams):
    pending = [[next(g), n, g] for n, g in enumerate(streams)]
    while pending:
        pending.sort(key=lambda entry: entry[:2])
        entry = pending[0]
        entry[0] = next(entry[2], None)
        if entry[0] is None:
            pending.pop(0)


def ring_gather(buf, span, ssem, rsem, z, x, base):
    half = buf.shape[-1] // 2
    quarter = half // 2
    started = []

    def block(h, first, second):
        return place(z + second, x + first) if h == 0 else place(z + first, x + second)

    def view(h, first, second, part):
        start, size = (h * half, half) if part == 0 else (h * half + (part - 1) * quarter, quarter)
        return buf.at[block(h, first, second), span, pl.ds(start, size)]

    def send(h, n, first, second, part, axis, d):
        ref = view(h, first, second, part)
        peer = {"tensor": block(h, d, 0) if axis == 0 else block(h, 0, d)}
        copy = remote(ref, ref, ssem.at[h, n], rsem.at[h, n], peer)
        copy.start()
        started.append(copy)

    def recv(h, n, first, second, part):
        ref = view(h, first, second, part)
        remote(ref, ref, ssem.at[h, n], rsem.at[h, n], {"tensor": block(h, 1, 0)}).wait_recv()

    offsets = (0, -1, 1, 2)

    def relay(n):
        k = offsets[n]
        for h in range(2):
            recv(h, 4 + 2 * n, k, -1, 0)
            send(h, 12 + 2 * n, k, -1, 1, 1, 1)
            recv(h, 5 + 2 * n, k, 1, 0)
            send(h, 13 + 2 * n, k, 1, 2, 1, -1)

    times = [base + v for v in GATHER_TIMES]
    yield times[0]
    for h in range(2):
        send(h, 0, 0, 0, 0, 0, 1)
        send(h, 1, 0, 0, 0, 0, -1)
    for h in range(2):
        send(h, 4, 0, 0, 0, 1, 1)
        send(h, 5, 0, 0, 0, 1, -1)
    yield times[1]
    for h in range(2):
        recv(h, 0, -1, 0, 0)
        send(h, 2, -1, 0, 1, 0, 1)
        recv(h, 1, 1, 0, 0)
        send(h, 3, 1, 0, 2, 0, -1)
        for n in (1, 2):
            send(h, 4 + 2 * n, offsets[n], 0, 0, 1, 1)
            send(h, 5 + 2 * n, offsets[n], 0, 0, 1, -1)
    yield times[2]
    relay(0)
    yield times[3]
    for h in range(2):
        recv(h, 2, 2, 0, 1)
        recv(h, 3, 2, 0, 2)
        send(h, 10, 2, 0, 0, 1, 1)
        send(h, 11, 2, 0, 0, 1, -1)
    for n in (1, 2, 3):
        yield times[3 + n]
        relay(n)
    yield times[7]
    for n in range(4):
        for h in range(2):
            recv(h, 12 + 2 * n, offsets[n], 2, 1)
            recv(h, 13 + 2 * n, offsets[n], 2, 2)
    for copy in started:
        copy.wait_send()


GATHER_TIMES = (0, 4, 5.5, 7, 9, 11, 14, 18)
REDUCE_TIMES = (5, 10, 13, 16)


def ring_reduce(part, span, r1, r2, held, s1, e1, s2, e2, z, x, base, finish):
    half = part.shape[-1] // 2
    quarter = half // 2
    started = []

    def columns(h, q):
        return pl.ds(h * half + q * quarter, quarter)

    def bundle(h, k, q):
        if h == 0:
            return part.at[wrap(z + k), :, span, columns(h, q)]
        return part.at[:, wrap(x + k), span, columns(h, q)]

    def mine(h, j, q):
        if h == 0:
            return part.at[z, wrap(x + j), span, columns(h, q)]
        return part.at[wrap(z + j), x, span, columns(h, q)]

    def other(h, j):
        return wrap(x + j) if h == 0 else wrap(z + j)

    def peer(h, axis, d):
        along_z = (h == 0) == (axis == 0)
        return {"tensor": place(z + d, x) if along_z else place(z, x + d)}

    def send1(h, slot, src, d):
        copy = remote(src, r1.at[h, slot], s1.at[h, slot], e1.at[h, slot], peer(h, 0, d))
        copy.start()
        started.append(copy)

    def recv1(h, slot):
        ref = r1.at[h, slot]
        remote(ref, ref, s1.at[h, slot], e1.at[h, slot], peer(h, 0, 1)).wait_recv()

    def send2(h, slot, src, d):
        copy = remote(src, r2.at[h, slot], s2.at[h, slot], e2.at[h, slot], peer(h, 1, d))
        copy.start()
        started.append(copy)

    def recv2(h, slot):
        ref = r2.at[h, slot]
        remote(ref, ref, s2.at[h, slot], e2.at[h, slot], peer(h, 0, 1)).wait_recv()

    def load(ref):
        return ref[...].astype(F32)

    def summed(h, j, q):
        a, b = ((2, 4), (1, 5))[q]
        n = other(h, j)
        return load(mine(h, j, q)) + load(r1.at[h, a, n]) + load(r1.at[h, b, n])

    times = [base + v for v in REDUCE_TIMES]
    for h in range(2):
        send1(h, 0, bundle(h, 2, 0), 1)
        send1(h, 3, bundle(h, 2, 1), -1)
    for h in range(2):
        send1(h, 1, bundle(h, 1, 1), 1)
        send1(h, 4, bundle(h, -1, 0), -1)
    yield times[0]
    for h in range(2):
        for slot, k, q, d in ((0, 1, 0, 1), (3, -1, 1, -1)):
            recv1(h, slot)
            r1[h, slot] = (load(r1.at[h, slot]) + load(bundle(h, k, q))).astype(BF16)
            send1(h, slot + 2, r1.at[h, slot], d)
    yield times[1]
    for h in range(2):
        for slot in (1, 4, 2, 5):
            recv1(h, slot)
        for place_, j, q, slot, d in ((0, 2, 0, 0, 1), (0, 2, 1, 3, -1), (1, 1, 1, 1, 1), (2, -1, 0, 4, -1)):
            held[h, place_, q] = summed(h, j, q).astype(BF16)
            send2(h, slot, held.at[h, place_, q], d)
    yield times[2]
    for h in range(2):
        for place_, j, q, slot, d in ((1, 1, 0, 0, 1), (2, -1, 1, 3, -1)):
            recv2(h, slot)
            held[h, place_, q] = (summed(h, j, q) + load(r2.at[h, slot])).astype(BF16)
            send2(h, slot + 2, held.at[h, place_, q], d)
    yield times[3]
    for h in range(2):
        for slot in (1, 4, 2, 5):
            recv2(h, slot)
        for q in range(2):
            a, b = ((2, 4), (1, 5))[q]
            finish(columns(h, q), summed(h, 0, q) + load(r2.at[h, a]) + load(r2.at[h, b]))
    for copy in started:
        copy.wait_send()


def product(lhs, w_ref, part, span):
    rows = lhs.shape[0] // GROUP

    def column(c, carry):
        cols = pl.ds(pl.multiple_of(c * 512, 512), 512)
        out = jnp.dot(lhs, w_ref[:, cols], preferred_element_type=F32).astype(BF16)
        part[:, :, span, cols] = out.reshape(SIDE, SIDE, rows, 512)
        return carry

    lax.fori_loop(0, part.shape[-1] // 512, column, 0)


def normalize(rows, gain):
    scale = lax.rsqrt(jnp.mean(rows * rows, axis=-1, keepdims=True) + EPSILON)
    return (rows * scale * gain).astype(BF16)


def find_rows(ids_ref, all_ids, wanted_by, table, found, recv, emb_ref, t, peers, sources, load, ks, kr, xs, xr, meanwhile):
    copies = []
    rows, width = emb_ref.shape
    wanted_by[...] = jnp.full_like(wanted_by, -1)
    wanted_by[:, :rows] = jnp.broadcast_to(ids_ref[...], (8, rows))
    for n, p in enumerate(peers):
        copy = remote(wanted_by, all_ids.at[t], ks.at[n], kr.at[n], {"tensor": p})
        copy.start()
        copies.append(copy)
    all_ids[t] = wanted_by[...]
    slots = GROUP * SLOTS
    owned = table.shape[0]
    square = (128, 128)
    row, lane = lax.broadcasted_iota(jnp.int32, square, 0), lax.broadcasted_iota(jnp.int32, square, 1)
    own = jnp.broadcast_to(wanted_by[:1, :], square)
    owner = jnp.right_shift(own, owned.bit_length() - 1).astype(F32)
    same = (owner == owner.T) & (row < lane)
    source = owner * SLOTS + jnp.sum(jnp.where(same, 1.0, 0.0), axis=0, keepdims=True)
    chosen = jnp.where((source == row.astype(F32)) & (own >= 0), 1.0, 0.0).T[:rows].astype(BF16)
    before = jnp.where(row < lane, 1.0, 0.0).astype(BF16)
    for n, p in enumerate(sources):
        remote(wanted_by, all_ids.at[p], ks.at[n], kr.at[n], {"tensor": p}).wait_recv()
    local_rows = all_ids[...].reshape(slots, 128) - t * owned
    inside = (local_rows >= 0) & (local_rows < owned)
    rank = jnp.dot(jnp.where(inside, 1.0, 0.0).astype(BF16), before, preferred_element_type=F32)
    slot = lax.rem(row, SLOTS).astype(F32)
    wanted = jnp.sum(
        jnp.where(inside & (rank == slot), local_rows.astype(F32), 0.0), axis=1, keepdims=True
    )
    pick = lax.broadcasted_iota(jnp.int32, (slots, owned), 1).astype(F32) == wanted
    pick = jnp.where(pick, 1.0, 0.0).astype(BF16)
    load.wait()
    parts = 2
    step = width // parts
    for c in range(parts):
        def fetch(b, carry):
            cols = pl.ds(pl.multiple_of(c * step + b * 512, 512), 512)
            out = jnp.dot(pick, table[:, cols], preferred_element_type=F32).astype(BF16)
            found[:, :, cols] = out.reshape(GROUP, SLOTS, 512)
            return carry

        lax.fori_loop(0, step // 512, fetch, 0)
        cols = pl.ds(c * step, step)
        for n, p in enumerate(peers):
            copy = remote(found.at[p, :, cols], recv.at[t, :, cols], xs.at[c, n], xr.at[c, n], {"tensor": p})
            copy.start()
            copies.append(copy)
        recv[t, :, cols] = found[t, :, cols]
    meanwhile()
    total = jnp.zeros((rows, 1), F32)
    for c in range(parts):
        cols = pl.ds(c * step, step)
        for n, p in enumerate(sources):
            ref = recv.at[p, :, cols]
            remote(ref, ref, xs.at[c, n], xr.at[c, n], {"tensor": p}).wait_recv()
        for b in range(step // 1024):
            cols = pl.ds(c * step + b * 1024, 1024)
            picked = jnp.dot(chosen, recv[:, :, cols].reshape(slots, 1024), preferred_element_type=F32)
            emb_ref[:, cols] = picked.astype(BF16)
            total += jnp.sum(picked * picked, axis=-1, keepdims=True)
    return copies, total


def document_starts(lengths_ref, positions):
    first = jnp.zeros_like(positions)
    start = jnp.int32(0)
    for d in range(lengths_ref.shape[0]):
        first = jnp.where(positions >= start, start, first)
        start = start + lengths_ref[d]
    return first


QB = 256
CHUNKS = 3


class Attention:
    def __init__(self, q, first, at, keys_at, att, win, relay, top, total, acc, ssem, rsem):
        self.refs = q, first, at, keys_at, att, win, top, total, acc
        t = lax.axis_index("tensor")
        self.r = r = lax.axis_index("dp")
        self.y, self.c = y, c = r // 2, lax.rem(r, 2)
        self.kind = kind = lax.rem(t, 2)
        partner = {"tensor": t + 1 - 2 * kind}
        up = {"dp": lax.rem(y + 1, SIDE) * 2 + c}
        down = {"dp": lax.rem(y + SIDE - 1, SIDE) * 2 + c}
        other = {"dp": y * 2 + 1 - c}

        def copies(chunk):
            def copy(n, src, dst, peer):
                return remote(src, dst, ssem.at[chunk, n], rsem.at[chunk, n], peer)

            def block(w, k):
                return win.at[w, k, chunk]

            own = block(4, kind)
            return {
                "swap": copy(0, own, own, partner),
                "swap_in": copy(0, own, block(4, 1 - kind), partner),
                "up": [copy(1 + k, block(4, k), block(2, k), up) for k in range(2)],
                "far_key": copy(3, block(2, 0), block(0, 0), up),
                "down_value": copy(4, block(4, 1), relay.at[chunk], down),
                "far_value": copy(5, relay.at[chunk], block(0, 1), down),
                "near": [copy(6 + k, block(4, k), block(3, k), other) for k in range(2)],
                "cross0": [copy(8 + k, block(2, k), block(1, k), other) for k in range(2)],
                "cross1": [copy(8 + k, block(2, k), block(3, k), other) for k in range(2)],
                "far1": [copy(10 + k, block(0, k), block(1, k), other) for k in range(2)],
            }

        self.copies = copies
        self.has_up, self.has_far = y < SIDE - 1, y < SIDE - 2
        self.got_up, self.got_far = y > 0, y > 1
        self.relays = (y == SIDE - 1) | (y == 0)

    def exchange(self, chunk, base):
        c = self.c
        d = self.copies(chunk)

        def when(condition, *acts):
            @pl.when(condition)
            def _():
                for act in acts:
                    act()

        def starts(name):
            return [copy.start for copy in d[name]]

        def recvs(name):
            return [copy.wait_recv for copy in d[name]]

        def sends(name):
            return [copy.wait_send for copy in d[name]]

        d["swap"].start()
        yield base + 3.5
        d["swap_in"].wait_recv()
        when(self.has_far, d["down_value"].start)
        when(self.has_up, *starts("up"))
        when(c == 0, *starts("near"))
        yield base + 8
        when(self.relays, d["down_value"].wait_recv, d["far_value"].start)
        when(self.got_up, d["up"][0].wait_recv)
        when(self.got_up & self.has_up, d["far_key"].start)
        when(self.got_up, d["up"][1].wait_recv)
        when(self.got_up & (c == 0), *starts("cross0"))
        when(self.got_up & (c == 1), *starts("cross1"))
        when(c == 1, *recvs("near"))
        yield base + 10
        when(self.got_up & (c == 0), *recvs("cross1"))
        yield base + 13
        when(self.got_far, d["far_key"].wait_recv, d["far_value"].wait_recv)
        when(self.got_far & (c == 1), *starts("far1"))
        when(self.got_up & (c == 1), *recvs("cross0"))
        yield base + 15
        when(self.got_far & (c == 0), *recvs("far1"))
        d["swap"].wait_send()
        when(c == 0, *sends("near"))
        when(self.got_up & (c == 0), *sends("cross0"))
        when(self.got_up & (c == 1), *sends("cross1"))
        when(self.got_far & (c == 1), *sends("far1"))
        when(self.has_far, d["down_value"].wait_send)
        when(self.has_up, *sends("up"))
        when(self.relays, d["far_value"].wait_send)
        when(self.got_up & self.has_up, d["far_key"].wait_send)

    def step(self, w, chunk, own):
        q, first_ref, at_ref, keys_at, att, win, m_ref, l_ref, acc_ref = self.refs
        rows = CHUNKS * QB
        span = pl.ds(chunk * QB, QB)
        queries = jnp.concatenate([q[span, :HD], q[span, HD:]], axis=0)
        first = first_ref[:, span]
        first = jnp.concatenate([first, first], axis=1)
        keys = win[w, 0].reshape(rows, HD)
        scores = lax.dot_general(keys, queries, (((1,), (1,)), ((), ())), preferred_element_type=F32)
        at = keys_at[...] + w * rows
        allowed = at >= first
        if own:
            query = at_ref[:, span]
            allowed &= at <= jnp.concatenate([query, query], axis=1)
        scores = jnp.where(allowed, scores, NEGATIVE)
        top = jnp.max(scores, axis=0, keepdims=True) * EXP_SCALE
        if not own:
            old = m_ref[chunk]
            top = jnp.maximum(old, top)
            decay = jnp.exp2(old - top)
        weights = jnp.exp2(scores * EXP_SCALE - top)
        total = jnp.sum(weights, axis=0, keepdims=True)
        added = lax.dot_general(
            win[w, 1].reshape(rows, HD), weights.astype(BF16), (((0,), (0,)), ((), ())), preferred_element_type=F32
        )
        l_ref[chunk] = total if own else l_ref[chunk] * decay + total
        acc_ref[chunk] = added if own else acc_ref[chunk] * decay + added
        m_ref[chunk] = top

    def earlier(self, w, chunk):
        @pl.when(self.r + w >= 4)
        def _():
            self.step(w, chunk, False)

    def finish(self, chunk):
        q, first_ref, at_ref, keys_at, att, win, m_ref, l_ref, acc_ref = self.refs
        span = pl.ds(chunk * QB, QB)
        out = acc_ref[chunk] / l_ref[chunk]
        att[span, :HD] = out[:, :QB].T.astype(BF16)
        att[span, HD:] = out[:, QB:].T.astype(BF16)


def layer_kernel(ids_ref, lengths_ref, inverse_ref, attn_gain_ref, mlp_gain_ref,
                 table_hbm, wq_hbm, wkv_hbm, wo_hbm, wg_hbm, wu_hbm, wd_hbm, out_ref,
                 table, wq, wkv, wo, wg, wu, wd, load_sem,
                 wanted_by, all_ids, found, recv, ks, kr, xs, xr,
                 emb, all_ref, q, cos_ref, sin_ref, first_ref, at_ref, keys_at, gs, gr,
                 win, relay, m_ref, l_ref, acc_ref, att, as_, ar,
                 stream, hid, gs2, gr2,
                 part, r1, r2, held, s1, e1, s2, e2, s1b, e1b, s2b, e2b):
    z, x = here()
    t = lax.axis_index("tensor")
    r = lax.axis_index("dp")
    y, c = r // 2, lax.rem(r, 2)
    loads = [
        pltpu.make_async_copy(src, dst, load_sem.at[n])
        for n, (src, dst) in enumerate((
            (table_hbm, table), (wq_hbm, wq), (wkv_hbm, wkv), (wo_hbm, wo), (wg_hbm, wg), (wu_hbm, wu), (wd_hbm, wd)
        ))
    ]
    for load in loads:
        load.start()
    peers = [lax.rem(t + n, GROUP) for n in range(1, GROUP)]
    sources = [lax.rem(t + GROUP - n, GROUP) for n in range(1, GROUP)]
    greet([{"tensor": p} for p in peers] + [
        {"dp": lax.rem(y + 1, SIDE) * 2 + c}, {"dp": lax.rem(y + SIDE - 1, SIDE) * 2 + c}, {"dp": y * 2 + 1 - c},
    ])
    rows, width = emb.shape
    span_rows = rows * GROUP
    each = rows // CHUNKS
    spans = [pl.ds(chunk * each, each) for chunk in range(CHUNKS)]

    def within(n):
        chunk = n // QB
        return (n - chunk * QB) // each * rows + chunk * each + lax.rem(n, each)

    def positions():
        lanes = within(lax.broadcasted_iota(jnp.int32, (1, span_rows), 1))
        first_ref[...] = document_starts(lengths_ref, r * span_rows + lanes) - (r - 4) * span_rows
        at_ref[...] = 4 * span_rows + lanes
        keys_at[...] = within(lax.broadcasted_iota(jnp.int32, (span_rows, 1), 0))
        sign = jnp.where(lax.broadcasted_iota(jnp.int32, (1, HD), 1) < HD // 2, -1.0, 1.0)

        def turn(b, carry):
            rows_of = pl.ds(pl.multiple_of(b * 64, 64), 64)
            place_of = r * span_rows + within(b * 64 + lax.broadcasted_iota(jnp.int32, (64, HD), 0))
            angle = (place_of - document_starts(lengths_ref, place_of)).astype(F32) * inverse_ref[...]
            cos_ref[rows_of, :] = jnp.cos(angle)
            sin_ref[rows_of, :] = jnp.sin(angle) * sign
            return carry

        lax.fori_loop(0, span_rows // 64, turn, 0)

    copies, total = find_rows(
        ids_ref, all_ids, wanted_by, table, found, recv, emb, t, peers, sources, loads[0], ks, kr, xs, xr, positions
    )
    scale = lax.rsqrt(total / width + EPSILON)
    for b in range(width // 1024):
        cols = pl.ds(b * 1024, 1024)
        all_ref[t, :, cols] = (emb[:, cols].astype(F32) * scale * attn_gain_ref[:, cols]).astype(BF16)
    loads[1].wait()
    loads[2].wait()
    keys_here = lax.rem(t, 2) == 0
    attention = Attention(q, first_ref, at_ref, keys_at, att, win, relay, m_ref, l_ref, acc_ref, as_, ar)

    def project(chunk):
        lhs = all_ref[:, spans[chunk], :].reshape(QB, width)
        span = pl.ds(chunk * QB, QB)
        cos, sin = cos_ref[span, :], sin_ref[span, :]
        queries = jnp.dot(lhs, wq[...], preferred_element_type=F32)
        for h in range(queries.shape[1] // HD):
            head = queries[:, h * HD:(h + 1) * HD]
            q[span, h * HD:(h + 1) * HD] = (head * cos + pltpu.roll(head, HD // 2, 1) * sin).astype(BF16)
        both = jnp.dot(lhs, wkv[...], preferred_element_type=F32)
        turned = both * cos + pltpu.roll(both, HD // 2, 1) * sin
        win[4, attention.kind, chunk] = jnp.where(keys_here, turned, both).astype(BF16)

    last = CHUNKS - 1
    exchanges = []

    def head(chunk):
        base = 9 * chunk
        yield from ring_gather(all_ref, spans[chunk], gs.at[chunk], gr.at[chunk], z, x, base)
        project(chunk)
        if chunk < last:
            yield from attention.exchange(chunk, base + 20)
        else:
            exchanges.append(attention.exchange(chunk, 0))
            next(exchanges[0])

    weave(*[head(chunk) for chunk in range(CHUNKS)])
    exchange = exchanges[0]
    next(exchange)
    for chunk in range(CHUNKS):
        attention.step(4, chunk, True)
    next(exchange)
    for chunk in range(CHUNKS):
        attention.earlier(2 + c, chunk)
    next(exchange)
    for chunk in range(CHUNKS):
        attention.earlier(3 - c, chunk)
    next(exchange)
    loads[3].wait()

    def tail(chunk):
        rows_of = spans[chunk]
        span = pl.ds(chunk * QB, QB)
        base = TAIL_TIMES[0] * chunk
        yield TAIL_TIMES[1] * chunk
        attention.earlier(c, chunk)
        if chunk == 0:
            for _ in exchange:
                pass
        attention.earlier(1 - c, chunk)
        attention.finish(chunk)
        product(att[span, :], wo, part, rows_of)

        def mixed(cols, value):
            stream[rows_of, cols] = (emb[rows_of, cols].astype(F32) + value).astype(BF16)

        buffers = r1.at[chunk], r2.at[chunk], held.at[chunk]
        sems = [s.at[chunk] for s in (s1, e1, s2, e2)]
        yield from ring_reduce(part, rows_of, *buffers, *sems, z, x, base, mixed)
        all_ref[t, rows_of] = normalize(stream[rows_of, :].astype(F32), mlp_gain_ref[...])
        base += REDUCE_TIMES[-1] + 1
        yield from ring_gather(all_ref, rows_of, gs2.at[chunk], gr2.at[chunk], z, x, base)
        if chunk == 0:
            for n in (4, 5, 6):
                loads[n].wait()
        lhs = all_ref[:, rows_of, :].reshape(QB, width)
        across = (((1,), (1,)), ((), ()))
        gated = lax.dot_general(lhs, wg[...], across, preferred_element_type=F32)
        upper = lax.dot_general(lhs, wu[...], across, preferred_element_type=F32)
        hid[...] = (gated / (1.0 + jnp.exp(-gated)) * upper).astype(BF16)
        base += GATHER_TIMES[-1] + 3
        yield base
        product(hid[...], wd, part, rows_of)

        def added(cols, value):
            out_ref[rows_of, cols] = (stream[rows_of, cols].astype(F32) + value).astype(BF16)

        sems = [s.at[chunk] for s in (s1b, e1b, s2b, e2b)]
        yield from ring_reduce(part, rows_of, *buffers, *sems, z, x, base + 3, added)

    weave(*[tail(chunk) for chunk in range(CHUNKS)])
    for copy in copies:
        copy.wait_send()


TAIL_TIMES = (9, 3)


def layer(ids, lengths, inverse, attn_gain, mlp_gain, table, wq, wkv, wo, wg, wu, wd):
    rows, width = ids.shape[1], table.shape[1]
    span = rows * GROUP
    each = rows // CHUNKS
    quarter = width // 4
    whole = pl.BlockSpec(memory_space=VMEM)
    outside = pl.BlockSpec(memory_space=pl.ANY)
    peers = DMA((GROUP - 1,))
    gather_sems = [DMA((CHUNKS, 2, 20))] * 2
    reduce_sems = [DMA((CHUNKS, 2, 6))] * 4
    return pl.pallas_call(
        layer_kernel,
        out_shape=jax.ShapeDtypeStruct((rows, width), BF16),
        in_specs=[whole, pl.BlockSpec(memory_space=pltpu.SMEM)] + [whole] * 3 + [outside] * 7,
        out_specs=whole,
        scratch_shapes=[
            *[VMEM(w.shape, BF16) for w in (table, wq, wkv, wo, wg, wu, wd)], DMA((7,)),
            VMEM((8, 128), jnp.int32), VMEM((GROUP, 8, 128), jnp.int32),
            VMEM((GROUP, SLOTS, width), BF16), VMEM((GROUP, SLOTS, width), BF16),
            peers, peers, DMA((2, GROUP - 1)), DMA((2, GROUP - 1)),
            VMEM((rows, width), BF16), VMEM((GROUP, rows, width), BF16),
            VMEM((span, wq.shape[1]), BF16),
            VMEM((span, HD), F32), VMEM((span, HD), F32),
            VMEM((1, span), jnp.int32), VMEM((1, span), jnp.int32), VMEM((span, 1), jnp.int32), *gather_sems,
            VMEM((5, 2, CHUNKS, QB, HD), BF16), VMEM((CHUNKS, QB, HD), BF16),
            VMEM((CHUNKS, 1, 2 * QB), F32), VMEM((CHUNKS, 1, 2 * QB), F32), VMEM((CHUNKS, HD, 2 * QB), F32),
            VMEM((span, 2 * HD), BF16), DMA((CHUNKS, 12)), DMA((CHUNKS, 12)),
            VMEM((rows, width), BF16), VMEM((QB, wg.shape[0]), BF16), *gather_sems,
            VMEM((SIDE, SIDE, rows, width), BF16),
            VMEM((CHUNKS, 2, 6, SIDE, each, quarter), BF16),
            VMEM((CHUNKS, 2, 6, each, quarter), BF16),
            VMEM((CHUNKS, 2, 3, 2, each, quarter), BF16),
            *reduce_sems, *reduce_sems,
        ],
        compiler_params=pltpu.CompilerParams(
            collective_id=0, has_side_effects=True, vmem_limit_bytes=63 * 2**20
        ),
        name="layer",
    )(ids, lengths, inverse, attn_gain, mlp_gain, table, wq, wkv, wo, wg, wu, wd)


def local(ids, doc_lengths, table, attn_gain, wq, wkv, wo, mlp_gain, w_gate, w_up, w_down):
    inverse = ROPE_BASE ** (-jnp.arange(HD // 2, dtype=jnp.float32) * 2.0 / HD)
    inverse = jnp.concatenate([inverse, inverse])[None, :]
    return layer(
        ids[None, :], doc_lengths, inverse, attn_gain[None, :], mlp_gain[None, :],
        table, wq, wkv, wo, w_gate.T, w_up.T, w_down,
    )


def solution(mesh):
    placed = (
        P(("dp", "tensor")),
        P(),
        P("tensor", None),
        P(),
        P(None, "tensor"),
        P(None, "tensor"),
        P("tensor", None),
        P(),
        P(None, "tensor"),
        P(None, "tensor"),
        P("tensor", None),
    )
    return jax.shard_map(
        local, mesh=mesh, in_specs=placed, out_specs=P(("dp", "tensor"), None), check_vma=False
    )
```

time: 195 us -> 209 us (1.072)
  Pallas kernels: 191 us -> 207 us
    pallas_call x1, Pallas kernels: 191 us -> 207 us  [layer(): pl.pallas_call(layer_kernel, out_shape=jax.ShapeDtypeStruct((rows, width)...]
where the time goes in v4:
time: 209 us
  Pallas kernels  207 us (99%)
    pallas_call x1, Pallas kernels, layer(): pl.pallas_call(layer_kernel, out_shape=jax.ShapeDtypeStruct((rows, width)...  207 us

profile of v4, /device:TPU:16, one launch (start us, length us, event | category | flops | bytes accessed | tf_op | source)
XLA Modules:
  0.0 208.9 jit_solution(1922859998766491846)
XLA Ops:
  0.0 0.6 maximum_bitcast_fusion.inverse_ref
  0.6 206.6 %layer.1 = bf16[48,4096]{1,0:T(8,128)(2,1)} custom-call(s32[1,48]{1,0:T(1,128)} %bitcast.11, s32[16]{0:T(128)} %lengths_ref.1, f32[1,128]{1,0:T(1,128)} %maximum_bitcast_fusion.inverse_ref, f32[1,4096]{1,0:T(1,128)} %bitcast.9, f32[1,4096]{1,0:T(1,128)} %bitcast.10, bf16[1024,4096]{1,0:T(8,128)(2,1)} %table_hbm.1, bf16[4096,256]{1,0:T(8,128)(2,1)} %wq_hbm.1, ...), custom_call_target="tpu_custom_call" | custom-call | tf_op jit(solution)/shard_map/layer/pallas_call | solution.py:607
  207.2 1.8 copy.13
  (1 shorter events, 0.0 us)

commit v5 on v3

--- a/solution.py
+++ b/solution.py
@@ -9,6 +9,8 @@
 SIDE = 4
 GROUP = SIDE * SIDE
 SLOTS = 8
+UNIT = 16
+UNITS = 3
 
 EPSILON = 1e-05
 ROPE_BASE = 500000.0
@@ -39,10 +41,6 @@
     for peer in peers:
         pl.semaphore_signal(barrier, inc=1, device_id=peer, device_id_type=MESH)
     pl.semaphore_wait(barrier, len(peers))
-
-
-def torus_peers(z, x):
-    return [{"tensor": place(z + a, x + b)} for a, b in ((0, 1), (0, -1), (1, 0), (-1, 0))]
 
 
 def remote(src, dst, send_sem, recv_sem, peer):
@@ -140,7 +138,7 @@
 
     def mine(h, k, j, q):
         a, b = at(h, k, j)
-        return part.at[a, b, :, pl.ds(h * half + q * quarter, quarter)]
+        return part.at[a, pl.ds(b * UNITS, UNITS), :, pl.ds(h * half + q * quarter, quarter)]
 
     def peer(h, axis, d):
         a, b = at(h, d, 0) if axis == 0 else at(h, 0, d)
@@ -225,13 +223,13 @@
         for q in range(2):
             a, b = ((2, 4), (1, 5))[q]
             value = summed(h, 0, q) + load(r2.at[h, a]) + load(r2.at[h, b])
-            finish(pl.ds(h * half + q * quarter, quarter), value)
+            finish(pl.ds(h * half + q * quarter, quarter), flat(value))
     for copy in started:
         copy.wait_send()
 
 
 def products(a_ref, w_ref, part, z, x):
-    rows, width = part.shape[2], part.shape[3]
+    rows, width = UNITS * UNIT, part.shape[3]
     half = width // 2
     step = min(512, half)
 
@@ -245,7 +243,8 @@
                 cols = pl.ds(pl.multiple_of(h * half + c * step, step), step)
                 out = jnp.dot(lhs, w_ref[:, cols], preferred_element_type=F32).astype(BF16)
                 for n, (a, b) in enumerate(blocks):
-                    part[a, b, :, cols] = out[n * rows:(n + 1) * rows]
+                    block = out[n * rows:(n + 1) * rows].reshape(UNITS, UNIT, step)
+                    part[a, pl.ds(b * UNITS, UNITS), :, cols] = block
                 return carry
 
             lax.fori_loop(0, half // step, column, 0)
@@ -256,6 +255,172 @@
             run([(a, wrap(x + k)) for a in range(SIDE)])
 
     return make
+
+
+def flat(block):
+    return block.reshape(-1, block.shape[-1])
+
+
+class Spread:
+    def __init__(self, wo_hbm, part, ssem, rsem, ysem, yrem, csem, crem, z, x):
+        r = lax.axis_index("dp")
+        self.y, self.c = r // 2, lax.rem(r, 2)
+        self.wo, self.part, self.z, self.x = wo_hbm, part, z, x
+        self.sems = (ssem, rsem), (ysem, yrem), (csem, crem)
+        self.half = part.shape[-1] // 2
+        self.started = []
+        self.slices = [(o, h) for h in range(2) for o in (1, 2, 3)]
+
+    def share(self, dy, other=False):
+        c = 1 - self.c if other else self.c
+        return lax.rem(self.y + dy + SIDE, SIDE) * 2 + c
+
+    def columns(self, h, q):
+        quarter = self.half // 2
+        return pl.ds(h * self.half, self.half) if q is None else pl.ds(h * self.half + q * quarter, quarter)
+
+    def view(self, o, share, h, q=None):
+        unit = 16 * (o - 1) + 2 * share
+        a = unit // 12
+        return self.part.at[a, pl.ds(unit - a * 12, 2), :, self.columns(h, q)]
+
+    def copy(self, phase, index, src, dst, peer, start):
+        send, recv = self.sems[phase]
+        copy = remote(src, dst, send.at[index], recv.at[index], peer)
+        if start:
+            copy.start()
+            self.started.append(copy)
+        else:
+            copy.wait_recv()
+
+    def along(self, h, d):
+        return {"tensor": place(self.z + d, self.x) if h == 0 else place(self.z, self.x + d)}
+
+    def plane(self, start):
+        own = self.share(0)
+        for h in range(2):
+            mine = self.wo.at[pl.ds(2 * own, 2), :, self.columns(h, None)]
+            for n, (o, d) in enumerate(((3, 1), (1, -1))):
+                dst = self.view(o, own, h)
+                self.copy(0, h * 4 + n, mine if start else dst, dst, self.along(h, d), start)
+
+    def plane_far(self, start):
+        own = self.share(0)
+        for h in range(2):
+            for n, (o, d) in enumerate(((3, 1), (1, -1))):
+                dst = self.view(2, own, h, n)
+                self.copy(0, h * 4 + 2 + n, self.view(o, own, h, n) if start else dst, dst, self.along(h, d), start)
+
+    def around(self, d):
+        return {"dp": lax.rem(self.y + d + SIDE, SIDE) * 2 + self.c}
+
+    def ring(self, start):
+        for n, (o, h) in enumerate(self.slices):
+            for k, d in enumerate((1, -1)):
+                ref = self.view(o, self.share(0 if start else -d), h)
+                self.copy(1, k * 9 + n, ref, ref, self.around(d), start)
+
+    def ring_far(self, start):
+        for n in range(3):
+            for k, d in enumerate((1, -1)):
+                o, h = self.slices[3 * k + n]
+                ref = self.view(o, self.share(-d if start else -2 * d), h)
+                self.copy(1, k * 9 + 6 + n, ref, ref, self.around(d), start)
+
+    def cores(self, start, steps):
+        peer = {"dp": self.y * 2 + 1 - self.c}
+        for dy in steps:
+            for n, (o, h) in enumerate(self.slices):
+                ref = self.view(o, self.share(dy, not start), h)
+                self.copy(2, dy * 6 + n, ref, ref, peer, start)
+
+    def drain(self):
+        for copy in self.started:
+            copy.wait_send()
+
+
+def short_reduce(att, att_z, att_x, wo, part, mine, got, ssem, rsem, bs, br, z, x, finish):
+    half = part.shape[-1] // 2
+    quarter = half // 2
+    started = []
+
+    def along(h, d):
+        return {"tensor": place(z + d, x) if h == 0 else place(z, x + d)}
+
+    def across(h, d):
+        return along(1 - h, d)
+
+    def rows_for(h, d):
+        return att.at[wrap(z + d)] if h == 0 else att.at[:, pl.ds(wrap(x + d) * UNITS, UNITS)]
+
+    def landing(h, o):
+        return (att_z, att_x)[h].at[o - 1]
+
+    def move(h, o):
+        return remote(rows_for(h, o), landing(h, SIDE - o), bs.at[h, o - 1], br.at[h, o - 1], along(h, o))
+
+    for h in range(2):
+        for o in (2, 1, 3):
+            copy = move(h, o)
+            copy.start()
+            started.append(copy)
+
+    def block(h, j, q):
+        n = wrap(x + j) if h == 0 else wrap(z + j)
+        return mine.at[h, pl.ds(n * UNITS, UNITS), :, pl.ds(q * quarter, quarter)]
+
+    def send(h, slot, src, d):
+        copy = remote(src, got.at[h, slot], ssem.at[h, slot], rsem.at[h, slot], across(h, d))
+        copy.start()
+        started.append(copy)
+
+    def recv(h, slot):
+        ref = got.at[h, slot]
+        remote(ref, ref, ssem.at[h, slot], rsem.at[h, slot], across(h, 1)).wait_recv()
+
+    def load(ref):
+        return ref[...].astype(F32)
+
+    step = min(512, quarter)
+
+    def make(h, q):
+        own = flat(rows_for(h, 0)[...])
+        others = jnp.concatenate([flat(landing(h, o)[...]) for o in (1, 2, 3)], axis=1)
+
+        def column(c, carry):
+            at = pl.multiple_of(q * quarter + c * step, step)
+            cols = pl.ds(h * half + at, step)
+            out = jnp.dot(own, flat(wo[:, :, cols]), preferred_element_type=F32)
+            weights = part[:, :, :, cols].reshape(3 * own.shape[1], step)
+            out = out + jnp.dot(others, weights, preferred_element_type=F32)
+            mine[h, :, :, pl.ds(at, step)] = out.astype(BF16).reshape(SIDE * UNITS, UNIT, step)
+            return carry
+
+        lax.fori_loop(0, quarter // step, column, 0)
+
+    for q in range(2):
+        for h in range(2):
+            if q == 0:
+                for o in (3, 1, 2):
+                    move(h, SIDE - o).wait_recv()
+            make(h, q)
+            d = 1 - 2 * q
+            send(h, 3 * q, block(h, 2, q), d)
+            send(h, (4, 1)[q], block(h, -d, q), -d)
+    for h in range(2):
+        for slot, q, d in ((0, 0, 1), (3, 1, -1)):
+            recv(h, slot)
+            got[h, slot] = (load(got.at[h, slot]) + load(block(h, d, q))).astype(BF16)
+            send(h, slot + 2, got.at[h, slot], d)
+    for h in range(2):
+        for slot in (1, 4, 2, 5):
+            recv(h, slot)
+        for q in range(2):
+            a, b = ((2, 4), (1, 5))[q]
+            value = load(block(h, 0, q)) + load(got.at[h, a]) + load(got.at[h, b])
+            finish(pl.ds(h * half + q * quarter, quarter), flat(value))
+    for copy in started:
+        copy.wait_send()
 
 
 def normalize(rows, gain):
@@ -493,10 +658,12 @@
 
     earlier(1 - c)
     for i in range(blocks):
-        span = pl.ds(i * QB, QB)
         out = acc_ref[i] / l_ref[i]
-        att_ref[span, :HD] = out[:, :QB].T.astype(BF16)
-        att_ref[span, HD:] = out[:, QB:].T.astype(BF16)
+        for h in range(2):
+            head = out[:, h * QB:(h + 1) * QB].T.astype(BF16)
+            for n in range(QB // UNIT):
+                unit = i * QB // UNIT + n
+                att_ref[unit // 12, unit % 12, :, h * HD:(h + 1) * HD] = head[n * UNIT:(n + 1) * UNIT]
 
     @pl.when(c == 0)
     def _():
@@ -545,7 +712,8 @@
                  emb, all_ref, q, pair, cos_ref, sin_ref, first_ref, gs, gr,
                  win, relay, m_ref, l_ref, acc_ref, att, as_, ar,
                  stream, hid, gs2, gr2,
-                 part, r1, r2, held, s1, e1, s2, e2, s1b, e1b, s2b, e2b):
+                 part, r1, r2, held, s1, e1, s2, e2,
+                 att_z, att_x, mine, got, ss, sr, bs, br, ps, pr, ys, yr, cs, cr):
     z, x = here()
     t = lax.axis_index("tensor")
     r = lax.axis_index("dp")
@@ -565,8 +733,12 @@
     ])
     rows, width = emb.shape
     span_rows = rows * GROUP
+    spread = Spread(wo_hbm, part, ps, pr, ys, yr, cs, cr, z, x)
+    spread.plane(True)
 
     def positions():
+        spread.plane(False)
+        spread.plane_far(True)
         lanes = r * span_rows + lax.broadcasted_iota(jnp.int32, (1, span_rows), 1)
         first_ref[...] = document_starts(lengths_ref, lanes) - (r - 4) * span_rows
         sign = jnp.where(lax.broadcasted_iota(jnp.int32, (1, HD), 1) < HD // 2, -1.0, 1.0)
@@ -591,8 +763,15 @@
     loads[1].wait()
     loads[2].wait()
     keys_here = lax.rem(t, 2) == 0
+    spread.plane_far(False)
+    spread.ring(True)
+    spread.cores(True, (0,))
 
     def project(dz):
+        if dz == 1:
+            spread.ring(False)
+            spread.ring_far(True)
+            spread.cores(True, (1, 3))
         lhs, span = row_group(all_ref, z, dz)
         cos, sin = cos_ref[span, :], sin_ref[span, :]
         queries = jnp.dot(lhs, wq[...], preferred_element_type=F32)
@@ -604,13 +783,18 @@
         pair[span, :] = jnp.where(keys_here, turned, both).astype(BF16)
 
     ring_gather(all_ref, gs, gr, z, x, project)
+    spread.ring_far(False)
+    spread.cores(True, (2,))
     attention(q, first_ref, pair, att, win, relay, m_ref, l_ref, acc_ref, as_, ar)
+    spread.cores(False, (0, 1, 3))
 
     def mixed(cols, value):
         stream[:, cols] = (emb[:, cols].astype(F32) + value).astype(BF16)
 
     loads[3].wait()
-    ring_reduce(part, r1, r2, held, s1, e1, s2, e2, z, x, products(att, wo, part, z, x), mixed)
+    spread.cores(False, (2,))
+    short_reduce(att, att_z, att_x, wo, part, mine, got, ss, sr, bs, br, z, x, mixed)
+    spread.drain()
     all_ref[t] = normalize(stream[...].astype(F32), mlp_gain_ref[...])
     loads[4].wait()
     loads[5].wait()
@@ -628,7 +812,7 @@
         out_ref[:, cols] = (stream[:, cols].astype(F32) + value).astype(BF16)
 
     loads[6].wait()
-    ring_reduce(part, r1, r2, held, s1b, e1b, s2b, e2b, z, x, products(hid, wd, part, z, x), added)
+    ring_reduce(part, r1, r2, held, s1, e1, s2, e2, z, x, products(hid, wd, part, z, x), added)
     for copy in copies:
         copy.wait_send()
 
@@ -638,6 +822,7 @@
     span = rows * GROUP
     blocks = span // QB
     quarter = width // 4
+    unit = (UNITS, UNIT)
     whole = pl.BlockSpec(memory_space=VMEM)
     outside = pl.BlockSpec(memory_space=pl.ANY)
     peers = DMA((GROUP - 1,))
@@ -657,13 +842,17 @@
             VMEM((span, HD), F32), VMEM((span, HD), F32), VMEM((1, span), jnp.int32), *GATHER_SEMS,
             VMEM((5, 2, span, HD), BF16), VMEM((span, HD), BF16),
             VMEM((blocks, 1, 2 * QB), F32), VMEM((blocks, 1, 2 * QB), F32), VMEM((blocks, HD, 2 * QB), F32),
-            VMEM((span, 2 * HD), BF16), DMA((12,)), DMA((12,)),
+            VMEM((SIDE, SIDE * UNITS, UNIT, 2 * HD), BF16), DMA((12,)), DMA((12,)),
             VMEM((rows, width), BF16), VMEM((span, wg.shape[0]), BF16), *GATHER_SEMS,
-            VMEM((SIDE, SIDE, rows, width), BF16),
-            VMEM((2, 6, SIDE, rows, quarter), BF16),
-            VMEM((2, 6, rows, quarter), BF16),
-            VMEM((2, 3, 2, rows, quarter), BF16),
-            *reduce_sems, *reduce_sems,
+            VMEM((SIDE, SIDE * UNITS, UNIT, width), BF16),
+            VMEM((2, 6, SIDE, *unit, quarter), BF16),
+            VMEM((2, 6, *unit, quarter), BF16),
+            VMEM((2, 3, 2, *unit, quarter), BF16),
+            *reduce_sems,
+            VMEM((SIDE - 1, SIDE * UNITS, UNIT, 2 * HD), BF16), VMEM((SIDE - 1, SIDE, *unit, 2 * HD), BF16),
+            VMEM((2, SIDE * UNITS, UNIT, 2 * quarter), BF16), VMEM((2, 6, *unit, quarter), BF16),
+            DMA((2, 6)), DMA((2, 6)), DMA((2, 3)), DMA((2, 3)),
+            DMA((8,)), DMA((8,)), DMA((18,)), DMA((18,)), DMA((24,)), DMA((24,)),
         ],
         compiler_params=pltpu.CompilerParams(
             collective_id=0, has_side_effects=True, vmem_limit_bytes=63 * 2**20
@@ -677,7 +866,7 @@
     inverse = jnp.concatenate([inverse, inverse])[None, :]
     return layer(
         ids[None, :], doc_lengths, inverse, attn_gain[None, :], mlp_gain[None, :],
-        table, wq, wkv, wo, w_gate.T, w_up.T, w_down,
+        table, wq, wkv, wo.reshape(-1, UNIT, wo.shape[1]), w_gate.T, w_up.T, w_down,
     )
 
 

time: 195 us -> 184 us (0.944); the launches traced: 193 us -> 184 us
  Pallas kernels: 191 us -> 182 us
    pallas_call x1, Pallas kernels: 191 us -> 182 us  [layer(): pl.pallas_call(layer_kernel, out_shape=jax.ShapeDtypeStruct((rows, width)...]
where the time goes in v5:
time: 184 us
  Pallas kernels  182 us (99%)
    pallas_call x1, Pallas kernels, layer(): pl.pallas_call(layer_kernel, out_shape=jax.ShapeDtypeStruct((rows, width)...  182 us

profile of v5, /device:TPU:16, one launch (start us, length us, event | category | flops | bytes accessed | tf_op | source)
XLA Modules:
  0.0 183.9 jit_solution(10576131773061229783)
XLA Ops:
  0.0 0.6 maximum_bitcast_fusion.inverse_ref
  0.6 181.5 %layer.1 = bf16[48,4096]{1,0:T(8,128)(2,1)} custom-call(s32[1,48]{1,0:T(1,128)} %bitcast.13, s32[16]{0:T(128)} %lengths_ref.1, f32[1,128]{1,0:T(1,128)} %maximum_bitcast_fusion.inverse_ref, f32[1,4096]{1,0:T(1,128)} %bitcast.11, f32[1,4096]{1,0:T(1,128)} %bitcast.12, bf16[1024,4096]{1,0:T(8,128)(2,1)} %table_hbm.1, bf16[4096,256]{1,0:T(8,128)(2,1)} %wq_hbm.1, ...), custom_call_target="tpu_custom_call" | custom-call | tf_op jit(solution)/shard_map/layer/pallas_call | solution.py:830
  182.1 1.8 copy.13
  (1 shorter events, 0.0 us)

commit v6 on v5

--- a/solution.py
+++ b/solution.py
@@ -1,3 +1,5 @@
+import functools
+
 import jax
 import jax.numpy as jnp
 from jax import lax
@@ -128,135 +130,6 @@
 GATHER_SEMS = [DMA((2, 20)), DMA((2, 20))]
 
 
-def ring_reduce(part, r1, r2, held, s1, e1, s2, e2, z, x, make, finish):
-    half = part.shape[-1] // 2
-    quarter = half // 2
-    started = []
-
-    def at(h, k, j):
-        return (wrap(z + k), wrap(x + j)) if h == 0 else (wrap(z + j), wrap(x + k))
-
-    def mine(h, k, j, q):
-        a, b = at(h, k, j)
-        return part.at[a, pl.ds(b * UNITS, UNITS), :, pl.ds(h * half + q * quarter, quarter)]
-
-    def peer(h, axis, d):
-        a, b = at(h, d, 0) if axis == 0 else at(h, 0, d)
-        return {"tensor": a * SIDE + b}
-
-    def send1(h, slot, j, src, d):
-        copy = remote(src, r1.at[h, slot, j], s1.at[h, slot, j], e1.at[h, slot, j], peer(h, 0, d))
-        copy.start()
-        started.append(copy)
-
-    def recv1(h, slot, j):
-        ref = r1.at[h, slot, j]
-        remote(ref, ref, s1.at[h, slot, j], e1.at[h, slot, j], peer(h, 0, 1)).wait_recv()
-
-    def send2(h, slot, src, d):
-        copy = remote(src, r2.at[h, slot], s2.at[h, slot], e2.at[h, slot], peer(h, 1, d))
-        copy.start()
-        started.append(copy)
-
-    def recv2(h, slot):
-        ref = r2.at[h, slot]
-        remote(ref, ref, s2.at[h, slot], e2.at[h, slot], peer(h, 0, 1)).wait_recv()
-
-    def load(ref):
-        return ref[...].astype(F32)
-
-    order = (2, 1, 3, 0)
-    for h in range(2):
-        make(h, 2)
-        for j in order:
-            send1(h, 0, j, mine(h, 2, j, 0), 1)
-            send1(h, 3, j, mine(h, 2, j, 1), -1)
-    for h in range(2):
-        make(h, 1)
-        for j in order:
-            send1(h, 1, j, mine(h, 1, j, 1), 1)
-        make(h, 3)
-        for j in order:
-            send1(h, 4, j, mine(h, 3, j, 0), -1)
-    for j in order:
-        for h in range(2):
-            recv1(h, 0, j)
-            r1[h, 0, j] = (load(r1.at[h, 0, j]) + load(mine(h, 1, j, 0))).astype(BF16)
-            send1(h, 2, j, r1.at[h, 0, j], 1)
-            recv1(h, 3, j)
-            r1[h, 3, j] = (load(r1.at[h, 3, j]) + load(mine(h, 3, j, 1))).astype(BF16)
-            send1(h, 5, j, r1.at[h, 3, j], -1)
-    for h in range(2):
-        make(h, 0)
-
-    def arrived(h, j):
-        for slot in (1, 4, 2, 5):
-            recv1(h, slot, j)
-
-    def summed(h, j, q):
-        a, b = ((2, 4), (1, 5))[q]
-        return load(mine(h, 0, j, q)) + load(r1.at[h, a, j]) + load(r1.at[h, b, j])
-
-    for h in range(2):
-        arrived(h, 2)
-        for q, slot, d in ((0, 0, 1), (1, 3, -1)):
-            held[h, 0, q] = summed(h, 2, q).astype(BF16)
-            send2(h, slot, held.at[h, 0, q], d)
-    for h in range(2):
-        arrived(h, 1)
-        held[h, 1, 1] = summed(h, 1, 1).astype(BF16)
-        send2(h, 1, held.at[h, 1, 1], 1)
-        arrived(h, 3)
-        held[h, 2, 0] = summed(h, 3, 0).astype(BF16)
-        send2(h, 4, held.at[h, 2, 0], -1)
-    for h in range(2):
-        recv2(h, 0)
-        held[h, 1, 0] = (summed(h, 1, 0) + load(r2.at[h, 0])).astype(BF16)
-        send2(h, 2, held.at[h, 1, 0], 1)
-        recv2(h, 3)
-        held[h, 2, 1] = (summed(h, 3, 1) + load(r2.at[h, 3])).astype(BF16)
-        send2(h, 5, held.at[h, 2, 1], -1)
-    for h in range(2):
-        arrived(h, 0)
-        for slot in (1, 4, 2, 5):
-            recv2(h, slot)
-        for q in range(2):
-            a, b = ((2, 4), (1, 5))[q]
-            value = summed(h, 0, q) + load(r2.at[h, a]) + load(r2.at[h, b])
-            finish(pl.ds(h * half + q * quarter, quarter), flat(value))
-    for copy in started:
-        copy.wait_send()
-
-
-def products(a_ref, w_ref, part, z, x):
-    rows, width = UNITS * UNIT, part.shape[3]
-    half = width // 2
-    step = min(512, half)
-
-    def make(h, k):
-        def run(blocks):
-            lhs = jnp.concatenate(
-                [a_ref[pl.ds(pl.multiple_of((a * SIDE + b) * rows, 16), rows), :] for a, b in blocks], axis=0
-            )
-
-            def column(c, carry):
-                cols = pl.ds(pl.multiple_of(h * half + c * step, step), step)
-                out = jnp.dot(lhs, w_ref[:, cols], preferred_element_type=F32).astype(BF16)
-                for n, (a, b) in enumerate(blocks):
-                    block = out[n * rows:(n + 1) * rows].reshape(UNITS, UNIT, step)
-                    part[a, pl.ds(b * UNITS, UNITS), :, cols] = block
-                return carry
-
-            lax.fori_loop(0, half // step, column, 0)
-
-        if h == 0:
-            run([(wrap(z + k), b) for b in range(SIDE)])
-        else:
-            run([(a, wrap(x + k)) for a in range(SIDE)])
-
-    return make
-
-
 def flat(block):
     return block.reshape(-1, block.shape[-1])
 
@@ -339,44 +212,94 @@
             copy.wait_send()
 
 
-def short_reduce(att, att_z, att_x, wo, part, mine, got, ssem, rsem, bs, br, z, x, finish):
-    half = part.shape[-1] // 2
+class SpreadDown:
+    def __init__(self, w_hbm, blocks, sems, z, x):
+        r = lax.axis_index("dp")
+        self.y, self.c = r // 2, lax.rem(r, 2)
+        self.w, self.blocks, self.sems, self.z, self.x = w_hbm, blocks, sems, z, x
+        self.units = blocks.shape[1] // SIDE
+        self.half = blocks.shape[-1] // 2
+        self.started = []
+
+    def columns(self, c, q=None):
+        size = self.half if q is None else self.half // 2
+        start = c * self.half + (0 if q is None else q * size)
+        return pl.ds(pl.multiple_of(start, size), size)
+
+    def rows(self, dy):
+        return pl.ds(lax.rem(self.y + dy + SIDE, SIDE) * self.units, self.units)
+
+    def view(self, o, dy, c, q=None):
+        return self.blocks.at[o - 1, self.rows(dy), :, self.columns(c, q)]
+
+    def copy(self, phase, index, src, dst, peer, start):
+        send, recv = self.sems[2 * phase:2 * phase + 2]
+        copy = remote(src, dst, send.at[index], recv.at[index], peer)
+        if start:
+            copy.start()
+            self.started.append(copy)
+        else:
+            copy.wait_recv()
+
+    def along(self, d):
+        return {"tensor": place(self.z + d * (1 - self.c), self.x + d * self.c)}
+
+    def plane(self, start):
+        for n, (o, d) in enumerate(((3, 1), (1, -1))):
+            dst = self.view(o, 0, self.c)
+            src = self.w.at[self.rows(0), :, self.columns(self.c)] if start else dst
+            self.copy(0, n, src, dst, self.along(d), start)
+
+    def plane_far(self, start):
+        for n, (o, d) in enumerate(((3, 1), (1, -1))):
+            dst = self.view(2, 0, self.c, n)
+            self.copy(0, 2 + n, self.view(o, 0, self.c, n) if start else dst, dst, self.along(d), start)
+
+    def around(self, d):
+        return {"dp": lax.rem(self.y + d + SIDE, SIDE) * 2 + self.c}
+
+    def ring(self, start):
+        for o in (1, 2, 3):
+            for k, d in enumerate((1, -1)):
+                ref = self.view(o, 0 if start else -d, self.c)
+                self.copy(1, k * 6 + o - 1, ref, ref, self.around(d), start)
+
+    def ring_far(self, start):
+        for o in (1, 2, 3):
+            for k, d in enumerate((1, -1)):
+                ref = self.view(o, -d if start else -2 * d, self.c, k)
+                self.copy(1, k * 6 + 2 + o, ref, ref, self.around(d), start)
+
+    def cores(self, start, steps):
+        peer = {"dp": self.y * 2 + 1 - self.c}
+        for dy in steps:
+            for o in (1, 2, 3):
+                ref = self.view(o, dy, self.c if start else 1 - self.c)
+                self.copy(2, dy * 3 + o - 1, ref, ref, peer, start)
+
+    def drain(self):
+        for copy in self.started:
+            copy.wait_send()
+
+
+def short_reduce(mine, got, ssem, rsem, z, x, arrive, multiply, finish):
+    half = mine.shape[-1]
     quarter = half // 2
     started = []
-
-    def along(h, d):
-        return {"tensor": place(z + d, x) if h == 0 else place(z, x + d)}
-
-    def across(h, d):
-        return along(1 - h, d)
-
-    def rows_for(h, d):
-        return att.at[wrap(z + d)] if h == 0 else att.at[:, pl.ds(wrap(x + d) * UNITS, UNITS)]
-
-    def landing(h, o):
-        return (att_z, att_x)[h].at[o - 1]
-
-    def move(h, o):
-        return remote(rows_for(h, o), landing(h, SIDE - o), bs.at[h, o - 1], br.at[h, o - 1], along(h, o))
-
-    for h in range(2):
-        for o in (2, 1, 3):
-            copy = move(h, o)
-            copy.start()
-            started.append(copy)
 
     def block(h, j, q):
         n = wrap(x + j) if h == 0 else wrap(z + j)
         return mine.at[h, pl.ds(n * UNITS, UNITS), :, pl.ds(q * quarter, quarter)]
 
     def send(h, slot, src, d):
-        copy = remote(src, got.at[h, slot], ssem.at[h, slot], rsem.at[h, slot], across(h, d))
+        peer = {"tensor": place(z, x + d) if h == 0 else place(z + d, x)}
+        copy = remote(src, got.at[h, slot], ssem.at[h, slot], rsem.at[h, slot], peer)
         copy.start()
         started.append(copy)
 
     def recv(h, slot):
         ref = got.at[h, slot]
-        remote(ref, ref, ssem.at[h, slot], rsem.at[h, slot], across(h, 1)).wait_recv()
+        remote(ref, ref, ssem.at[h, slot], rsem.at[h, slot], {"tensor": place(z, x + 1)}).wait_recv()
 
     def load(ref):
         return ref[...].astype(F32)
@@ -384,16 +307,10 @@
     step = min(512, quarter)
 
     def make(h, q):
-        own = flat(rows_for(h, 0)[...])
-        others = jnp.concatenate([flat(landing(h, o)[...]) for o in (1, 2, 3)], axis=1)
-
         def column(c, carry):
             at = pl.multiple_of(q * quarter + c * step, step)
-            cols = pl.ds(h * half + at, step)
-            out = jnp.dot(own, flat(wo[:, :, cols]), preferred_element_type=F32)
-            weights = part[:, :, :, cols].reshape(3 * own.shape[1], step)
-            out = out + jnp.dot(others, weights, preferred_element_type=F32)
-            mine[h, :, :, pl.ds(at, step)] = out.astype(BF16).reshape(SIDE * UNITS, UNIT, step)
+            out = multiply(h, pl.ds(h * half + at, step)).astype(BF16)
+            mine[h, :, :, pl.ds(at, step)] = out.reshape(SIDE * UNITS, UNIT, step)
             return carry
 
         lax.fori_loop(0, quarter // step, column, 0)
@@ -401,8 +318,7 @@
     for q in range(2):
         for h in range(2):
             if q == 0:
-                for o in (3, 1, 2):
-                    move(h, SIDE - o).wait_recv()
+                arrive(h)
             make(h, q)
             d = 1 - 2 * q
             send(h, 3 * q, block(h, 2, q), d)
@@ -419,6 +335,41 @@
             a, b = ((2, 4), (1, 5))[q]
             value = load(block(h, 0, q)) + load(got.at[h, a]) + load(got.at[h, b])
             finish(pl.ds(h * half + q * quarter, quarter), flat(value))
+    for copy in started:
+        copy.wait_send()
+
+
+def mix(att, att_z, att_x, wo, part, mine, got, ssem, rsem, bs, br, z, x, finish):
+    started = []
+
+    def rows_for(h, d):
+        return att.at[wrap(z + d)] if h == 0 else att.at[:, pl.ds(wrap(x + d) * UNITS, UNITS)]
+
+    def landing(h, o):
+        return (att_z, att_x)[h].at[o - 1]
+
+    def move(h, o):
+        peer = {"tensor": place(z + o, x) if h == 0 else place(z, x + o)}
+        return remote(rows_for(h, o), landing(h, SIDE - o), bs.at[h, o - 1], br.at[h, o - 1], peer)
+
+    for h in range(2):
+        for o in (2, 1, 3):
+            copy = move(h, o)
+            copy.start()
+            started.append(copy)
+
+    def arrive(h):
+        for o in (3, 1, 2):
+            move(h, SIDE - o).wait_recv()
+
+    def multiply(h, cols):
+        own = flat(rows_for(h, 0)[...])
+        others = jnp.concatenate([flat(landing(h, o)[...]) for o in (1, 2, 3)], axis=1)
+        out = jnp.dot(own, flat(wo[:, :, cols]), preferred_element_type=F32)
+        weights = part[:, :, :, cols].reshape(others.shape[1], out.shape[1])
+        return out + jnp.dot(others, weights, preferred_element_type=F32)
+
+    short_reduce(mine, got, ssem, rsem, z, x, arrive, multiply, finish)
     for copy in started:
         copy.wait_send()
 
@@ -510,7 +461,7 @@
 QB = 256
 
 
-def attention(q_ref, first_ref, pair_ref, att_ref, win_ref, relay, m_ref, l_ref, acc_ref, ssem, rsem):
+def attention(q_ref, first_ref, pair_ref, att_ref, win_ref, relay, m_ref, l_ref, acc_ref, ssem, rsem, early, late):
     t = lax.axis_index("tensor")
     r = lax.axis_index("dp")
     y, c = r // 2, lax.rem(r, 2)
@@ -592,6 +543,7 @@
         for k in range(2):
             near[k].start()
 
+    early()
     for i in range(blocks):
         step(4, i, (i + 1) * QB, True)
 
@@ -633,6 +585,7 @@
             cross1[k].wait_recv()
 
     earlier(3 - c)
+    late()
 
     @pl.when(got_far)
     def _():
@@ -712,8 +665,8 @@
                  emb, all_ref, q, pair, cos_ref, sin_ref, first_ref, gs, gr,
                  win, relay, m_ref, l_ref, acc_ref, att, as_, ar,
                  stream, hid, gs2, gr2,
-                 part, r1, r2, held, s1, e1, s2, e2,
-                 att_z, att_x, mine, got, ss, sr, bs, br, ps, pr, ys, yr, cs, cr):
+                 part, att_z, att_x, mine, got, ss, sr, bs, br, ps, pr, ys, yr, cs, cr,
+                 down_blocks, hid_z, hid_x, ss2, sr2, zs, zr, hs, hr, *down_sems):
     z, x = here()
     t = lax.axis_index("tensor")
     r = lax.axis_index("dp")
@@ -735,8 +688,11 @@
     span_rows = rows * GROUP
     spread = Spread(wo_hbm, part, ps, pr, ys, yr, cs, cr, z, x)
     spread.plane(True)
+    down = SpreadDown(wd_hbm, down_blocks, down_sems, z, x)
+    hidden_width = wg.shape[0]
 
     def positions():
+        hid[:, :, :, hidden_width:] = jnp.zeros((*hid.shape[:3], hid.shape[3] - hidden_width), BF16)
         spread.plane(False)
         spread.plane_far(True)
         lanes = r * span_rows + lax.broadcasted_iota(jnp.int32, (1, span_rows), 1)
@@ -785,34 +741,93 @@
     ring_gather(all_ref, gs, gr, z, x, project)
     spread.ring_far(False)
     spread.cores(True, (2,))
-    attention(q, first_ref, pair, att, win, relay, m_ref, l_ref, acc_ref, as_, ar)
+
+    def late():
+        down.plane(False)
+        down.plane_far(True)
+
+    attention(
+        q, first_ref, pair, att, win, relay, m_ref, l_ref, acc_ref, as_, ar, functools.partial(down.plane, True), late
+    )
     spread.cores(False, (0, 1, 3))
+    down.plane_far(False)
+    down.ring(True)
+    down.cores(True, (0,))
 
     def mixed(cols, value):
         stream[:, cols] = (emb[:, cols].astype(F32) + value).astype(BF16)
 
     loads[3].wait()
     spread.cores(False, (2,))
-    short_reduce(att, att_z, att_x, wo, part, mine, got, ss, sr, bs, br, z, x, mixed)
+    mix(att, att_z, att_x, wo, part, mine, got, ss, sr, bs, br, z, x, mixed)
     spread.drain()
     all_ref[t] = normalize(stream[...].astype(F32), mlp_gain_ref[...])
     loads[4].wait()
     loads[5].wait()
 
+    loads[6].wait()
+    moves = []
+
+    def hidden_to_z(dz):
+        o = dz % SIDE
+        return remote(
+            hid.at[wrap(z + dz)], hid_z.at[SIDE - o - 1], zs.at[o - 1], zr.at[o - 1], {"tensor": place(z + o, x)}
+        )
+
+    def hidden_to_x(dz, o):
+        src = hid.at[wrap(z + dz), pl.ds(wrap(x + o) * UNITS, UNITS)]
+        dst = hid_x.at[SIDE - o - 1, wrap(z + dz)]
+        return remote(src, dst, hs.at[dz % SIDE, o - 1], hr.at[dz % SIDE, o - 1], {"tensor": place(z, x + o)})
+
     def gate(dz):
+        if dz == 0:
+            down.ring(False)
+            down.ring_far(True)
+            down.cores(True, (1, 3))
         lhs, span = row_group(all_ref, z, dz)
         across = (((1,), (1,)), ((), ()))
         gated = lax.dot_general(lhs, wg[...], across, preferred_element_type=F32)
         upper = lax.dot_general(lhs, wu[...], across, preferred_element_type=F32)
-        hid[span, :] = (gated / (1.0 + jnp.exp(-gated)) * upper).astype(BF16)
+        value = (gated / (1.0 + jnp.exp(-gated)) * upper).astype(BF16)
+        hid[wrap(z + dz), :, :, :hidden_width] = value.reshape(SIDE * UNITS, UNIT, hidden_width)
+        if dz:
+            moves.append(hidden_to_z(dz))
+        moves.extend(hidden_to_x(dz, o) for o in (2, 1, 3))
+        for copy in moves[-4 if dz else -3:]:
+            copy.start()
 
     ring_gather(all_ref, gs2, gr2, z, x, gate)
+    down.ring_far(False)
+    down.cores(True, (2,))
+
+    def arrive(h):
+        if h == 0:
+            for dz in (-1, 1, 2):
+                hidden_to_z(dz).wait_recv()
+            down.cores(False, (0, 1, 3, 2))
+        else:
+            for dz in (0, -1, 1, 2):
+                for o in (1, 3, 2):
+                    hidden_to_x(dz, o).wait_recv()
+
+    def multiply(h, cols):
+        def left(block):
+            return block.reshape(-1, hidden_width)
+
+        own = hid[z, :, :, :hidden_width] if h == 0 else hid[:, pl.ds(x * UNITS, UNITS), :, :hidden_width]
+        out = jnp.dot(left(own), flat(wd[:, :, cols]), preferred_element_type=F32)
+        for n in range(SIDE - 1):
+            block = hid_z[n, :, :, :hidden_width] if h == 0 else hid_x[n, :, :, :, :hidden_width]
+            out = out + jnp.dot(left(block), flat(down_blocks[n, :, :, cols]), preferred_element_type=F32)
+        return out
 
     def added(cols, value):
         out_ref[:, cols] = (stream[:, cols].astype(F32) + value).astype(BF16)
 
-    loads[6].wait()
-    ring_reduce(part, r1, r2, held, s1, e1, s2, e2, z, x, products(hid, wd, part, z, x), added)
+    short_reduce(mine, got, ss2, sr2, z, x, arrive, multiply, added)
+    for copy in moves:
+        copy.wait_send()
+    down.drain()
     for copy in copies:
         copy.wait_send()
 
@@ -823,10 +838,10 @@
     blocks = span // QB
     quarter = width // 4
     unit = (UNITS, UNIT)
+    padded = -(-wg.shape[0] // 128) * 128
     whole = pl.BlockSpec(memory_space=VMEM)
     outside = pl.BlockSpec(memory_space=pl.ANY)
     peers = DMA((GROUP - 1,))
-    reduce_sems = [DMA((2, 6, SIDE)), DMA((2, 6, SIDE)), DMA((2, 6)), DMA((2, 6))]
     return pl.pallas_call(
         layer_kernel,
         out_shape=jax.ShapeDtypeStruct((rows, width), BF16),
@@ -843,16 +858,16 @@
             VMEM((5, 2, span, HD), BF16), VMEM((span, HD), BF16),
             VMEM((blocks, 1, 2 * QB), F32), VMEM((blocks, 1, 2 * QB), F32), VMEM((blocks, HD, 2 * QB), F32),
             VMEM((SIDE, SIDE * UNITS, UNIT, 2 * HD), BF16), DMA((12,)), DMA((12,)),
-            VMEM((rows, width), BF16), VMEM((span, wg.shape[0]), BF16), *GATHER_SEMS,
+            VMEM((rows, width), BF16), VMEM((SIDE, SIDE * UNITS, UNIT, padded), BF16), *GATHER_SEMS,
             VMEM((SIDE, SIDE * UNITS, UNIT, width), BF16),
-            VMEM((2, 6, SIDE, *unit, quarter), BF16),
-            VMEM((2, 6, *unit, quarter), BF16),
-            VMEM((2, 3, 2, *unit, quarter), BF16),
-            *reduce_sems,
             VMEM((SIDE - 1, SIDE * UNITS, UNIT, 2 * HD), BF16), VMEM((SIDE - 1, SIDE, *unit, 2 * HD), BF16),
             VMEM((2, SIDE * UNITS, UNIT, 2 * quarter), BF16), VMEM((2, 6, *unit, quarter), BF16),
             DMA((2, 6)), DMA((2, 6)), DMA((2, 3)), DMA((2, 3)),
             DMA((8,)), DMA((8,)), DMA((18,)), DMA((18,)), DMA((24,)), DMA((24,)),
+            VMEM((SIDE - 1, *wd.shape), BF16),
+            VMEM((SIDE - 1, SIDE * UNITS, UNIT, padded), BF16), VMEM((SIDE - 1, SIDE, *unit, padded), BF16),
+            DMA((2, 6)), DMA((2, 6)), DMA((SIDE - 1,)), DMA((SIDE - 1,)), DMA((SIDE, SIDE - 1)), DMA((SIDE, SIDE - 1)),
+            DMA((4,)), DMA((4,)), DMA((12,)), DMA((12,)), DMA((12,)), DMA((12,)),
         ],
         compiler_params=pltpu.CompilerParams(
             collective_id=0, has_side_effects=True, vmem_limit_bytes=63 * 2**20
@@ -866,7 +881,7 @@
     inverse = jnp.concatenate([inverse, inverse])[None, :]
     return layer(
         ids[None, :], doc_lengths, inverse, attn_gain[None, :], mlp_gain[None, :],
-        table, wq, wkv, wo.reshape(-1, UNIT, wo.shape[1]), w_gate.T, w_up.T, w_down,
+        table, wq, wkv, wo.reshape(-1, UNIT, wo.shape[1]), w_gate.T, w_up.T, w_down.reshape(-1, UNIT, wo.shape[1]),
     )
 
 

time: 184 us -> 177 us (0.962)
  Pallas kernels: 182 us -> 174 us
    pallas_call x1, Pallas kernels: 182 us -> 174 us  [layer(): pl.pallas_call(layer_kernel, out_shape=jax.ShapeDtypeStruct((rows, width)...]
where the time goes in v6:
time: 177 us
  Pallas kernels  174 us (98%)
  local copies, waits for them, and re-layouts  1.77 us (1%)
    pallas_call x1, Pallas kernels, layer(): pl.pallas_call(layer_kernel, out_shape=jax.ShapeDtypeStruct((rows, width)...  174 us

profile of v6, /device:TPU:16, one launch (start us, length us, event | category | flops | bytes accessed | tf_op | source)
XLA Modules:
  0.0 176.9 jit_solution(16338478113684149487)
XLA Ops:
  0.0 0.6 maximum_bitcast_fusion.inverse_ref
  0.6 174.5 %layer.1 = bf16[48,4096]{1,0:T(8,128)(2,1)} custom-call(s32[1,48]{1,0:T(1,128)} %bitcast.15, s32[16]{0:T(128)} %lengths_ref.1, f32[1,128]{1,0:T(1,128)} %maximum_bitcast_fusion.inverse_ref, f32[1,4096]{1,0:T(1,128)} %bitcast.13, f32[1,4096]{1,0:T(1,128)} %bitcast.14, bf16[1024,4096]{1,0:T(8,128)(2,1)} %table_hbm.1, bf16[4096,256]{1,0:T(8,128)(2,1)} %wq_hbm.1, ...), custom_call_target="tpu_custom_call" | custom-call | tf_op jit(solution)/shard_map/layer/pallas_call | solution.py:845
  175.1 1.8 copy.13
  (1 shorter events, 0.0 us)

commit v7 on v6

--- a/solution.py
+++ b/solution.py
@@ -2,6 +2,7 @@
 
 import jax
 import jax.numpy as jnp
+import numpy as np
 from jax import lax
 from jax.experimental import pallas as pl
 from jax.experimental.pallas import tpu as pltpu
@@ -132,6 +133,50 @@
 
 def flat(block):
     return block.reshape(-1, block.shape[-1])
+
+
+def flat_units(block):
+    return block.reshape(-1, UNIT, block.shape[-1])
+
+
+class Moves:
+    def __init__(self, rows, to_z, to_x, zs, zr, xs, xr, z, x):
+        self.refs = rows, to_z, to_x, zs, zr, xs, xr
+        self.z, self.x = z, x
+        self.started = []
+
+    def along_z(self, dz):
+        rows, to_z, to_x, zs, zr, xs, xr = self.refs
+        o = dz % SIDE
+        peer = {"tensor": place(self.z + o, self.x)}
+        return remote(rows.at[wrap(self.z + dz)], to_z.at[SIDE - o - 1], zs.at[o - 1], zr.at[o - 1], peer)
+
+    def along_x(self, dz, o):
+        rows, to_z, to_x, zs, zr, xs, xr = self.refs
+        zz = wrap(self.z + dz)
+        src = rows.at[zz, pl.ds(wrap(self.x + o) * UNITS, UNITS)]
+        sems = xs.at[dz % SIDE, o - 1], xr.at[dz % SIDE, o - 1]
+        return remote(src, to_x.at[SIDE - o - 1, zz], *sems, {"tensor": place(self.z, self.x + o)})
+
+    def finished(self, dz):
+        moves = [self.along_z(dz)] if dz else []
+        moves += [self.along_x(dz, o) for o in (2, 1, 3)]
+        for move in moves:
+            move.start()
+        self.started += moves
+
+    def arrive(self, h):
+        if h == 0:
+            for dz in (-1, 1, 2):
+                self.along_z(dz).wait_recv()
+        else:
+            for dz in (2, 1, -1, 0):
+                for o in (1, 3, 2):
+                    self.along_x(dz, o).wait_recv()
+
+    def drain(self):
+        for move in self.started:
+            move.wait_send()
 
 
 class Spread:
@@ -339,39 +384,16 @@
         copy.wait_send()
 
 
-def mix(att, att_z, att_x, wo, part, mine, got, ssem, rsem, bs, br, z, x, finish):
-    started = []
-
-    def rows_for(h, d):
-        return att.at[wrap(z + d)] if h == 0 else att.at[:, pl.ds(wrap(x + d) * UNITS, UNITS)]
-
-    def landing(h, o):
-        return (att_z, att_x)[h].at[o - 1]
-
-    def move(h, o):
-        peer = {"tensor": place(z + o, x) if h == 0 else place(z, x + o)}
-        return remote(rows_for(h, o), landing(h, SIDE - o), bs.at[h, o - 1], br.at[h, o - 1], peer)
-
-    for h in range(2):
-        for o in (2, 1, 3):
-            copy = move(h, o)
-            copy.start()
-            started.append(copy)
-
-    def arrive(h):
-        for o in (3, 1, 2):
-            move(h, SIDE - o).wait_recv()
-
+def mix(moves, att, att_z, att_x, wo, part, mine, got, ssem, rsem, z, x, finish):
     def multiply(h, cols):
-        own = flat(rows_for(h, 0)[...])
-        others = jnp.concatenate([flat(landing(h, o)[...]) for o in (1, 2, 3)], axis=1)
+        own = flat(att[z] if h == 0 else att[:, pl.ds(x * UNITS, UNITS)])
+        others = jnp.concatenate([flat((att_z, att_x)[h][n]) for n in range(SIDE - 1)], axis=1)
         out = jnp.dot(own, flat(wo[:, :, cols]), preferred_element_type=F32)
         weights = part[:, :, :, cols].reshape(others.shape[1], out.shape[1])
         return out + jnp.dot(others, weights, preferred_element_type=F32)
 
-    short_reduce(mine, got, ssem, rsem, z, x, arrive, multiply, finish)
-    for copy in started:
-        copy.wait_send()
+    short_reduce(mine, got, ssem, rsem, z, x, moves.arrive, multiply, finish)
+    moves.drain()
 
 
 def normalize(rows, gain):
@@ -458,16 +480,13 @@
     return first
 
 
-QB = 256
-
-
-def attention(q_ref, first_ref, pair_ref, att_ref, win_ref, relay, m_ref, l_ref, acc_ref, ssem, rsem, early, late):
+def attention(q_ref, first_ref, pair_ref, att_ref, win_ref, relay, m_ref, l_ref, acc_ref, ssem, rsem, z, early, late, done):
     t = lax.axis_index("tensor")
     r = lax.axis_index("dp")
     y, c = r // 2, lax.rem(r, 2)
     kind = lax.rem(t, 2)
     rows = q_ref.shape[0]
-    blocks = rows // QB
+    group = rows // SIDE
     partner = {"tensor": t + 1 - 2 * kind}
     up = {"dp": lax.rem(y + 1, SIDE) * 2 + c}
     down = {"dp": lax.rem(y + SIDE - 1, SIDE) * 2 + c}
@@ -477,18 +496,16 @@
         return remote(src, dst, ssem.at[n], rsem.at[n], peer)
 
     def step(w, i, count, causal):
-        span = pl.ds(i * QB, QB)
+        span = pl.ds(pl.multiple_of(i * group, UNIT), group)
         q = jnp.concatenate([q_ref[span, :HD], q_ref[span, HD:]], axis=0)
-        first = first_ref[:, span]
-        first = jnp.concatenate([first, first], axis=1)
         scores = lax.dot_general(
             win_ref[w, 0, :count, :], q, (((1,), (1,)), ((), ())), preferred_element_type=F32
         )
         at = lax.broadcasted_iota(jnp.int32, (count, 1), 0) + w * rows
-        allowed = at >= first
+        allowed = at >= first_ref[i]
         if causal:
-            query = lax.broadcasted_iota(jnp.int32, (1, QB), 1) + (4 * rows + i * QB)
-            allowed &= at <= jnp.concatenate([query, query], axis=1)
+            query = lax.rem(lax.broadcasted_iota(jnp.int32, (1, 2 * group), 1), group)
+            allowed &= at <= query + (4 * rows + i * group)
         scores = jnp.where(allowed, scores, NEGATIVE)
         top = jnp.max(scores, axis=0, keepdims=True) * EXP_SCALE
         if not causal:
@@ -505,10 +522,10 @@
         acc_ref[i] = added if causal else acc_ref[i] * decay + added
         m_ref[i] = top
 
-    def earlier(w):
+    def earlier(w, steps=range(SIDE)):
         @pl.when(r + w >= 4)
         def _():
-            for i in range(blocks):
+            for i in steps:
                 step(w, i, rows, False)
 
     swap = copy(0, pair_ref, win_ref.at[4, kind], partner)
@@ -544,8 +561,8 @@
             near[k].start()
 
     early()
-    for i in range(blocks):
-        step(4, i, (i + 1) * QB, True)
+    for i in range(SIDE):
+        step(4, i, (i + 1) * group, True)
 
     @pl.when(relays)
     def _():
@@ -602,21 +619,22 @@
         for k in range(2):
             cross0[k].wait_recv()
 
-    earlier(c)
+    order = [wrap(z + dz) for dz in (2, 1, -1, 0)]
+    earlier(c, order[:2])
 
     @pl.when(got_far & (c == 0))
     def _():
         for k in range(2):
             far1[k].wait_recv()
 
-    earlier(1 - c)
-    for i in range(blocks):
-        out = acc_ref[i] / l_ref[i]
+    for n, i in enumerate(order):
+        if n > 1:
+            earlier(c, [i])
+        earlier(1 - c, [i])
+        out = (acc_ref[i] / l_ref[i]).T.astype(BF16)
         for h in range(2):
-            head = out[:, h * QB:(h + 1) * QB].T.astype(BF16)
-            for n in range(QB // UNIT):
-                unit = i * QB // UNIT + n
-                att_ref[unit // 12, unit % 12, :, h * HD:(h + 1) * HD] = head[n * UNIT:(n + 1) * UNIT]
+            att_ref[i, :, :, h * HD:(h + 1) * HD] = flat_units(out[h * group:(h + 1) * group])
+        done((2, 1, -1, 0)[n])
 
     @pl.when(c == 0)
     def _():
@@ -665,7 +683,7 @@
                  emb, all_ref, q, pair, cos_ref, sin_ref, first_ref, gs, gr,
                  win, relay, m_ref, l_ref, acc_ref, att, as_, ar,
                  stream, hid, gs2, gr2,
-                 part, att_z, att_x, mine, got, ss, sr, bs, br, ps, pr, ys, yr, cs, cr,
+                 part, att_z, att_x, mine, got, ss, sr, bs, br, bxs, bxr, ps, pr, ys, yr, cs, cr,
                  down_blocks, hid_z, hid_x, ss2, sr2, zs, zr, hs, hr, *down_sems):
     z, x = here()
     t = lax.axis_index("tensor")
@@ -695,8 +713,10 @@
         hid[:, :, :, hidden_width:] = jnp.zeros((*hid.shape[:3], hid.shape[3] - hidden_width), BF16)
         spread.plane(False)
         spread.plane_far(True)
-        lanes = r * span_rows + lax.broadcasted_iota(jnp.int32, (1, span_rows), 1)
-        first_ref[...] = document_starts(lengths_ref, lanes) - (r - 4) * span_rows
+        group = span_rows // SIDE
+        for i in range(SIDE):
+            lanes = lax.rem(lax.broadcasted_iota(jnp.int32, (1, 2 * group), 1), group) + (r * span_rows + i * group)
+            first_ref[i] = document_starts(lengths_ref, lanes) - (r - 4) * span_rows
         sign = jnp.where(lax.broadcasted_iota(jnp.int32, (1, HD), 1) < HD // 2, -1.0, 1.0)
 
         def turn(b, carry):
@@ -742,12 +762,15 @@
     spread.ring_far(False)
     spread.cores(True, (2,))
 
+    moves_of = Moves(att, att_z, att_x, bs, br, bxs, bxr, z, x)
+
     def late():
         down.plane(False)
         down.plane_far(True)
 
     attention(
-        q, first_ref, pair, att, win, relay, m_ref, l_ref, acc_ref, as_, ar, functools.partial(down.plane, True), late
+        q, first_ref, pair, att, win, relay, m_ref, l_ref, acc_ref, as_, ar, z,
+        functools.partial(down.plane, True), late, moves_of.finished
     )
     spread.cores(False, (0, 1, 3))
     down.plane_far(False)
@@ -759,25 +782,14 @@
 
     loads[3].wait()
     spread.cores(False, (2,))
-    mix(att, att_z, att_x, wo, part, mine, got, ss, sr, bs, br, z, x, mixed)
+    mix(moves_of, att, att_z, att_x, wo, part, mine, got, ss, sr, z, x, mixed)
     spread.drain()
     all_ref[t] = normalize(stream[...].astype(F32), mlp_gain_ref[...])
     loads[4].wait()
     loads[5].wait()
 
     loads[6].wait()
-    moves = []
-
-    def hidden_to_z(dz):
-        o = dz % SIDE
-        return remote(
-            hid.at[wrap(z + dz)], hid_z.at[SIDE - o - 1], zs.at[o - 1], zr.at[o - 1], {"tensor": place(z + o, x)}
-        )
-
-    def hidden_to_x(dz, o):
-        src = hid.at[wrap(z + dz), pl.ds(wrap(x + o) * UNITS, UNITS)]
-        dst = hid_x.at[SIDE - o - 1, wrap(z + dz)]
-        return remote(src, dst, hs.at[dz % SIDE, o - 1], hr.at[dz % SIDE, o - 1], {"tensor": place(z, x + o)})
+    hidden = Moves(hid, hid_z, hid_x, zs, zr, hs, hr, z, x)
 
     def gate(dz):
         if dz == 0:
@@ -790,25 +802,16 @@
         upper = lax.dot_general(lhs, wu[...], across, preferred_element_type=F32)
         value = (gated / (1.0 + jnp.exp(-gated)) * upper).astype(BF16)
         hid[wrap(z + dz), :, :, :hidden_width] = value.reshape(SIDE * UNITS, UNIT, hidden_width)
-        if dz:
-            moves.append(hidden_to_z(dz))
-        moves.extend(hidden_to_x(dz, o) for o in (2, 1, 3))
-        for copy in moves[-4 if dz else -3:]:
-            copy.start()
+        hidden.finished(dz)
 
     ring_gather(all_ref, gs2, gr2, z, x, gate)
     down.ring_far(False)
     down.cores(True, (2,))
 
     def arrive(h):
+        hidden.arrive(h)
         if h == 0:
-            for dz in (-1, 1, 2):
-                hidden_to_z(dz).wait_recv()
             down.cores(False, (0, 1, 3, 2))
-        else:
-            for dz in (0, -1, 1, 2):
-                for o in (1, 3, 2):
-                    hidden_to_x(dz, o).wait_recv()
 
     def multiply(h, cols):
         def left(block):
@@ -825,8 +828,7 @@
         out_ref[:, cols] = (stream[:, cols].astype(F32) + value).astype(BF16)
 
     short_reduce(mine, got, ss2, sr2, z, x, arrive, multiply, added)
-    for copy in moves:
-        copy.wait_send()
+    hidden.drain()
     down.drain()
     for copy in copies:
         copy.wait_send()
@@ -835,7 +837,7 @@
 def layer(ids, lengths, inverse, attn_gain, mlp_gain, table, wq, wkv, wo, wg, wu, wd):
     rows, width = ids.shape[1], table.shape[1]
     span = rows * GROUP
-    blocks = span // QB
+    group = span // SIDE
     quarter = width // 4
     unit = (UNITS, UNIT)
     padded = -(-wg.shape[0] // 128) * 128
@@ -854,15 +856,16 @@
             peers, peers, DMA((2, GROUP - 1)), DMA((2, GROUP - 1)),
             VMEM((rows, width), BF16), VMEM((GROUP, rows, width), BF16),
             VMEM((span, wq.shape[1]), BF16), VMEM((span, HD), BF16),
-            VMEM((span, HD), F32), VMEM((span, HD), F32), VMEM((1, span), jnp.int32), *GATHER_SEMS,
+            VMEM((span, HD), F32), VMEM((span, HD), F32), VMEM((SIDE, 1, 2 * group), jnp.int32), *GATHER_SEMS,
             VMEM((5, 2, span, HD), BF16), VMEM((span, HD), BF16),
-            VMEM((blocks, 1, 2 * QB), F32), VMEM((blocks, 1, 2 * QB), F32), VMEM((blocks, HD, 2 * QB), F32),
+            VMEM((SIDE, 1, 2 * group), F32), VMEM((SIDE, 1, 2 * group), F32), VMEM((SIDE, HD, 2 * group), F32),
             VMEM((SIDE, SIDE * UNITS, UNIT, 2 * HD), BF16), DMA((12,)), DMA((12,)),
             VMEM((rows, width), BF16), VMEM((SIDE, SIDE * UNITS, UNIT, padded), BF16), *GATHER_SEMS,
             VMEM((SIDE, SIDE * UNITS, UNIT, width), BF16),
             VMEM((SIDE - 1, SIDE * UNITS, UNIT, 2 * HD), BF16), VMEM((SIDE - 1, SIDE, *unit, 2 * HD), BF16),
             VMEM((2, SIDE * UNITS, UNIT, 2 * quarter), BF16), VMEM((2, 6, *unit, quarter), BF16),
-            DMA((2, 6)), DMA((2, 6)), DMA((2, 3)), DMA((2, 3)),
+            DMA((2, 6)), DMA((2, 6)),
+            DMA((SIDE - 1,)), DMA((SIDE - 1,)), DMA((SIDE, SIDE - 1)), DMA((SIDE, SIDE - 1)),
             DMA((8,)), DMA((8,)), DMA((18,)), DMA((18,)), DMA((24,)), DMA((24,)),
             VMEM((SIDE - 1, *wd.shape), BF16),
             VMEM((SIDE - 1, SIDE * UNITS, UNIT, padded), BF16), VMEM((SIDE - 1, SIDE, *unit, padded), BF16),
@@ -877,8 +880,8 @@
 
 
 def local(ids, doc_lengths, table, attn_gain, wq, wkv, wo, mlp_gain, w_gate, w_up, w_down):
-    inverse = ROPE_BASE ** (-jnp.arange(HD // 2, dtype=jnp.float32) * 2.0 / HD)
-    inverse = jnp.concatenate([inverse, inverse])[None, :]
+    inverse = np.float32(ROPE_BASE) ** (-np.arange(HD // 2, dtype=np.float32) * np.float32(2.0 / HD))
+    inverse = jnp.asarray(np.concatenate([inverse, inverse])[None, :], F32)
     return layer(
         ids[None, :], doc_lengths, inverse, attn_gain[None, :], mlp_gain[None, :],
         table, wq, wkv, wo.reshape(-1, UNIT, wo.shape[1]), w_gate.T, w_up.T, w_down.reshape(-1, UNIT, wo.shape[1]),

time: 177 us -> 177 us (level)
  no operation moved by 1% of the time
where the time goes in v7:
time: 177 us; the launch traced here: 176 us
  Pallas kernels  175 us (99%)
  local copies, waits for them, and re-layouts  1.77 us (1%)
    pallas_call x1, Pallas kernels, layer(): pl.pallas_call(layer_kernel, out_shape=jax.ShapeDtypeStruct((rows, width)...  175 us

profile of v7, /device:TPU:16, one launch (start us, length us, event | category | flops | bytes accessed | tf_op | source)
XLA Modules:
  0.0 176.4 jit_solution(14760548567908493308)
XLA Ops:
  0.0 174.6 %layer.1 = bf16[48,4096]{1,0:T(8,128)(2,1)} custom-call(s32[1,48]{1,0:T(1,128)} %bitcast.13, s32[16]{0:T(128)} %lengths_ref.1, f32[1,128]{1,0:T(1,128)} %constant.2.clone.inverse_ref, f32[1,4096]{1,0:T(1,128)} %bitcast.11, f32[1,4096]{1,0:T(1,128)} %bitcast.12, bf16[1024,4096]{1,0:T(8,128)(2,1)} %table_hbm.1, bf16[4096,256]{1,0:T(8,128)(2,1)} %wq_hbm.1, ...), custom_call_target="tpu_custom_call" | custom-call | tf_op jit(solution)/shard_map/layer/pallas_call | solution.py:847
  174.6 1.8 %copy.14 = bf16[48,4096]{1,0:T(8,128)(2,1)} copy(bf16[48,4096]{1,0:T(8,128)(2,1)} %layer.1) | data formatting | bytes 786432

commit v8 on v7

--- a/solution.py
+++ b/solution.py
@@ -53,7 +53,7 @@
     )
 
 
-def ring_gather(buf, ssem, rsem, z, x, ready):
+def ring_gather(buf, ssem, rsem, z, x, ready, begun=lambda: None):
     half = buf.shape[-1] // 2
     quarter = half // 2
     started = []
@@ -83,6 +83,7 @@
     for h in range(2):
         send(h, 4, 0, 0, 0, 1, 1)
         send(h, 5, 0, 0, 0, 1, -1)
+    begun()
     for h in range(2):
         recv(h, 0, -1, 0, 0)
         send(h, 2, -1, 0, 1, 0, 1)
@@ -408,7 +409,7 @@
     return lhs, pl.ds(pl.multiple_of(zz * SIDE * rows, 16), SIDE * rows)
 
 
-def find_rows(ids_ref, all_ids, wanted_by, table, found, recv, emb_ref, t, peers, sources, load, ks, kr, xs, xr, meanwhile):
+def find_rows(ids_ref, all_ids, wanted_by, table, found, recv, emb_ref, t, peers, sources, load, ks, kr, xs, xr, asked, meanwhile):
     copies = []
     rows, width = emb_ref.shape
     wanted_by[...] = jnp.full_like(wanted_by, -1)
@@ -430,6 +431,7 @@
     before = jnp.where(row < lane, 1.0, 0.0).astype(BF16)
     for n, p in enumerate(sources):
         remote(wanted_by, all_ids.at[p], ks.at[n], kr.at[n], {"tensor": p}).wait_recv()
+    asked()
     local_rows = all_ids[...].reshape(slots, 128) - t * owned
     inside = (local_rows >= 0) & (local_rows < owned)
     rank = jnp.dot(jnp.where(inside, 1.0, 0.0).astype(BF16), before, preferred_element_type=F32)
@@ -528,105 +530,91 @@
             for i in steps:
                 step(w, i, rows, False)
 
-    swap = copy(0, pair_ref, win_ref.at[4, kind], partner)
-    swap.start()
-    win_ref[4, kind] = pair_ref[...]
-    swap_in = copy(0, pair_ref, win_ref.at[4, 1 - kind], partner)
-    up_key = copy(1, win_ref.at[4, 0], win_ref.at[2, 0], up)
-    up_value = copy(2, win_ref.at[4, 1], win_ref.at[2, 1], up)
-    far_key = copy(3, win_ref.at[2, 0], win_ref.at[0, 0], up)
-    down_value = copy(4, win_ref.at[4, 1], relay, down)
-    far_value = copy(5, relay, win_ref.at[0, 1], down)
-    near = [copy(6 + k, win_ref.at[4, k], win_ref.at[3, k], other) for k in range(2)]
-    cross0 = [copy(8 + k, win_ref.at[2, k], win_ref.at[1, k], other) for k in range(2)]
-    cross1 = [copy(8 + k, win_ref.at[2, k], win_ref.at[3, k], other) for k in range(2)]
-    far1 = [copy(10 + k, win_ref.at[0, k], win_ref.at[1, k], other) for k in range(2)]
+    piece = rows // 2
+
+    def block(w, k, p):
+        return win_ref.at[w, k, pl.ds(p * piece, piece)]
+
+    def pieces(n, src, dst, peer):
+        return [copy(2 * n + p, src(p), dst(p), peer) for p in range(2)]
+
+    def within(n, source, target, k, peer):
+        return pieces(n, lambda p: block(source, k, p), lambda p: block(target, k, p), peer)
+
+    def mine(p):
+        return pair_ref.at[pl.ds(p * piece, piece)]
+
+    def held(p):
+        return relay.at[pl.ds(p * piece, piece)]
+
+    def when(condition, *acts):
+        @pl.when(condition)
+        def _():
+            for act in acts:
+                act()
+
+    def starts(copies):
+        return [one.start for one in copies]
+
+    def recvs(copies):
+        return [one.wait_recv for one in copies]
+
+    def sends(copies):
+        return [one.wait_send for one in copies]
+
+    lacking = 1 - kind
+    swap = pieces(0, mine, lambda p: block(4, kind, p), partner)
+    swap_in = pieces(0, mine, lambda p: block(4, lacking, p), partner)
+    up_own = pieces(1, mine, lambda p: block(2, kind, p), up)
+    up_other = within(2, 4, 2, lacking, up)
+    down_own = pieces(3, mine, held, down)
+    far_own = pieces(4, held, lambda p: block(0, kind, p), down)
+    far_other = within(5, 2, 0, lacking, up)
+    near_own = pieces(6, mine, lambda p: block(3, kind, p), other)
+    near_other = within(7, 4, 3, lacking, other)
+    cross0_own, cross0_other = within(8, 2, 1, kind, other), within(9, 2, 1, lacking, other)
+    cross1_own, cross1_other = within(8, 2, 3, kind, other), within(9, 2, 3, lacking, other)
+    far1 = within(10, 0, 1, kind, other) + within(11, 0, 1, lacking, other)
     has_up, has_far = y < SIDE - 1, y < SIDE - 2
     got_up, got_far = y > 0, y > 1
     relays = (y == SIDE - 1) | (y == 0)
-    swap_in.wait_recv()
-
-    @pl.when(has_far)
-    def _():
-        down_value.start()
-
-    @pl.when(has_up)
-    def _():
-        up_key.start()
-        up_value.start()
-
-    @pl.when(c == 0)
-    def _():
-        for k in range(2):
-            near[k].start()
-
+    for p in range(2):
+        swap[p].start()
+    when(has_up, *starts(up_own))
+    when(has_far, *starts(down_own))
+    when(c == 0, *starts(near_own))
+    win_ref[4, kind] = pair_ref[...]
+    for p in range(2):
+        swap_in[p].wait_recv()
+        when(has_up, up_other[p].start)
+        when(c == 0, near_other[p].start)
+        when(relays, down_own[p].wait_recv, far_own[p].start)
     early()
     for i in range(SIDE):
         step(4, i, (i + 1) * group, True)
 
-    @pl.when(relays)
-    def _():
-        down_value.wait_recv()
-        far_value.start()
-
-    @pl.when(got_up)
-    def _():
-        up_key.wait_recv()
-
-        @pl.when(has_up)
-        def _():
-            far_key.start()
-
-        up_value.wait_recv()
-
-        @pl.when(c == 0)
-        def _():
-            for k in range(2):
-                cross0[k].start()
-
-        @pl.when(c == 1)
-        def _():
-            for k in range(2):
-                cross1[k].start()
-
-    @pl.when(c == 1)
-    def _():
-        for k in range(2):
-            near[k].wait_recv()
-
+    when(got_up, *recvs(up_own))
+    when(got_up & (c == 0), *starts(cross0_own))
+    when(got_up & (c == 1), *starts(cross1_own))
+    for p in range(2):
+        when(got_up, up_other[p].wait_recv)
+        when(got_up & has_up, far_other[p].start)
+        when(got_up & (c == 0), cross0_other[p].start)
+        when(got_up & (c == 1), cross1_other[p].start)
+    when(c == 1, *recvs(near_own + near_other))
     earlier(2 + c)
 
-    @pl.when(got_up & (c == 0))
-    def _():
-        for k in range(2):
-            cross1[k].wait_recv()
-
+    when(got_up & (c == 0), *recvs(cross1_own + cross1_other))
     earlier(3 - c)
     late()
 
-    @pl.when(got_far)
-    def _():
-        far_key.wait_recv()
-        far_value.wait_recv()
-
-        @pl.when(c == 1)
-        def _():
-            for k in range(2):
-                far1[k].start()
-
-    @pl.when(got_up & (c == 1))
-    def _():
-        for k in range(2):
-            cross0[k].wait_recv()
-
+    when(got_far, *recvs(far_own + far_other))
+    when(got_far & (c == 1), *starts(far1))
+    when(got_up & (c == 1), *recvs(cross0_own + cross0_other))
     order = [wrap(z + dz) for dz in (2, 1, -1, 0)]
     earlier(c, order[:2])
 
-    @pl.when(got_far & (c == 0))
-    def _():
-        for k in range(2):
-            far1[k].wait_recv()
-
+    when(got_far & (c == 0), *recvs(far1))
     for n, i in enumerate(order):
         if n > 1:
             earlier(c, [i])
@@ -636,44 +624,16 @@
             att_ref[i, :, :, h * HD:(h + 1) * HD] = flat_units(out[h * group:(h + 1) * group])
         done((2, 1, -1, 0)[n])
 
-    @pl.when(c == 0)
-    def _():
-        for k in range(2):
-            near[k].wait_send()
-
-    @pl.when(got_up & (c == 0))
-    def _():
-        for k in range(2):
-            cross0[k].wait_send()
-
-    @pl.when(got_up & (c == 1))
-    def _():
-        for k in range(2):
-            cross1[k].wait_send()
-
-    @pl.when(got_far & (c == 1))
-    def _():
-        for k in range(2):
-            far1[k].wait_send()
-
-    @pl.when(has_far)
-    def _():
-        down_value.wait_send()
-
-    @pl.when(has_up)
-    def _():
-        up_key.wait_send()
-        up_value.wait_send()
-
-    @pl.when(relays)
-    def _():
-        far_value.wait_send()
-
-    @pl.when(got_up & has_up)
-    def _():
-        far_key.wait_send()
-
-    swap.wait_send()
+    when(c == 0, *sends(near_own + near_other))
+    when(got_up & (c == 0), *sends(cross0_own + cross0_other))
+    when(got_up & (c == 1), *sends(cross1_own + cross1_other))
+    when(got_far & (c == 1), *sends(far1))
+    when(has_far, *sends(down_own))
+    when(has_up, *sends(up_own + up_other))
+    when(relays, *sends(far_own))
+    when(got_up & has_up, *sends(far_other))
+    for one in swap:
+        one.wait_send()
 
 
 def layer_kernel(ids_ref, lengths_ref, inverse_ref, attn_gain_ref, mlp_gain_ref,
@@ -705,7 +665,6 @@
     rows, width = emb.shape
     span_rows = rows * GROUP
     spread = Spread(wo_hbm, part, ps, pr, ys, yr, cs, cr, z, x)
-    spread.plane(True)
     down = SpreadDown(wd_hbm, down_blocks, down_sems, z, x)
     hidden_width = wg.shape[0]
 
@@ -730,7 +689,8 @@
         lax.fori_loop(0, span_rows // 64, turn, 0)
 
     copies, total = find_rows(
-        ids_ref, all_ids, wanted_by, table, found, recv, emb, t, peers, sources, loads[0], ks, kr, xs, xr, positions
+        ids_ref, all_ids, wanted_by, table, found, recv, emb, t, peers, sources, loads[0], ks, kr, xs, xr,
+        functools.partial(spread.plane, True), positions,
     )
     scale = lax.rsqrt(total / width + EPSILON)
     for b in range(width // 1024):
@@ -739,12 +699,14 @@
     loads[1].wait()
     loads[2].wait()
     keys_here = lax.rem(t, 2) == 0
-    spread.plane_far(False)
-    spread.ring(True)
-    spread.cores(True, (0,))
+
+    def begun():
+        spread.plane_far(False)
+        spread.ring(True)
+        spread.cores(True, (0,))
 
     def project(dz):
-        if dz == 1:
+        if dz == 0:
             spread.ring(False)
             spread.ring_far(True)
             spread.cores(True, (1, 3))
@@ -758,7 +720,7 @@
         turned = both * cos + pltpu.roll(both, HD // 2, 1) * sin
         pair[span, :] = jnp.where(keys_here, turned, both).astype(BF16)
 
-    ring_gather(all_ref, gs, gr, z, x, project)
+    ring_gather(all_ref, gs, gr, z, x, project, begun)
     spread.ring_far(False)
     spread.cores(True, (2,))
 
@@ -859,7 +821,7 @@
             VMEM((span, HD), F32), VMEM((span, HD), F32), VMEM((SIDE, 1, 2 * group), jnp.int32), *GATHER_SEMS,
             VMEM((5, 2, span, HD), BF16), VMEM((span, HD), BF16),
             VMEM((SIDE, 1, 2 * group), F32), VMEM((SIDE, 1, 2 * group), F32), VMEM((SIDE, HD, 2 * group), F32),
-            VMEM((SIDE, SIDE * UNITS, UNIT, 2 * HD), BF16), DMA((12,)), DMA((12,)),
+            VMEM((SIDE, SIDE * UNITS, UNIT, 2 * HD), BF16), DMA((24,)), DMA((24,)),
             VMEM((rows, width), BF16), VMEM((SIDE, SIDE * UNITS, UNIT, padded), BF16), *GATHER_SEMS,
             VMEM((SIDE, SIDE * UNITS, UNIT, width), BF16),
             VMEM((SIDE - 1, SIDE * UNITS, UNIT, 2 * HD), BF16), VMEM((SIDE - 1, SIDE, *unit, 2 * HD), BF16),

time: 177 us -> 166 us (0.938)
  Pallas kernels: 175 us -> 163 us
    pallas_call x1, Pallas kernels: 175 us -> 163 us  [layer(): pl.pallas_call(layer_kernel, out_shape=jax.ShapeDtypeStruct((rows, width)...]
where the time goes in v8:
time: 166 us; the launch traced here: 164 us
  Pallas kernels  163 us (98%)
  local copies, waits for them, and re-layouts  1.77 us (1%)
    pallas_call x1, Pallas kernels, layer(): pl.pallas_call(layer_kernel, out_shape=jax.ShapeDtypeStruct((rows, width)...  163 us

profile of v8, /device:TPU:16, one launch (start us, length us, event | category | flops | bytes accessed | tf_op | source)
XLA Modules:
  0.0 164.4 jit_solution(15752349263801596835)
XLA Ops:
  0.0 162.6 %layer.1 = bf16[48,4096]{1,0:T(8,128)(2,1)} custom-call(s32[1,48]{1,0:T(1,128)} %bitcast.13, s32[16]{0:T(128)} %lengths_ref.1, f32[1,128]{1,0:T(1,128)} %constant.2.clone.inverse_ref, f32[1,4096]{1,0:T(1,128)} %bitcast.11, f32[1,4096]{1,0:T(1,128)} %bitcast.12, bf16[1024,4096]{1,0:T(8,128)(2,1)} %table_hbm.1, bf16[4096,256]{1,0:T(8,128)(2,1)} %wq_hbm.1, ...), custom_call_target="tpu_custom_call" | custom-call | tf_op jit(solution)/shard_map/layer/pallas_call | solution.py:809
  162.6 1.8 %copy.14 = bf16[48,4096]{1,0:T(8,128)(2,1)} copy(bf16[48,4096]{1,0:T(8,128)(2,1)} %layer.1) | data formatting | bytes 786432

commit v9 on v8

--- a/solution.py
+++ b/solution.py
@@ -328,7 +328,7 @@
             copy.wait_send()
 
 
-def short_reduce(mine, got, ssem, rsem, z, x, arrive, multiply, finish):
+def short_reduce(mine, got, ssem, rsem, z, x, order, arrive, multiply, finish, begun=lambda: None):
     half = mine.shape[-1]
     quarter = half // 2
     started = []
@@ -362,19 +362,21 @@
         lax.fori_loop(0, quarter // step, column, 0)
 
     for q in range(2):
-        for h in range(2):
+        for h in order:
             if q == 0:
                 arrive(h)
             make(h, q)
             d = 1 - 2 * q
             send(h, 3 * q, block(h, 2, q), d)
             send(h, (4, 1)[q], block(h, -d, q), -d)
-    for h in range(2):
+        if q == 0:
+            begun()
+    for h in order:
         for slot, q, d in ((0, 0, 1), (3, 1, -1)):
             recv(h, slot)
             got[h, slot] = (load(got.at[h, slot]) + load(block(h, d, q))).astype(BF16)
             send(h, slot + 2, got.at[h, slot], d)
-    for h in range(2):
+    for h in order:
         for slot in (1, 4, 2, 5):
             recv(h, slot)
         for q in range(2):
@@ -385,7 +387,7 @@
         copy.wait_send()
 
 
-def mix(moves, att, att_z, att_x, wo, part, mine, got, ssem, rsem, z, x, finish):
+def mix(moves, att, att_z, att_x, wo, part, mine, got, ssem, rsem, z, x, finish, begun):
     def multiply(h, cols):
         own = flat(att[z] if h == 0 else att[:, pl.ds(x * UNITS, UNITS)])
         others = jnp.concatenate([flat((att_z, att_x)[h][n]) for n in range(SIDE - 1)], axis=1)
@@ -393,7 +395,7 @@
         weights = part[:, :, :, cols].reshape(others.shape[1], out.shape[1])
         return out + jnp.dot(others, weights, preferred_element_type=F32)
 
-    short_reduce(mine, got, ssem, rsem, z, x, moves.arrive, multiply, finish)
+    short_reduce(mine, got, ssem, rsem, z, x, (0, 1), moves.arrive, multiply, finish, begun)
     moves.drain()
 
 
@@ -735,16 +737,18 @@
         functools.partial(down.plane, True), late, moves_of.finished
     )
     spread.cores(False, (0, 1, 3))
-    down.plane_far(False)
-    down.ring(True)
-    down.cores(True, (0,))
+
+    def onward():
+        down.plane_far(False)
+        down.ring(True)
+        down.cores(True, (0,))
 
     def mixed(cols, value):
         stream[:, cols] = (emb[:, cols].astype(F32) + value).astype(BF16)
 
     loads[3].wait()
     spread.cores(False, (2,))
-    mix(moves_of, att, att_z, att_x, wo, part, mine, got, ss, sr, z, x, mixed)
+    mix(moves_of, att, att_z, att_x, wo, part, mine, got, ss, sr, z, x, mixed, onward)
     spread.drain()
     all_ref[t] = normalize(stream[...].astype(F32), mlp_gain_ref[...])
     loads[4].wait()
@@ -772,7 +776,7 @@
 
     def arrive(h):
         hidden.arrive(h)
-        if h == 0:
+        if h == 1:
             down.cores(False, (0, 1, 3, 2))
 
     def multiply(h, cols):
@@ -789,7 +793,7 @@
     def added(cols, value):
         out_ref[:, cols] = (stream[:, cols].astype(F32) + value).astype(BF16)
 
-    short_reduce(mine, got, ss2, sr2, z, x, arrive, multiply, added)
+    short_reduce(mine, got, ss2, sr2, z, x, (1, 0), arrive, multiply, added)
     hidden.drain()
     down.drain()
     for copy in copies:

time: 166 us -> 165 us (level)
  Pallas kernels: 163 us -> 161 us
where the time goes in v9:
time: 165 us; the launch traced here: 163 us
  Pallas kernels  161 us (98%)
  local copies, waits for them, and re-layouts  1.77 us (1%)
    pallas_call x1, Pallas kernels, layer(): pl.pallas_call(layer_kernel, out_shape=jax.ShapeDtypeStruct((rows, width)...  161 us

profile of v9, /device:TPU:16, one launch (start us, length us, event | category | flops | bytes accessed | tf_op | source)
XLA Modules:
  0.0 163.1 jit_solution(1947452040470444817)
XLA Ops:
  0.0 161.4 %layer.1 = bf16[48,4096]{1,0:T(8,128)(2,1)} custom-call(s32[1,48]{1,0:T(1,128)} %bitcast.13, s32[16]{0:T(128)} %lengths_ref.1, f32[1,128]{1,0:T(1,128)} %constant.2.clone.inverse_ref, f32[1,4096]{1,0:T(1,128)} %bitcast.11, f32[1,4096]{1,0:T(1,128)} %bitcast.12, bf16[1024,4096]{1,0:T(8,128)(2,1)} %table_hbm.1, bf16[4096,256]{1,0:T(8,128)(2,1)} %wq_hbm.1, ...), custom_call_target="tpu_custom_call" | custom-call | tf_op jit(solution)/shard_map/layer/pallas_call | solution.py:813
  161.4 1.8 %copy.14 = bf16[48,4096]{1,0:T(8,128)(2,1)} copy(bf16[48,4096]{1,0:T(8,128)(2,1)} %layer.1) | data formatting | bytes 786432

commit v10 on v9

--- a/solution.py
+++ b/solution.py
@@ -12,6 +12,7 @@
 SIDE = 4
 GROUP = SIDE * SIDE
 SLOTS = 8
+PARTS = 4
 UNIT = 16
 UNITS = 3
 
@@ -444,7 +445,7 @@
     pick = lax.broadcasted_iota(jnp.int32, (slots, owned), 1).astype(F32) == wanted
     pick = jnp.where(pick, 1.0, 0.0).astype(BF16)
     load.wait()
-    parts = 2
+    parts = PARTS
     step = width // parts
     for c in range(parts):
         def fetch(b, carry):
@@ -819,7 +820,7 @@
             *[VMEM(w.shape, BF16) for w in (table, wq, wkv, wo, wg, wu, wd)], DMA((7,)),
             VMEM((8, 128), jnp.int32), VMEM((GROUP, 8, 128), jnp.int32),
             VMEM((GROUP, SLOTS, width), BF16), VMEM((GROUP, SLOTS, width), BF16),
-            peers, peers, DMA((2, GROUP - 1)), DMA((2, GROUP - 1)),
+            peers, peers, DMA((PARTS, GROUP - 1)), DMA((PARTS, GROUP - 1)),
             VMEM((rows, width), BF16), VMEM((GROUP, rows, width), BF16),
             VMEM((span, wq.shape[1]), BF16), VMEM((span, HD), BF16),
             VMEM((span, HD), F32), VMEM((span, HD), F32), VMEM((SIDE, 1, 2 * group), jnp.int32), *GATHER_SEMS,

time: 165 us -> 165 us (level)
  no operation moved by 1% of the time
where the time goes in v10:
time: 165 us; the launch traced here: 164 us
  Pallas kernels  162 us (98%)
  local copies, waits for them, and re-layouts  1.77 us (1%)
    pallas_call x1, Pallas kernels, layer(): pl.pallas_call(layer_kernel, out_shape=jax.ShapeDtypeStruct((rows, width)...  162 us

profile of v10, /device:TPU:16, one launch (start us, length us, event | category | flops | bytes accessed | tf_op | source)
XLA Modules:
  0.0 164.0 jit_solution(14409831941691608725)
XLA Ops:
  0.0 162.2 %layer.1 = bf16[48,4096]{1,0:T(8,128)(2,1)} custom-call(s32[1,48]{1,0:T(1,128)} %bitcast.13, s32[16]{0:T(128)} %lengths_ref.1, f32[1,128]{1,0:T(1,128)} %constant.2.clone.inverse_ref, f32[1,4096]{1,0:T(1,128)} %bitcast.11, f32[1,4096]{1,0:T(1,128)} %bitcast.12, bf16[1024,4096]{1,0:T(8,128)(2,1)} %table_hbm.1, bf16[4096,256]{1,0:T(8,128)(2,1)} %wq_hbm.1, ...), custom_call_target="tpu_custom_call" | custom-call | tf_op jit(solution)/shard_map/layer/pallas_call | solution.py:814
  162.2 1.8 %copy.14 = bf16[48,4096]{1,0:T(8,128)(2,1)} copy(bf16[48,4096]{1,0:T(8,128)(2,1)} %layer.1) | data formatting | bytes 786432
